TPU v7x, 32 devices: a whole 2x2x4 slice. The times are simulated.
32 devices in a mesh: dp: 8 (over y, x, core), seq: 4 (over z).
Axes of the slice: x: 2, y: 2, z: 4, core: 2. Of those that a mesh axis runs over, the one named last changes fastest.
Arguments:
- hidden_in: bfloat16 [8192, 2048], P(('dp', 'seq')), may hold values from -60 to 60
- layer_input: bfloat16 [8192, 256], P(('dp', 'seq')), may hold values from -6 to 6
- seq_lengths: int32 [8], P('dp'), may hold values from 256 to 1024, as said below
- cotangent: bfloat16 [8192, 2048], P(('dp', 'seq')), may hold values from -6 to 6
- query_weight: bfloat16 [2048, 2048], P(('dp', 'seq')), may hold values from -0.125 to 0.125
- key_matrix: bfloat16 [2048, 512], P(('dp', 'seq')), may hold values from -0.125 to 0.125
- value_matrix: bfloat16 [2048, 512], P(('dp', 'seq')), may hold values from -0.125 to 0.125
- output_weight: bfloat16 [2048, 2048], P(('dp', 'seq')), may hold values from -0.125 to 0.125
- laurel_left: bfloat16 [2048, 64], P(('dp', 'seq')), may hold values from -0.125 to 0.125
- laurel_right: bfloat16 [64, 2048], P(None, ('dp', 'seq')), may hold values from -0.75 to 0.75
- input_gate: bfloat16 [2048, 256], P(('dp', 'seq')), may hold values from -0.125 to 0.125
- input_projection: bfloat16 [256, 2048], P(None, ('dp', 'seq')), may hold values from -0.375 to 0.375
- gate_weight: bfloat16 [2048, 8192], P(('dp', 'seq')), may hold values from -0.125 to 0.125
- up_weight: bfloat16 [2048, 8192], P(('dp', 'seq')), may hold values from -0.125 to 0.125
- down_weight: bfloat16 [8192, 2048], P(('dp', 'seq')), may hold values from -0.0625 to 0.0625
- norm_gains: bfloat16 [6, 2048], P(None, ('dp', 'seq')), may hold values from 0.5 to 1.5
- head_gains: bfloat16 [2, 256], P(None, ('dp', 'seq')), may hold values from 0.19921875 to 0.5
Outputs:
- block_out: float32 [8192, 2048], P(('dp', 'seq'))
- d_hidden: float32 [8192, 2048], P(('dp', 'seq'))
- d_query_weight: float32 [2048, 2048], P(('dp', 'seq'))
- d_key_weight: float32 [2048, 512], P(('dp', 'seq'))
- d_value_weight: float32 [2048, 512], P(('dp', 'seq'))
- d_output_weight: float32 [2048, 2048], P(('dp', 'seq'))
- d_laurel_left: float32 [2048, 64], P(('dp', 'seq'))
- d_laurel_right: float32 [64, 2048], P(None, ('dp', 'seq'))
- d_input_gate: float32 [2048, 256], P(('dp', 'seq'))
- d_input_projection: float32 [256, 2048], P(None, ('dp', 'seq'))
- d_gate_weight: float32 [2048, 8192], P(('dp', 'seq'))
- d_up_weight: float32 [2048, 8192], P(('dp', 'seq'))
- d_down_weight: float32 [8192, 2048], P(('dp', 'seq'))
- d_norm_gains: float32 [6, 2048], P(None, ('dp', 'seq'))
- d_head_gains: float32 [2, 256], P(None, ('dp', 'seq'))
Inputs may be any that keep to these rules, and one draw needn't show every extreme that they name: `seq_lengths`: one sequence has exactly 1024 tokens and another exactly a quarter of 1024.
All inputs are finite; a program needn't handle non-finite values.
Results may differ from a plain program's by a relative error of at most 0.018.
Values may be sent and summed in bfloat16 or wider, within the bound.
A program may use at most 640 MiB of HBM per device.

v0:
```python
from functools import partial

import jax
import jax.numpy as jnp
from jax import lax
from jax.sharding import PartitionSpec as P

QUERY_HEADS = 8
KEY_VALUE_HEADS = 2
HEAD_SIZE = 256
FF = 8192
WINDOW = 512


EPSILON = 1e-06
ROPE_BASE = 10000.0
HALF_ROOT = 0.7071067811865476
MASKED = -1e30


def from_behind(block, axis, distance):
    devices = range(lax.axis_size(axis))
    route = [(i - distance, i) for i in devices if i - distance in devices]
    return lax.ppermute(block, axis, route)


def rms_norm(value, gain):
    return value * lax.rsqrt(jnp.mean(value * value, axis=-1, keepdims=True) + EPSILON) * gain


def unit_norm(value):
    return rms_norm(value, 1.0)


def rotate(value, positions):
    half = value.shape[-1] // 2
    inverse = ROPE_BASE ** (-jnp.arange(half, dtype=jnp.float32) * 2.0 / value.shape[-1])
    angle = positions.astype(jnp.float32)[:, None] * inverse[None, :]
    cosine = jnp.cos(angle)[:, None, :]
    sine = jnp.sin(angle)[:, None, :]
    first = value[..., :half]
    second = value[..., half:]
    return jnp.concatenate(
        [first * cosine - second * sine, second * cosine + first * sine], axis=-1
    )


def head_norm(value, gain, positions):
    return rotate(rms_norm(value, gain), positions)


def gated(gate, other):
    return jax.nn.gelu(gate, approximate=True) * other


def matrix_result(left, right):
    return jnp.dot(left, right, preferred_element_type=jnp.float32)


def times_transposed(left, right):
    return lax.dot_general(
        left, right, (((1,), (1,)), ((), ())), preferred_element_type=jnp.float32
    )


def transposed_times(left, right):
    return lax.dot_general(
        left, right, (((0,), (0,)), ((), ())), preferred_element_type=jnp.float32
    )


def masked_scores(grouped_rows, key_rows, query_places, key_places, score_scale):
    scores = (
        jnp.einsum("qkgd,tkd->kgqt", grouped_rows, key_rows, preferred_element_type=jnp.float32)
        * score_scale
    )
    allowed = (
        (key_places[None, :] <= query_places[:, None])
        & (query_places[:, None] - key_places[None, :] < WINDOW)
        & (key_places[None, :] >= 0)
    )
    return jnp.where(allowed, scores, MASKED)


def on_device(
    hidden_in,
    layer_input,
    seq_lengths,
    cotangent,
    query_weight,
    key_matrix,
    value_matrix,
    output_weight,
    laurel_left,
    laurel_right,
    input_gate,
    input_projection,
    gate_weight,
    up_weight,
    down_weight,
    norm_gains,
    head_gains,
):
    row_number_total = hidden_in.shape[0]
    hop_count = max(1, WINDOW // row_number_total)
    query_group_count = QUERY_HEADS // KEY_VALUE_HEADS
    score_scale = 1.0
    seq_index = lax.axis_index("seq")
    query_places = seq_index * row_number_total + jnp.arange(row_number_total, dtype=jnp.int32)
    key_places = (seq_index - hop_count) * row_number_total + jnp.arange(
        (hop_count + 1) * row_number_total, dtype=jnp.int32
    )
    live_rows = (query_places < seq_lengths[0]).astype(jnp.float32)[:, None]
    gathered = (
        lax.all_gather(query_weight, ("dp", "seq"), axis=0, tiled=True),
        lax.all_gather(key_matrix, ("dp", "seq"), axis=0, tiled=True),
        lax.all_gather(value_matrix, ("dp", "seq"), axis=0, tiled=True),
        lax.all_gather(output_weight, ("dp", "seq"), axis=0, tiled=True),
        lax.all_gather(laurel_left, ("dp", "seq"), axis=0, tiled=True),
        lax.all_gather(laurel_right, ("dp", "seq"), axis=1, tiled=True),
        lax.all_gather(input_gate, ("dp", "seq"), axis=0, tiled=True),
        lax.all_gather(input_projection, ("dp", "seq"), axis=1, tiled=True),
        lax.all_gather(norm_gains, ("dp", "seq"), axis=1, tiled=True),
        lax.all_gather(head_gains, ("dp", "seq"), axis=1, tiled=True),
    )
    (
        query_all,
        key_full_rows,
        value_full_rows,
        output_all,
        left_all,
        right_all,
        side_gate_all,
        side_output_all,
        gain_all,
        head_all,
    ) = gathered
    gain_rows = gain_all.astype(jnp.float32)
    head_rows = head_all.astype(jnp.float32)
    hidden = hidden_in.astype(jnp.float32)
    side_input = layer_input.astype(jnp.float32)
    head_apply = partial(head_norm, positions=query_places)
    normed = rms_norm(hidden, gain_rows[0])
    normalized_reduced = normed.astype(jnp.bfloat16)
    query_raw = matrix_result(normalized_reduced, query_all).reshape(
        row_number_total, QUERY_HEADS, HEAD_SIZE
    )
    key_unrotated = matrix_result(normalized_reduced, key_full_rows).reshape(
        row_number_total, KEY_VALUE_HEADS, HEAD_SIZE
    )
    value_projected = matrix_result(normalized_reduced, value_full_rows).reshape(
        row_number_total, KEY_VALUE_HEADS, HEAD_SIZE
    )
    query_reduced = head_apply(query_raw, head_rows[0]).astype(jnp.bfloat16)
    key_low = head_apply(key_unrotated, head_rows[1]).astype(jnp.bfloat16)
    value_low = unit_norm(value_projected).astype(jnp.bfloat16)
    moving = jnp.stack([key_low, value_low])
    kv_parts = [moving]
    for hop_index in range(hop_count):
        moving = from_behind(moving, "seq", 1)
        kv_parts.insert(0, moving)
    kv_window = jnp.concatenate(kv_parts, axis=1)
    grouped_rows = query_reduced.reshape(
        row_number_total, KEY_VALUE_HEADS, query_group_count, HEAD_SIZE
    )
    scores = masked_scores(grouped_rows, kv_window[0], query_places, key_places, score_scale)
    row_top = jnp.max(scores, axis=-1, keepdims=True)
    weights = jnp.exp(scores - row_top)
    row_total = jnp.sum(weights, axis=-1, keepdims=True)
    log_total = row_top + jnp.log(row_total)
    probs_low = (weights / row_total).astype(jnp.bfloat16)
    mixed_low = (
        jnp.einsum("kgqt,tkd->qkgd", probs_low, kv_window[1], preferred_element_type=jnp.float32)
        .reshape(row_number_total, QUERY_HEADS * HEAD_SIZE)
        .astype(jnp.bfloat16)
    )
    attention_raw = matrix_result(mixed_low, output_all)
    branch_one = hidden + rms_norm(attention_raw, gain_rows[1])
    left_low = matrix_result(normalized_reduced, left_all).astype(jnp.bfloat16)
    right_raw = matrix_result(left_low, right_all)
    merged = (branch_one + normed + rms_norm(right_raw, gain_rows[2])) * HALF_ROOT
    expand_low = rms_norm(merged, gain_rows[3]).astype(jnp.bfloat16)
    pieces = (
        lax.all_gather(gate_weight, ("dp", "seq"), axis=0, tiled=True),
        lax.all_gather(up_weight, ("dp", "seq"), axis=0, tiled=True),
    )
    columns = expand_low
    gate_raw = matrix_result(columns, pieces[0])
    up_raw = matrix_result(columns, pieces[1])
    act_low = gated(gate_raw, up_raw).astype(jnp.bfloat16)
    columns = act_low
    reduced_raw = matrix_result(
        columns, lax.all_gather(down_weight, ("dp", "seq"), axis=0, tiled=True)
    )
    after_feed = merged + rms_norm(reduced_raw, gain_rows[4])
    after_low = after_feed.astype(jnp.bfloat16)
    side_raw = matrix_result(after_low, side_gate_all)
    side_low = gated(side_raw, side_input).astype(jnp.bfloat16)
    side_out = matrix_result(side_low, side_output_all)
    block_out = (after_feed + rms_norm(side_out, gain_rows[5])) * live_rows
    again = (
        lax.all_gather(query_weight, ("dp", "seq"), axis=0, tiled=True),
        lax.all_gather(key_matrix, ("dp", "seq"), axis=0, tiled=True),
        lax.all_gather(value_matrix, ("dp", "seq"), axis=0, tiled=True),
        lax.all_gather(output_weight, ("dp", "seq"), axis=0, tiled=True),
        lax.all_gather(laurel_left, ("dp", "seq"), axis=0, tiled=True),
        lax.all_gather(laurel_right, ("dp", "seq"), axis=1, tiled=True),
        lax.all_gather(input_gate, ("dp", "seq"), axis=0, tiled=True),
        lax.all_gather(input_projection, ("dp", "seq"), axis=1, tiled=True),
    )
    (
        query_back,
        key_back,
        value_back,
        output_back,
        left_back,
        right_back,
        side_gate_back,
        side_output_back,
    ) = again
    upstream = cotangent.astype(jnp.float32) * live_rows
    _, pull_side_norm = jax.vjp(rms_norm, side_out, gain_rows[5])
    grad_side_out, gain_grad_five = pull_side_norm(upstream)
    grad_side_low = grad_side_out.astype(jnp.bfloat16)
    grad_projection = transposed_times(side_low, grad_side_low)
    _, pull_side_gate = jax.vjp(gated, side_raw, side_input)
    grad_side_raw = pull_side_gate(times_transposed(grad_side_low, side_output_back))[0].astype(
        jnp.bfloat16
    )
    grad_side_gate = transposed_times(after_low, grad_side_raw)
    grad_after = upstream + times_transposed(grad_side_raw, side_gate_back)
    _, pull_reduce_norm = jax.vjp(rms_norm, reduced_raw, gain_rows[4])
    grad_reduced, gain_grad_four = pull_reduce_norm(grad_after)
    grad_reduced_low = grad_reduced.astype(jnp.bfloat16)
    grad_product = times_transposed(
        grad_reduced_low, lax.all_gather(down_weight, ("dp", "seq"), axis=0, tiled=True)
    )
    _, pull_gated = jax.vjp(gated, gate_raw, up_raw)
    grad_gate_raw, grad_up_raw = pull_gated(grad_product)
    grad_gate_low = grad_gate_raw.astype(jnp.bfloat16)
    grad_up_low = grad_up_raw.astype(jnp.bfloat16)
    pieces = (
        lax.all_gather(gate_weight, ("dp", "seq"), axis=0, tiled=True),
        lax.all_gather(up_weight, ("dp", "seq"), axis=0, tiled=True),
    )
    part = times_transposed(grad_gate_low, pieces[0]) + times_transposed(grad_up_low, pieces[1])
    grad_down = lax.psum_scatter(
        transposed_times(act_low, grad_reduced_low), ("dp", "seq"), scatter_dimension=0, tiled=True
    )
    both_low = jnp.concatenate([grad_gate_low, grad_up_low], axis=1)
    grad_both = lax.psum_scatter(
        transposed_times(expand_low, both_low), ("dp", "seq"), scatter_dimension=0, tiled=True
    )
    grad_gate = grad_both[:, :FF]
    grad_up = grad_both[:, FF:]
    _, pull_expand_norm = jax.vjp(rms_norm, merged, gain_rows[3])
    grad_merged_part, gain_grad_three = pull_expand_norm(part)
    grad_sum = (grad_after + grad_merged_part) * HALF_ROOT
    _, pull_laurel_norm = jax.vjp(rms_norm, right_raw, gain_rows[2])
    grad_right, gain_grad_two = pull_laurel_norm(grad_sum)
    grad_right_low = grad_right.astype(jnp.bfloat16)
    grad_laurel_right = transposed_times(left_low, grad_right_low)
    grad_left_low = times_transposed(grad_right_low, right_back).astype(jnp.bfloat16)
    grad_laurel_left = transposed_times(normalized_reduced, grad_left_low)
    _, pull_attention_norm = jax.vjp(rms_norm, attention_raw, gain_rows[1])
    grad_attention, gain_grad_one = pull_attention_norm(grad_sum)
    grad_attention_low = grad_attention.astype(jnp.bfloat16)
    grad_output = transposed_times(mixed_low, grad_attention_low)
    grad_mixed_low = (
        times_transposed(grad_attention_low, output_back)
        .astype(jnp.bfloat16)
        .reshape(row_number_total, KEY_VALUE_HEADS, query_group_count, HEAD_SIZE)
    )
    scores_again = masked_scores(grouped_rows, kv_window[0], query_places, key_places, score_scale)
    probs_again = jnp.exp(scores_again - log_total)
    probs_again_low = probs_again.astype(jnp.bfloat16)
    grad_probs = jnp.einsum(
        "qkgd,tkd->kgqt", grad_mixed_low, kv_window[1], preferred_element_type=jnp.float32
    )
    row_inner = jnp.sum(probs_again * grad_probs, axis=-1, keepdims=True)
    grad_scores_low = (probs_again * (grad_probs - row_inner)).astype(jnp.bfloat16)
    grad_query_rot = (
        jnp.einsum(
            "kgqt,tkd->qkgd", grad_scores_low, kv_window[0], preferred_element_type=jnp.float32
        )
        * score_scale
    ).reshape(row_number_total, QUERY_HEADS, HEAD_SIZE)
    grad_keys = (
        jnp.einsum(
            "kgqt,qkgd->tkd", grad_scores_low, grouped_rows, preferred_element_type=jnp.float32
        )
        * score_scale
    )
    grad_values = jnp.einsum(
        "kgqt,qkgd->tkd", probs_again_low, grad_mixed_low, preferred_element_type=jnp.float32
    )
    grad_window = jnp.stack([grad_keys, grad_values])
    carried = grad_window[:, :row_number_total]
    for hop_index in range(hop_count - 1, -1, -1):
        carried = from_behind(carried.astype(jnp.bfloat16), "seq", -1).astype(carried.dtype)
        begin = (hop_count - hop_index) * row_number_total
        carried = carried + grad_window[:, begin : begin + row_number_total]
    _, pull_query = jax.vjp(head_apply, query_raw, head_rows[0])
    grad_query_raw, head_grad_zero = pull_query(grad_query_rot)
    _, pull_key = jax.vjp(head_apply, key_unrotated, head_rows[1])
    key_gradient_unrotated, head_grad_one = pull_key(carried[0])
    _, pull_value = jax.vjp(unit_norm, value_projected)
    value_gradient_projected = pull_value(carried[1])[0]
    grad_query_low = grad_query_raw.reshape(row_number_total, QUERY_HEADS * HEAD_SIZE).astype(
        jnp.bfloat16
    )
    key_gradient_reduced = key_gradient_unrotated.reshape(
        row_number_total, KEY_VALUE_HEADS * HEAD_SIZE
    ).astype(jnp.bfloat16)
    value_gradient_reduced = value_gradient_projected.reshape(
        row_number_total, KEY_VALUE_HEADS * HEAD_SIZE
    ).astype(jnp.bfloat16)
    grad_query_weight = transposed_times(normalized_reduced, grad_query_low)
    grad_key_weight = transposed_times(normalized_reduced, key_gradient_reduced)
    grad_value_weight = transposed_times(normalized_reduced, value_gradient_reduced)
    grad_normed = (
        grad_sum
        + times_transposed(grad_left_low, left_back)
        + times_transposed(grad_query_low, query_back)
        + times_transposed(key_gradient_reduced, key_back)
        + times_transposed(value_gradient_reduced, value_back)
    )
    _, pull_input_norm = jax.vjp(rms_norm, hidden, gain_rows[0])
    grad_hidden_part, gain_grad_zero = pull_input_norm(grad_normed)
    grad_hidden = grad_sum + grad_hidden_part
    grad_gains = jnp.stack(
        [
            gain_grad_zero,
            gain_grad_one,
            gain_grad_two,
            gain_grad_three,
            gain_grad_four,
            gain_grad_five,
        ]
    )
    grad_heads = jnp.stack([head_grad_zero, head_grad_one])
    summed = (
        lax.psum_scatter(grad_query_weight, ("dp", "seq"), scatter_dimension=0, tiled=True),
        lax.psum_scatter(grad_key_weight, ("dp", "seq"), scatter_dimension=0, tiled=True),
        lax.psum_scatter(grad_value_weight, ("dp", "seq"), scatter_dimension=0, tiled=True),
        lax.psum_scatter(grad_output, ("dp", "seq"), scatter_dimension=0, tiled=True),
        lax.psum_scatter(grad_laurel_left, ("dp", "seq"), scatter_dimension=0, tiled=True),
        lax.psum_scatter(grad_laurel_right, ("dp", "seq"), scatter_dimension=1, tiled=True),
        lax.psum_scatter(grad_side_gate, ("dp", "seq"), scatter_dimension=0, tiled=True),
        lax.psum_scatter(grad_projection, ("dp", "seq"), scatter_dimension=1, tiled=True),
        lax.psum_scatter(grad_gains, ("dp", "seq"), scatter_dimension=1, tiled=True),
        lax.psum_scatter(grad_heads, ("dp", "seq"), scatter_dimension=1, tiled=True),
    )
    (
        part_query,
        part_key,
        part_value,
        part_output,
        part_left,
        part_right,
        part_gate,
        part_projection,
        part_gains,
        part_heads,
    ) = summed
    return (
        block_out,
        grad_hidden,
        part_query,
        part_key,
        part_value,
        part_output,
        part_left,
        part_right,
        part_gate,
        part_projection,
        grad_gate,
        grad_up,
        grad_down,
        part_gains,
        part_heads,
    )


def solution(mesh):
    return jax.shard_map(
        on_device,
        mesh=mesh,
        in_specs=(
            P(("dp", "seq"), None),
            P(("dp", "seq"), None),
            P("dp"),
            P(("dp", "seq"), None),
            P(("dp", "seq"), None),
            P(("dp", "seq"), None),
            P(("dp", "seq"), None),
            P(("dp", "seq"), None),
            P(("dp", "seq"), None),
            P(None, ("dp", "seq")),
            P(("dp", "seq"), None),
            P(None, ("dp", "seq")),
            P(("dp", "seq"), None),
            P(("dp", "seq"), None),
            P(("dp", "seq"), None),
            P(None, ("dp", "seq")),
            P(None, ("dp", "seq")),
        ),
        out_specs=(
            P(("dp", "seq"), None),
            P(("dp", "seq"), None),
            P(("dp", "seq"), None),
            P(("dp", "seq"), None),
            P(("dp", "seq"), None),
            P(("dp", "seq"), None),
            P(("dp", "seq"), None),
            P(None, ("dp", "seq")),
            P(("dp", "seq"), None),
            P(None, ("dp", "seq")),
            P(("dp", "seq"), None),
            P(("dp", "seq"), None),
            P(("dp", "seq"), None),
            P(None, ("dp", "seq")),
            P(None, ("dp", "seq")),
        ),
        check_vma=False,
    )
```

profile of v0, /device:TPU:1, one launch (start us, length us, event | category | flops | bytes accessed | tf_op | source)
XLA Modules:
  0.0 6119.7 jit_solution(13953519353288872445)
XLA Ops:
  15.6 64.1 %all-gather.1 = bf16[32,8,2]{1,2,0:T(2,128)(2,1)S(1)} all-gather(bf16[1,8,2]{1,2,0:T(2,128)(2,1)S(1)} %bitcast.292), channel_id=1, replica_groups=mesh['dp'=8,'seq'=4] {'dp','seq'}, dimensions={0}, use_global_device_ids=true | all-gather | bytes 1056 | tf_op jit(solution)/shard_map/all_gather | solution.py:124
  80.0 64.1 %all-gather = bf16[32,64,6]{1,2,0:T(8,128)(2,1)S(1)} all-gather(bf16[1,64,6]{1,2,0:T(8,128)(2,1)S(1)} %bitcast.291), channel_id=1, replica_groups=mesh['dp'=8,'seq'=4] {'dp','seq'}, dimensions={0}, use_global_device_ids=true | all-gather | bytes 25344 | tf_op jit(solution)/shard_map/all_gather | solution.py:123
  144.3 74.3 %all_gather.57 = bf16[64,2048]{0,1:T(8,128)(2,1)S(1)} all-gather(bf16[64,64]{0,1:T(8,128)(2,1)S(1)} %copy.186), channel_id=1, replica_groups=mesh['dp'=8,'seq'=4] {'dp','seq'}, dimensions={1}, use_global_device_ids=true | all-gather | bytes 270336 | tf_op jit(solution)/shard_map/all_gather | solution.py:120
  218.5 75.3 %all_gather.56 = bf16[2048,64]{1,0:T(8,128)(2,1)S(1)} all-gather(bf16[64,64]{1,0:T(8,128)(2,1)S(1)} %copy-done.93), channel_id=1, replica_groups=mesh['dp'=8,'seq'=4] {'dp','seq'}, dimensions={0}, use_global_device_ids=true | all-gather | bytes 270336 | tf_op jit(solution)/shard_map/all_gather | solution.py:119
  308.4 19.7 collective-permute-done
  328.2 10.3 collective-permute-start.1
  340.6 4.8 collective-permute-done.1
  347.8 6.1 fusion.103
  366.3 6.2 multiply_reduce_fusion.16
  375.4 131.6 %all-gather.20.cloned.1.call-done = bf16[2048,8192]{1,0:T(8,128)(2,1)} async-done(((bf16[64,8192]{1,0:T(8,128)(2,1)}), bf16[2048,8192]{1,0:T(8,128)(2,1)}) %all-gather.20.cloned.1.call-update) | async-done | bytes 33554448 | tf_op jit(solution)/shard_map/all_gather | solution.py:184
  507.1 18.0 fusion.116
  525.1 177.7 %all-gather.22.cloned.1.call-done = bf16[2048,8192]{1,0:T(8,128)(2,1)} async-done(((bf16[64,8192]{1,0:T(8,128)(2,1)}), bf16[2048,8192]{1,0:T(8,128)(2,1)}) %all-gather.22.cloned.1.call-update) | async-done | bytes 33554448 | tf_op jit(solution)/shard_map/all_gather | solution.py:185
  702.9 23.9 multiply_convert_fusion.1
  726.8 172.0 %all-gather.24.cloned.1.call-done = bf16[8192,2048]{1,0:T(8,128)(2,1)} async-done(((bf16[256,2048]{1,0:T(8,128)(2,1)}), bf16[8192,2048]{1,0:T(8,128)(2,1)}) %all-gather.24.cloned.1.call-update) | async-done | bytes 33554448 | tf_op jit(solution)/shard_map/all_gather | solution.py:193
  898.8 16.7 multiply_reduce_fusion.13
  917.2 36.5 all-gather.26.cloned.1.call-done
  956.1 53.4 all-gather.28.cloned.1.call-done
  1019.3 23.5 multiply_convert_fusion
  1042.8 17.0 fusion.117
  1059.9 17.2 multiply_reduce_fusion.3
  1082.6 5.7 convolution_convert_fusion
  1089.1 4.2 fusion.41
  1093.3 5.1 fusion.11
  1098.5 3.2 fusion.13
  1101.7 3.3 convolution_bitcast_fusion.1
  1109.0 3.1 fusion.112
  1128.7 5.1 collective-permute-done.2
  1136.5 5.9 fusion.118
  1142.9 9.3 collective-permute-done.3
  1167.7 47.0 fusion.7
  1222.4 2.9 fusion.96
  1226.2 2.9 fusion.98
  1230.3 8.3 fusion.100
  1240.2 8.2 fusion.119
  1249.7 25.5 fusion.120
  1276.8 40.0 all-reduce.5
  1317.4 3.6 fusion.36
  1321.0 52.2 reduce-scatter.34.cloned.1.call-done
  1374.6 1884.2 %all-reduce.8.cloned.1.call-done = f32[2048,16384]{1,0:T(8,128)} async-done(((f32[2048,16384]{1,0:T(8,128)}), f32[2048,16384]{1,0:T(8,128)}) %all-reduce.8.cloned.1.call-update) | async-done | bytes 134217744
  3258.8 4.9 fusion.111
  3263.8 127.7 %reduce-scatter.24.cloned.1.call-done = f32[64,64]{1,0:T(8,128)} async-done(((f32[2048,64]{1,0:T(8,128)}), f32[64,64]{1,0:T(8,128)}) %reduce-scatter.24.cloned.1.call-update) | async-done | bytes 16400 | tf_op jit(solution)/shard_map/reduce_scatter | solution.py:347
  3391.4 137.9 %reduce-scatter.26.cloned.1.call-done = f32[64,256]{1,0:T(8,128)} async-done(((f32[2048,256]{1,0:T(8,128)}), f32[64,256]{1,0:T(8,128)}) %reduce-scatter.26.cloned.1.call-update) | async-done | bytes 65552 | tf_op jit(solution)/shard_map/reduce_scatter | solution.py:349
  3529.3 139.3 %reduce-scatter.28.cloned.1.call-done = f32[256,64]{0,1:T(8,128)} async-done(((f32[256,2048]{0,1:T(8,128)}), f32[256,64]{0,1:T(8,128)}) %reduce-scatter.28.cloned.1.call-update) | async-done | bytes 65552 | tf_op jit(solution)/shard_map/reduce_scatter | solution.py:350
  3668.7 148.6 %reduce-scatter.20.cloned.1.call-done = f32[64,512]{1,0:T(8,128)} async-done(((f32[2048,512]{1,0:T(8,128)}), f32[64,512]{1,0:T(8,128)}) %reduce-scatter.20.cloned.1.call-update) | async-done | bytes 131088 | tf_op jit(solution)/shard_map/reduce_scatter | solution.py:345
  3817.2 149.3 %reduce-scatter.18.cloned.1.call-done = f32[64,512]{1,0:T(8,128)} async-done(((f32[2048,512]{1,0:T(8,128)}), f32[64,512]{1,0:T(8,128)}) %reduce-scatter.18.cloned.1.call-update) | async-done | bytes 131088 | tf_op jit(solution)/shard_map/reduce_scatter | solution.py:344
  3966.5 369.2 %reduce-scatter.16.cloned.1.call-done = f32[64,2048]{1,0:T(8,128)} async-done(((f32[2048,2048]{1,0:T(8,128)}), f32[64,2048]{1,0:T(8,128)}) %reduce-scatter.16.cloned.1.call-update) | async-done | bytes 524304 | tf_op jit(solution)/shard_map/reduce_scatter | solution.py:343
  4335.7 365.2 %reduce-scatter.22.cloned.1.call-done = f32[64,2048]{1,0:T(8,128)} async-done(((f32[2048,2048]{1,0:T(8,128)}), f32[64,2048]{1,0:T(8,128)}) %reduce-scatter.22.cloned.1.call-update) | async-done | bytes 524304 | tf_op jit(solution)/shard_map/reduce_scatter | solution.py:346
  4700.9 1411.5 %reduce-scatter.30.cloned.1.call-done = f32[256,2048]{1,0:T(8,128)} async-done(((f32[8192,2048]{1,0:T(8,128)}), f32[256,2048]{1,0:T(8,128)}) %reduce-scatter.30.cloned.1.call-update) | async-done | bytes 2097168 | tf_op jit(solution)/shard_map/reduce_scatter | solution.py:247
  (391 shorter events, 117.2 us)
Async XLA Ops:
  7.2 289.5 %all-gather.14.cloned.1.call-start = ((), (), s32[]{:S(2)}) async-start(), calls=%async_computation.11 | async-start | bytes 2162688 | tf_op jit(solution)/shard_map/all_gather | solution.py:117
  7.9 292.0 %all-gather.12.cloned.1.call-start = ((), (), s32[]{:S(2)}) async-start(), calls=%async_computation.10 | async-start | bytes 2162688 | tf_op jit(solution)/shard_map/all_gather | solution.py:116
  8.7 339.1 %all-gather.16.cloned.1.call-start = ((), (), s32[]{:S(2)}) async-start(), calls=%async_computation.12 | async-start | bytes 8650752 | tf_op jit(solution)/shard_map/all_gather | solution.py:115
  9.4 356.9 %all-gather.18.cloned.1.call-start = ((), (), s32[]{:S(2)}) async-start(), calls=%async_computation.13 | async-start | bytes 8650752 | tf_op jit(solution)/shard_map/all_gather | solution.py:118
  10.0 70.0 %copy-start.107 = (bf16[6,64]{1,0:T(8,128)(2,1)S(1)}, bf16[6,64]{1,0:T(8,128)(2,1)}, u32[]{:S(2)}) copy-start(bf16[6,64]{1,0:T(8,128)(2,1)} %param.32) | copy-start | bytes 2308
  10.0 497.1 %all-gather.20.cloned.1.call-start = ((), (), s32[]{:S(2)}) async-start(), calls=%async_computation.14 | async-start | bytes 34603008 | tf_op jit(solution)/shard_map/all_gather | solution.py:184
  10.6 207.9 %copy-start.93 = (bf16[64,64]{1,0:T(8,128)(2,1)S(1)}, bf16[64,64]{1,0:T(8,128)(2,1)}, u32[]{:S(2)}) copy-start(bf16[64,64]{1,0:T(8,128)(2,1)} %param.25) | copy-start | bytes 24580
  10.6 692.2 %all-gather.22.cloned.1.call-start = ((), (), s32[]{:S(2)}) async-start(), calls=%async_computation.15 | async-start | bytes 34603008 | tf_op jit(solution)/shard_map/all_gather | solution.py:185
  11.2 887.6 %all-gather.24.cloned.1.call-start = ((), (), s32[]{:S(2)}) async-start(), calls=%async_computation.16 | async-start | bytes 34603008 | tf_op jit(solution)/shard_map/all_gather | solution.py:193
  11.9 941.8 %all-gather.26.cloned.1.call-start = ((), (), s32[]{:S(2)}) async-start(), calls=%async_computation.17 | async-start | bytes 1081344 | tf_op jit(solution)/shard_map/all_gather | solution.py:121
  12.7 996.8 %all-gather.28.cloned.1.call-start = ((), (), s32[]{:S(2)}) async-start(), calls=%async_computation.18 | async-start | bytes 1081344 | tf_op jit(solution)/shard_map/all_gather | solution.py:122
  13.4 1261.8 %reduce-scatter.32.cloned.1.call-start = ((), (), s32[]{:S(2)}) async-start(), calls=%async_computation.27 | async-start | bytes 1081344
  15.0 357.5 %copy-start.75 = (f32[256]{0:T(256)}, f32[256]{0:T(256)S(1)}, u32[]{:S(2)}) copy-start(f32[256]{0:T(256)S(1)} %fusion.78) | copy-start | bytes 3076
  80.0 225.4 %copy-start.95 = (f32[1,256]{1,0:T(1,128)}, f32[1,256]{1,0:T(1,128)S(1)}, u32[]{:S(2)}) copy-start(f32[1,256]{1,0:T(1,128)S(1)} %get-tuple-element.63) | copy-start | bytes 3076
  80.0 277.8 %copy-start.91 = (f32[1,256]{1,0:T(1,128)}, f32[1,256]{1,0:T(1,128)S(1)}, u32[]{:S(2)}) copy-start(f32[1,256]{1,0:T(1,128)S(1)} %get-tuple-element.62) | copy-start | bytes 3076
  144.2 228.3 %copy-start.63 = (f32[1,2048]{1,0:T(1,128)}, f32[1,2048]{1,0:T(1,128)S(1)}, u32[]{:S(2)}) copy-start(f32[1,2048]{1,0:T(1,128)S(1)} %get-tuple-element.61) | copy-start | bytes 24580
  218.5 76.4 %copy-start.36 = (bf16[64,2048]{0,1:T(8,128)(2,1)}, bf16[64,2048]{0,1:T(8,128)(2,1)S(1)}, u32[]{:S(2)}) copy-start(bf16[64,2048]{0,1:T(8,128)(2,1)S(1)} %all_gather.57) | copy-start | bytes 786436
  294.4 64.7 %copy-start.49 = (f32[256,128]{1,0:T(8,128)}, f32[256,128]{1,0:T(8,128)S(1)}, u32[]{:S(2)}) copy-start(f32[256,128]{1,0:T(8,128)S(1)} %get-tuple-element.64) | copy-start | bytes 393220
  305.2 33.2 copy-start.89
  305.2 33.8 copy-start.108
  305.7 22.4 collective-permute-start
  328.2 17.3 collective-permute-start.1
  375.4 327.4 %copy-start.40 = (bf16[256,2048]{1,0:T(8,128)(2,1)}, bf16[256,2048]{1,0:T(8,128)(2,1)S(1)}, u32[]{:S(2)}) copy-start(bf16[256,2048]{1,0:T(8,128)(2,1)S(1)} %multiply_convert_fusion.2) | copy-start | bytes 3145732
  898.8 18.1 copy-start.13
  917.2 95.5 %copy-start.8 = (f32[256,2048]{1,0:T(8,128)}, f32[256,2048]{1,0:T(8,128)S(1)}, u32[]{:S(2)}) copy-start(f32[256,2048]{1,0:T(8,128)S(1)} %multiply_add_fusion) | copy-start | bytes 6291460
  917.2 92.3 %copy-start.66 = (bf16[256,256]{1,0:T(8,128)(2,1)S(1)}, bf16[256,256]{1,0:T(8,128)(2,1)}, u32[]{:S(2)}) copy-start(bf16[256,256]{1,0:T(8,128)(2,1)} %param.18) | copy-start | bytes 393220
  956.1 55.3 copy-start.24
  1019.3 23.5 copy-start.38
  1059.8 17.2 copy-start.11
  1059.8 17.2 copy-start.16
  1059.8 17.2 copy-start.79
  1059.9 17.2 copy-start.80
  1093.3 21.3 copy-start.19
  1108.9 264.3 %reduce-scatter.34.cloned.1.call-start = ((), (), s32[]{:S(2)}) async-start(), calls=%async_computation.28 | async-start | bytes 1081344
  1115.5 18.3 collective-permute-start.2
  1135.0 17.2 collective-permute-start.3
  1167.6 2091.2 %all-reduce.8.cloned.1.call-start = ((), (), s32[]{:S(2)}) async-start(), calls=%async_computation.29 | async-start | bytes 268435456
  1214.7 2176.7 %reduce-scatter.24.cloned.1.call-start = ((), (), s32[]{:S(2)}) async-start(), calls=%async_computation.23 | async-start | bytes 1081344 | tf_op jit(solution)/shard_map/reduce_scatter | solution.py:347
  1217.3 2312.1 %reduce-scatter.26.cloned.1.call-start = ((), (), s32[]{:S(2)}) async-start(), calls=%async_computation.24 | async-start | bytes 2162688 | tf_op jit(solution)/shard_map/reduce_scatter | solution.py:349
  1219.2 2449.5 %reduce-scatter.28.cloned.1.call-start = ((), (), s32[]{:S(2)}) async-start(), calls=%async_computation.25 | async-start | bytes 2162688 | tf_op jit(solution)/shard_map/reduce_scatter | solution.py:350
  1222.4 2594.8 %reduce-scatter.20.cloned.1.call-start = ((), (), s32[]{:S(2)}) async-start(), calls=%async_computation.21 | async-start | bytes 4325376 | tf_op jit(solution)/shard_map/reduce_scatter | solution.py:345
  1225.3 2741.2 %reduce-scatter.18.cloned.1.call-start = ((), (), s32[]{:S(2)}) async-start(), calls=%async_computation.20 | async-start | bytes 4325376 | tf_op jit(solution)/shard_map/reduce_scatter | solution.py:344
  1229.1 3106.6 %reduce-scatter.16.cloned.1.call-start = ((), (), s32[]{:S(2)}) async-start(), calls=%async_computation.19 | async-start | bytes 17301504 | tf_op jit(solution)/shard_map/reduce_scatter | solution.py:343
  1238.7 3462.2 %reduce-scatter.22.cloned.1.call-start = ((), (), s32[]{:S(2)}) async-start(), calls=%async_computation.22 | async-start | bytes 17301504 | tf_op jit(solution)/shard_map/reduce_scatter | solution.py:346
  1248.5 4863.9 %reduce-scatter.30.cloned.1.call-start = ((), (), s32[]{:S(2)}) async-start(), calls=%async_computation.26 | async-start | bytes 69206016 | tf_op jit(solution)/shard_map/reduce_scatter | solution.py:247
  1275.1 42.3 copy-start.100
  1275.1 42.3 copy-start.102
  1275.1 42.3 copy-start.7
  (88 other events, 292.3 us)
Sparse Core Ops, SparseCore 0:
  11.0 58.9 all-gather.13
  72.9 55.4 all-gather.11
  131.3 78.4 all-gather.15
  212.6 79.8 all-gather.17
  295.2 211.7 all-gather.19
  509.9 192.9 all-gather.21
  705.8 192.9 all-gather.23
  901.8 51.9 all-gather.25
  956.7 52.7 all-gather.27
  1109.0 129.7 reduce-scatter.31
  1241.2 131.9 reduce-scatter.33
  1379.5 1879.3 all-reduce.7
  3261.7 129.7 reduce-scatter.23
  3394.2 135.0 reduce-scatter.25
  3532.0 136.5 reduce-scatter.27
  3671.5 145.7 reduce-scatter.19
  3820.0 146.4 reduce-scatter.17
  3969.3 366.3 reduce-scatter.15
  4338.7 362.1 reduce-scatter.21
  4703.8 1408.5 reduce-scatter.29
where the time goes:
time: 6130 us; the launch traced here: 6120 us
  waiting for transfers between devices  5400 us (88%)
  blocking collectives  318 us (5%)
  matrix products  278 us (5%)
    unnamed x23, waiting for transfers between devices  1940 us
    reduce_scatter x1, waiting for transfers between devices, on_device(): lax.psum_scatter(transposed_times(act_low, grad_reduced_low), ('dp', 'seq...  1410 us
    reduce_scatter x1, waiting for transfers between devices, on_device(): lax.psum_scatter(grad_query_weight, ('dp', 'seq'), scatter_dimension=0, t...  369 us
    reduce_scatter x1, waiting for transfers between devices, on_device(): lax.psum_scatter(grad_output, ('dp', 'seq'), scatter_dimension=0, tiled=T...  365 us
    all_gather x1, waiting for transfers between devices, on_device(): lax.all_gather(up_weight, ('dp', 'seq'), axis=0, tiled=True)  178 us
    all_gather x1, waiting for transfers between devices, on_device(): lax.all_gather(down_weight, ('dp', 'seq'), axis=0, tiled=True)  172 us
    reduce_scatter x1, waiting for transfers between devices, on_device(): lax.psum_scatter(grad_key_weight, ('dp', 'seq'), scatter_dimension=0, til...  149 us
    reduce_scatter x1, waiting for transfers between devices, on_device(): lax.psum_scatter(grad_value_weight, ('dp', 'seq'), scatter_dimension=0, t...  149 us
  transfers between devices with their start and end apart: 24, of which 19 were waited for; matrix products, arithmetic and copies ran while one was open for 4% of the time, Pallas kernels for 0%

commit v1 on v0

v1 whole, which is shorter than its diff:
```python
import jax
import jax.numpy as jnp
from jax import lax
from jax.sharding import Mesh, PartitionSpec as P

QUERY_HEADS = 8
KEY_VALUE_HEADS = 2
HEAD_SIZE = 256
WINDOW = 512
EPSILON = 1e-06
ROPE_BASE = 10000.0
HALF_ROOT = 0.7071067811865476
MASKED = -1e30
GELU_SCALE = 0.7978845608028654
GELU_CUBE = 0.044715
F32 = jnp.float32
BF16 = jnp.bfloat16


def dot(left, right, left_dim=1, right_dim=0):
    return lax.dot_general(
        left, right, (((left_dim,), (right_dim,)), ((), ())), preferred_element_type=F32
    )


def inverse_rms(value):
    return lax.rsqrt(jnp.mean(value * value, axis=-1, keepdims=True) + EPSILON)


def rms_back(value, inverse, gain, grad):
    scaled = grad * gain
    inner = jnp.mean(scaled * value, axis=-1, keepdims=True)
    unit = value * inverse
    return inverse * (scaled - unit * (inverse * inner)), grad * unit


def rope_tables(positions):
    half = HEAD_SIZE // 2
    rate = ROPE_BASE ** (-jnp.arange(half, dtype=F32) * 2.0 / HEAD_SIZE)
    angle = positions.astype(F32)[:, None] * rate[None, :]
    return jnp.cos(angle)[:, None, :], jnp.sin(angle)[:, None, :]


def rotate(value, cosine, sine):
    half = value.shape[-1] // 2
    first, second = value[..., :half], value[..., half:]
    return jnp.concatenate(
        [first * cosine - second * sine, second * cosine + first * sine], axis=-1
    )


def gelu_tanh(value):
    return jnp.tanh(GELU_SCALE * (value + GELU_CUBE * value * value * value))


def gelu(value):
    return 0.5 * value * (1.0 + gelu_tanh(value))


def gelu_slope(value):
    t = gelu_tanh(value)
    inner = GELU_SCALE * (1.0 + 3.0 * GELU_CUBE * value * value)
    return 0.5 * (1.0 + t) + 0.5 * value * (1.0 - t * t) * inner


def shift(block, pieces, distance):
    route = [
        (c * pieces + i, c * pieces + i + distance)
        for c in range(2)
        for i in range(pieces)
        if 0 <= i + distance < pieces
    ]
    return lax.ppermute(block, "g", route)


def group_gather(block):
    return lax.all_gather(block, "g", axis=0, tiled=True)


def group_scatter(partial):
    return lax.psum_scatter(partial, "g", scatter_dimension=0, tiled=True)


def column_chunks(weight, planes, ranks):
    depth, width = weight.shape
    part = width // (planes * ranks)
    split = weight.reshape(depth, planes, ranks, part).transpose(2, 0, 1, 3)
    moved = lax.all_to_all(split.reshape(ranks, depth, planes * part), "g", 0, 0)
    return lax.all_gather(
        moved.reshape(ranks * depth, planes * part), "pl", axis=0, tiled=True
    )


def column_chunks_back(grad, planes, ranks):
    mine = lax.psum_scatter(grad.astype(BF16), "pl", scatter_dimension=0, tiled=True)
    depth, width = mine.shape[0] // ranks, mine.shape[1]
    part = width // planes
    moved = lax.all_to_all(mine.reshape(ranks, depth, width), "g", 0, 0)
    moved = moved.reshape(ranks, depth, planes, part).transpose(1, 2, 0, 3)
    return moved.reshape(depth, planes * ranks * part).astype(F32)


def layer(planes, ranks, *args):
    (
        hidden_in,
        layer_input,
        seq_lengths,
        cotangent,
        gate_weight,
        up_weight,
        down_weight,
        first,
        second,
        head_gain,
    ) = args
    rows, width = hidden_in.shape
    pieces = ranks // 2
    hops = max(1, WINDOW // rows)
    groups = QUERY_HEADS // KEY_VALUE_HEADS
    piece = lax.rem(lax.axis_index("g"), pieces)
    places = piece * rows + jnp.arange(rows, dtype=jnp.int32)
    key_places = (piece - hops) * rows + jnp.arange((hops + 1) * rows, dtype=jnp.int32)
    live = (places < seq_lengths[0]).astype(F32)[:, None]

    head_width = QUERY_HEADS * HEAD_SIZE
    kv_width = KEY_VALUE_HEADS * HEAD_SIZE
    rank = first.shape[1] - head_width - 2 * kv_width
    side = layer_input.shape[1]
    head_gain = head_gain.astype(F32)
    output_all = second[:, :head_width]
    at = head_width
    side_gate_all = second[:, at : at + side]
    at += side
    right_all = second[:, at : at + rank]
    at += rank
    projection_all = second[:, at : at + side]
    at += side
    gains = second[:, at:].T.astype(F32)
    gate_cols = column_chunks(gate_weight, planes, ranks)
    up_cols = column_chunks(up_weight, planes, ranks)
    down_rows = lax.all_gather(down_weight, "pl", axis=0, tiled=True)

    hidden = hidden_in.astype(F32)
    side_input = layer_input.astype(F32)
    cosine, sine = rope_tables(places)

    hidden_inv = inverse_rms(hidden)
    normed = hidden * hidden_inv * gains[0]
    normed_low = normed.astype(BF16)
    raw = dot(normed_low, first)
    query_raw = raw[:, :head_width].reshape(rows, QUERY_HEADS, HEAD_SIZE)
    key_raw = raw[:, head_width : head_width + kv_width].reshape(rows, KEY_VALUE_HEADS, HEAD_SIZE)
    value_raw = raw[:, head_width + kv_width : head_width + 2 * kv_width].reshape(
        rows, KEY_VALUE_HEADS, HEAD_SIZE
    )
    left_low = raw[:, head_width + 2 * kv_width :].astype(BF16)
    query_inv = inverse_rms(query_raw)
    key_inv = inverse_rms(key_raw)
    value_inv = inverse_rms(value_raw)
    query_low = rotate(query_raw * query_inv * head_gain[0], cosine, sine).astype(BF16)
    key_low = rotate(key_raw * key_inv * head_gain[1], cosine, sine).astype(BF16)
    value_low = (value_raw * value_inv).astype(BF16)
    moving = jnp.stack([key_low, value_low])
    window = [moving]
    for hop in range(hops):
        moving = shift(moving, pieces, 1)
        window.insert(0, moving)
    window = jnp.concatenate(window, axis=1)
    grouped = query_low.reshape(rows, KEY_VALUE_HEADS, groups, HEAD_SIZE)
    scores = jnp.einsum("qkgd,tkd->kgqt", grouped, window[0], preferred_element_type=F32)
    allowed = (
        (key_places[None, :] <= places[:, None])
        & (places[:, None] - key_places[None, :] < WINDOW)
        & (key_places[None, :] >= 0)
    )
    scores = jnp.where(allowed, scores, MASKED)
    weights = jnp.exp(scores - jnp.max(scores, axis=-1, keepdims=True))
    probs = weights / jnp.sum(weights, axis=-1, keepdims=True)
    probs_low = probs.astype(BF16)
    mixed = (
        jnp.einsum("kgqt,tkd->qkgd", probs_low, window[1], preferred_element_type=F32)
        .reshape(rows, head_width)
        .astype(BF16)
    )
    attention_raw = dot(mixed, output_all)
    attention_inv = inverse_rms(attention_raw)
    right_raw = dot(left_low, right_all, 1, 1)
    right_inv = inverse_rms(right_raw)
    merged = (
        hidden
        + attention_raw * attention_inv * gains[1]
        + normed
        + right_raw * right_inv * gains[2]
    ) * HALF_ROOT
    merged_inv = inverse_rms(merged)
    expand_low = (merged * merged_inv * gains[3]).astype(BF16)

    expand_all = group_gather(expand_low)
    gate_raw = dot(expand_all, gate_cols)
    up_raw = dot(expand_all, up_cols)
    act_low = (gelu(gate_raw) * up_raw).astype(BF16)
    reduced_raw = group_scatter(dot(act_low, down_rows).astype(BF16)).astype(F32)
    reduced_inv = inverse_rms(reduced_raw)
    after_feed = merged + reduced_raw * reduced_inv * gains[4]
    after_low = after_feed.astype(BF16)
    side_raw = dot(after_low, side_gate_all)
    side_low = (gelu(side_raw) * side_input).astype(BF16)
    side_out = dot(side_low, projection_all, 1, 1)
    side_inv = inverse_rms(side_out)
    block_out = (after_feed + side_out * side_inv * gains[5]) * live

    upstream = cotangent.astype(F32) * live
    grad_side, gain_five = rms_back(side_out, side_inv, gains[5], upstream)
    grad_side_low = grad_side.astype(BF16)
    grad_side_raw = (
        dot(grad_side_low, projection_all) * side_input * gelu_slope(side_raw)
    ).astype(BF16)
    grad_after = upstream + dot(grad_side_raw, side_gate_all, 1, 1)
    grad_reduced, gain_four = rms_back(reduced_raw, reduced_inv, gains[4], grad_after)
    grad_reduced_low = grad_reduced.astype(BF16)

    grad_reduced_all = group_gather(grad_reduced_low)
    grad_product = dot(grad_reduced_all, down_rows, 1, 1)
    grad_gate_low = (grad_product * up_raw * gelu_slope(gate_raw)).astype(BF16)
    grad_up_low = (grad_product * gelu(gate_raw)).astype(BF16)
    part = group_scatter(
        (dot(grad_gate_low, gate_cols, 1, 1) + dot(grad_up_low, up_cols, 1, 1)).astype(BF16)
    ).astype(F32)
    grad_down = lax.psum_scatter(
        dot(act_low, grad_reduced_all, 0, 0).astype(BF16), "pl", scatter_dimension=0, tiled=True
    ).astype(F32)
    grad_gate = column_chunks_back(dot(expand_all, grad_gate_low, 0, 0), planes, ranks)
    grad_up = column_chunks_back(dot(expand_all, grad_up_low, 0, 0), planes, ranks)

    grad_merged, gain_three = rms_back(merged, merged_inv, gains[3], part)
    grad_sum = (grad_after + grad_merged) * HALF_ROOT
    grad_right, gain_two = rms_back(right_raw, right_inv, gains[2], grad_sum)
    grad_right_low = grad_right.astype(BF16)
    grad_left_low = dot(grad_right_low, right_all).astype(BF16)
    grad_attention, gain_one = rms_back(attention_raw, attention_inv, gains[1], grad_sum)
    grad_attention_low = grad_attention.astype(BF16)
    grad_mixed = (
        dot(grad_attention_low, output_all, 1, 1)
        .astype(BF16)
        .reshape(rows, KEY_VALUE_HEADS, groups, HEAD_SIZE)
    )
    grad_probs = jnp.einsum("qkgd,tkd->kgqt", grad_mixed, window[1], preferred_element_type=F32)
    inner = jnp.sum(probs * grad_probs, axis=-1, keepdims=True)
    grad_scores = (probs * (grad_probs - inner)).astype(BF16)
    grad_query_rot = jnp.einsum(
        "kgqt,tkd->qkgd", grad_scores, window[0], preferred_element_type=F32
    ).reshape(rows, QUERY_HEADS, HEAD_SIZE)
    grad_window = jnp.stack(
        [
            jnp.einsum("kgqt,qkgd->tkd", grad_scores, grouped, preferred_element_type=F32),
            jnp.einsum("kgqt,qkgd->tkd", probs_low, grad_mixed, preferred_element_type=F32),
        ]
    )
    carried = grad_window[:, :rows]
    for hop in range(hops - 1, -1, -1):
        begin = (hops - hop) * rows
        carried = shift(carried.astype(BF16), pieces, -1).astype(F32)
        carried = carried + grad_window[:, begin : begin + rows]
    grad_query, head_zero = rms_back(
        query_raw, query_inv, head_gain[0], rotate(grad_query_rot, cosine, -sine)
    )
    grad_key, head_one = rms_back(
        key_raw, key_inv, head_gain[1], rotate(carried[0], cosine, -sine)
    )
    grad_value, _ = rms_back(value_raw, value_inv, 1.0, carried[1])
    grad_raw = jnp.concatenate(
        [
            grad_query.reshape(rows, head_width).astype(BF16),
            grad_key.reshape(rows, kv_width).astype(BF16),
            grad_value.reshape(rows, kv_width).astype(BF16),
            grad_left_low,
        ],
        axis=1,
    )
    grad_normed = grad_sum + dot(grad_raw, first, 1, 1)
    grad_input, gain_zero = rms_back(hidden, hidden_inv, gains[0], grad_normed)
    grad_hidden = grad_sum + grad_input

    gain_grads = jnp.stack(
        [
            jnp.sum(g, axis=0)
            for g in (gain_zero, gain_one, gain_two, gain_three, gain_four, gain_five)
        ]
    )
    head_grads = jnp.stack([jnp.sum(head_zero, axis=(0, 1)), jnp.sum(head_one, axis=(0, 1))])

    def spread(grad, dim=0):
        grad = lax.psum_scatter(grad, "pl", scatter_dimension=dim, tiled=True)
        return lax.psum_scatter(grad, "g", scatter_dimension=dim, tiled=True)

    early = jnp.concatenate(
        [
            dot(mixed, grad_attention_low, 0, 0),
            dot(after_low, grad_side_raw, 0, 0),
            dot(grad_right_low, left_low, 0, 0),
            dot(grad_side_low, side_low, 0, 0),
        ],
        axis=1,
    ).astype(BF16)
    early = spread(early).astype(F32)
    late = spread(dot(normed_low, grad_raw, 0, 0).astype(BF16)).astype(F32)
    d_gains = spread(gain_grads, 1)
    d_heads = spread(head_grads, 1)
    d_output = early[:, :head_width]
    at = head_width
    d_side_gate = early[:, at : at + side]
    at += side
    d_right = early[:, at : at + rank].T
    at += rank
    d_projection = early[:, at : at + side].T
    d_query = late[:, :head_width]
    d_key = late[:, head_width : head_width + kv_width]
    d_value = late[:, head_width + kv_width : head_width + 2 * kv_width]
    d_left = late[:, head_width + 2 * kv_width :]
    return (
        block_out,
        grad_hidden,
        d_query,
        d_key,
        d_value,
        d_output,
        d_left,
        d_right,
        d_side_gate,
        d_projection,
        grad_gate,
        grad_up,
        grad_down,
        d_gains,
        d_heads,
    )


def gather_weights(
    query_weight,
    key_matrix,
    value_matrix,
    output_weight,
    laurel_left,
    laurel_right,
    input_gate,
    input_projection,
    norm_gains,
    head_gains,
):
    both = ("dp", "seq")
    first = jnp.concatenate([query_weight, key_matrix, value_matrix, laurel_left], axis=1)
    second = jnp.concatenate(
        [output_weight, input_gate, laurel_right.T, input_projection.T, norm_gains.T], axis=1
    )
    return (
        lax.all_gather(first, both, axis=0, tiled=True),
        lax.all_gather(second, both, axis=0, tiled=True),
        lax.all_gather(head_gains, both, axis=1, tiled=True),
    )


def solution(mesh):
    pieces = mesh.shape["seq"]
    planes, ranks = mesh.shape["dp"] // 2, 2 * pieces
    grid = Mesh(mesh.devices.reshape(planes, ranks), ("pl", "g"))

    def body(*args):
        whole_row, whole_column = P(("dp", "seq"), None), P(None, ("dp", "seq"))
        gathered = jax.shard_map(
            gather_weights,
            mesh=mesh,
            in_specs=(whole_row,) * 5
            + (whole_column, whole_row, whole_column, whole_column, whole_column),
            out_specs=(P(None, None),) * 3,
            check_vma=False,
        )(*args[4:12], *args[15:17])
        row, column = P(("pl", "g"), None), P(None, ("pl", "g"))
        lengths = jnp.repeat(args[2], pieces)
        return jax.shard_map(
            lambda *inner: layer(planes, ranks, *inner),
            mesh=grid,
            in_specs=(row, row, P(("pl", "g")), row, row, row, row) + (P(None, None),) * 3,
            out_specs=(row,) * 7 + (column, row, column) + (row,) * 3 + (column,) * 2,
            check_vma=False,
        )(args[0], args[1], lengths, args[3], *args[12:15], *gathered)

    return body
```

time: 6130 us -> 1720 us (0.28)
  waiting for transfers between devices: 5400 us -> 1130 us
  blocking collectives: 318 us -> 163 us
    reduce_scatter x8, waiting for transfers between devices: 2850 us -> 650 us  [the longest x2 325 us: group_scatter(): return lax.psum_scatter(partial, 'g', scatter_dimension=0, tiled=True)]
    unnamed x23, waiting for transfers between devices: 1940 us -> 156 us
    all_gather x9 -> x7, waiting for transfers between devices: 571 us -> 299 us  [the longest x2 125 us: group_gather(): return lax.all_gather(block, 'g', axis=0, tiled=True)]
    all_gather x4 -> x1, blocking collectives: 278 us -> 85.9 us  [gather_weights(): lax.all_gather(head_gains, both, axis=1, tiled=True)]
    dot_general x37 -> x30, matrix products: 277 us -> 219 us  [the longest x24 210 us: dot(): lax.dot_general(left, right, (((left_dim,), (right_dim,)), ((), ())), pre...]
  transfers between devices with their start and end apart: 24 -> 26, of which waited for: 19 -> 21; matrix products, arithmetic and copies ran while one was open for 4% -> 12% of each run, Pallas kernels for 0% -> 0%
where the time goes in v1:
time: 1720 us; the launch traced here: 1710 us
  waiting for transfers between devices  1130 us (66%)
  matrix products  219 us (13%)
  blocking collectives  163 us (9%)
  local copies, waits for them, and re-layouts  81.3 us (5%)
  other arithmetic  66.2 us (4%)
  starting transfers between devices  31 us (2%)
    reduce_scatter x2, waiting for transfers between devices, group_scatter(): return lax.psum_scatter(partial, 'g', scatter_dimension=0, tiled=True)  325 us
    dot_general x24, matrix products, dot(): lax.dot_general(left, right, (((left_dim,), (right_dim,)), ((), ())), pre...  210 us
    reduce_scatter x3, waiting for transfers between devices, spread(): grad = lax.psum_scatter(grad, 'pl', scatter_dimension=dim, tiled=True)  176 us
    unnamed x23, waiting for transfers between devices  156 us
    all_gather x2, waiting for transfers between devices, group_gather(): return lax.all_gather(block, 'g', axis=0, tiled=True)  125 us
    reduce_scatter x2, waiting for transfers between devices, column_chunks_back(): lax.psum_scatter(grad.astype(BF16), 'pl', scatter_dimension=0, tiled=True)  100 us
    all_gather x1, waiting for transfers between devices, gather_weights(): lax.all_gather(first, both, axis=0, tiled=True)  96.1 us
    all_gather x1, blocking collectives, gather_weights(): lax.all_gather(head_gains, both, axis=1, tiled=True)  85.9 us
  transfers between devices with their start and end apart: 26, of which 21 were waited for; matrix products, arithmetic and copies ran while one was open for 12% of the time, Pallas kernels for 0%

profile of v1, /device:TPU:1, one launch (start us, length us, event | category | flops | bytes accessed | tf_op | source)
XLA Modules:
  0.0 1709.3 jit_solution(12293138748879400752)
XLA Ops:
  14.9 6.5 all-to-all-start
  21.4 85.9 %all-gather = bf16[32,8,2]{1,2,0:T(2,128)(2,1)S(1)} all-gather(bf16[1,8,2]{1,2,0:T(2,128)(2,1)S(1)} %bitcast.299), channel_id=1, replica_groups=mesh['dp'=8,'seq'=4] {'dp','seq'}, dimensions={0}, use_global_device_ids=true | all-gather | bytes 1056 | tf_op jit(solution)/shard_map/all_gather | solution.py:359
  112.7 3.8 all-gather.11.cloned.1.call-done
  117.8 3.1 slice_reduce_fusion
  120.9 96.1 %all-gather.9.cloned.1.call-done = bf16[2048,3136]{1,0:T(8,128)(2,1)} async-done(((bf16[64,3136]{1,0:T(8,128)(2,1)}), bf16[2048,3136]{1,0:T(8,128)(2,1)}) %all-gather.9.cloned.1.call-update) | async-done | bytes 12845072 | tf_op jit(solution)/shard_map/all_gather | solution.py:357
  216.9 8.9 fusion.95
  235.9 3.2 collective-permute-start
  240.2 9.2 collective-permute-done
  249.4 5.5 collective-permute-start.1
  281.5 59.6 %all_to_all.20 = bf16[8,64,1024]{2,1,0:T(8,128)(2,1)} all-to-all(bf16[8,64,1024]{2,1,0:T(8,128)(2,1)} %reshape.414), channel_id=1, replica_groups=mesh['dp'=8,'seq'=4] {'dp':(4)2,'seq'}, dimensions={0} | all-to-all | bytes 2097152 | tf_op jit(solution)/shard_map/all_to_all | solution.py:88
  342.0 41.6 %all-gather.13.cloned.1.call-done = bf16[2048,2048]{1,0:T(8,128)(2,1)} async-done(((bf16[256,2048]{1,0:T(8,128)(2,1)}), bf16[2048,2048]{1,0:T(8,128)(2,1)}) %all-gather.13.cloned.1.call-update) | async-done | bytes 8388624 | tf_op jit(solution)/shard_map/all_gather | solution.py:77
  383.6 14.5 fusion.121
  398.1 37.6 %all-gather.17.cloned.1.call-done = bf16[2048,1024]{1,0:T(8,128)(2,1)} async-done(((bf16[512,1024]{1,0:T(8,128)(2,1)}), bf16[2048,1024]{1,0:T(8,128)(2,1)}) %all-gather.17.cloned.1.call-update) | async-done | bytes 4194320 | tf_op jit(solution)/shard_map/all_gather | solution.py:89
  435.7 17.6 %multiply_convert_fusion.1 = (bf16[2048,1024]{1,0:T(8,128)(2,1)}, f32[2048,1024]{1,0:T(8,128)}) fusion(f32[2048,1024]{1,0:T(8,128)} %fusion.121, bf16[2048,2048]{1,0:T(8,128)(2,1)} %all-gather.13.cloned.1.call-done, bf16[2048,1024]{1,0:T(8,128)(2,1)} %all-gather.17.cloned.1.call-done), kind=kOutput, calls=%fused_computation.15 | convolution fusion | flops 8610906112 | bytes 33554432 | tf_op jit(solution)/shard_map/dot_general | solution.py:21
  453.3 36.9 %all-gather.19.cloned.1.call-done = bf16[1024,2048]{1,0:T(8,128)(2,1)} async-done(((bf16[256,2048]{1,0:T(8,128)(2,1)}), bf16[1024,2048]{1,0:T(8,128)(2,1)}) %all-gather.19.cloned.1.call-update) | async-done | bytes 4194320 | tf_op jit(solution)/shard_map/all_gather | solution.py:141
  490.1 13.9 convolution_convert_fusion.2
  505.0 166.3 %reduce-scatter.22.cloned.1.call-done = bf16[256,2048]{1,0:T(8,128)(2,1)} async-done(((bf16[2048,2048]{1,0:T(8,128)(2,1)}), bf16[256,2048]{1,0:T(8,128)(2,1)}) %reduce-scatter.22.cloned.1.call-update) | async-done | bytes 1048592 | tf_op jit(solution)/shard_map/reduce_scatter | solution.py:81
  690.9 83.3 %all-gather.21.cloned.1.call-done = bf16[2048,2048]{1,0:T(8,128)(2,1)} async-done(((bf16[256,2048]{1,0:T(8,128)(2,1)}), bf16[2048,2048]{1,0:T(8,128)(2,1)}) %all-gather.21.cloned.1.call-update) | async-done | bytes 8388624 | tf_op jit(solution)/shard_map/all_gather | solution.py:77
  774.2 24.2 %multiply_convert_fusion = (bf16[2048,1024]{1,0:T(8,128)(2,1)}, bf16[2048,1024]{1,0:T(8,128)(2,1)}) fusion(f32[2048,1024]{1,0:T(8,128)} %fusion.121, f32[2048,1024]{1,0:T(8,128)} %get-tuple-element.161, bf16[2048,2048]{1,0:T(8,128)(2,1)} %all-gather.21.cloned.1.call-done, bf16[1024,2048]{1,0:T(8,128)(2,1)} %all-gather.19.cloned.1.call-done), kind=kOutput, calls=%fused_computation.14 | convolution fusion | flops 8638169088 | bytes 37748736 | tf_op jit(solution)/shard_map/dot_general | solution.py:21
  798.5 15.5 fusion.122
  813.9 16.3 add_convert_fusion
  836.9 158.8 %reduce-scatter.24.cloned.1.call-done = bf16[256,2048]{1,0:T(8,128)(2,1)} async-done(((bf16[2048,2048]{1,0:T(8,128)(2,1)}), bf16[256,2048]{1,0:T(8,128)(2,1)}) %reduce-scatter.24.cloned.1.call-update) | async-done | bytes 1048592 | tf_op jit(solution)/shard_map/reduce_scatter | solution.py:81
  997.9 4.3 multiply_reduce_fusion.1
  1005.2 6.9 fusion.25
  1013.6 3.9 fusion.61
  1029.3 8.9 collective-permute-done.2
  1041.7 5.7 convolution_convert_fusion.1
  1047.4 5.7 collective-permute-done.3
  1061.3 11.3 fusion.40
  1073.6 20.1 %pad_maximum_fusion = bf16[2048,2624]{0,1:T(8,128)(2,1)} fusion(bf16[2048,256]{0,1:T(8,128)(2,1)S(1)} %copy-done.31, bf16[2048,64]{0,1:T(8,128)(2,1)S(1)} %copy-done.48, bf16[2048,256]{0,1:T(8,128)(2,1)S(1)} %copy-done.30, bf16[2048,2048]{0,1:T(8,128)(2,1)} %convolution_convert_fusion.1), kind=kLoop, calls=%fused_computation.5 | loop fusion | flops 42991616 | bytes 21495808 | tf_op jit(solution)/shard_map/concatenate | solution.py:296
  1095.3 10.8 convolution_convert_fusion
  1106.7 14.9 convolution_convert_fusion.5
  1121.6 14.3 convolution_convert_fusion.4
  1136.2 14.4 convolution_convert_fusion.3
  1153.3 54.3 %reduce-scatter.28.cloned.1.call-done = bf16[512,2624]{0,1:T(8,128)(2,1)} async-done(((bf16[2048,2624]{0,1:T(8,128)(2,1)}), bf16[512,2624]{0,1:T(8,128)(2,1)}) %reduce-scatter.28.cloned.1.call-update) | async-done | bytes 2686992 | tf_op jit(solution)/shard_map/reduce_scatter | solution.py:293
  1207.6 4.5 copy.240
  1212.2 121.6 %reduce-scatter.26.cloned.1.call-done = bf16[512,3136]{0,1:T(8,128)(2,1)} async-done(((bf16[2048,3136]{0,1:T(8,128)(2,1)}), bf16[512,3136]{0,1:T(8,128)(2,1)}) %reduce-scatter.26.cloned.1.call-update) | async-done | bytes 3211280 | tf_op jit(solution)/shard_map/reduce_scatter | solution.py:293
  1333.8 5.7 copy.238
  1339.5 50.3 %reduce-scatter.30.cloned.1.call-done = bf16[512,1024]{1,0:T(8,128)(2,1)} async-done(((bf16[2048,1024]{1,0:T(8,128)(2,1)}), bf16[512,1024]{1,0:T(8,128)(2,1)}) %reduce-scatter.30.cloned.1.call-update) | async-done | bytes 1048592 | tf_op jit(solution)/shard_map/reduce_scatter | solution.py:95
  1389.8 5.4 all-to-all-start.2
  1395.2 50.1 %reduce-scatter.32.cloned.1.call-done = bf16[512,1024]{1,0:T(8,128)(2,1)} async-done(((bf16[2048,1024]{1,0:T(8,128)(2,1)}), bf16[512,1024]{1,0:T(8,128)(2,1)}) %reduce-scatter.32.cloned.1.call-update) | async-done | bytes 1048592 | tf_op jit(solution)/shard_map/reduce_scatter | solution.py:95
  1445.3 5.6 all-to-all-start.3
  1452.1 49.0 %reduce-scatter.34.cloned.1.call-done = bf16[256,2048]{1,0:T(8,128)(2,1)} async-done(((bf16[1024,2048]{1,0:T(8,128)(2,1)}), bf16[256,2048]{1,0:T(8,128)(2,1)}) %reduce-scatter.34.cloned.1.call-update) | async-done | bytes 1048592 | tf_op jit(solution)/shard_map/reduce_scatter | solution.py:229
  1517.5 10.2 reduce-scatter.44.cloned.1.call-done
  1528.5 17.8 %all-reduce = f32[2,64]{1,0:T(2,128)S(1)} all-reduce(f32[2,64]{1,0:T(2,128)S(1)} %copy.245), channel_id=14, replica_groups=mesh['dp'=8,'seq'=4] {'dp':(4)2,'seq'}, use_global_device_ids=true, to_apply=%region_43.45.clone | all-reduce | flops 128 | bytes 1024
  1546.9 16.1 reduce-scatter.42.cloned.1.call-done
  1564.4 60.6 %reduce-scatter.40.cloned.1.call-done = bf16[64,2624]{1,0:T(8,128)(2,1)} async-done(((bf16[512,2624]{1,0:T(8,128)(2,1)}), bf16[64,2624]{1,0:T(8,128)(2,1)}) %reduce-scatter.40.cloned.1.call-update) | async-done | bytes 335888
  1629.7 68.0 %reduce-scatter.38.cloned.1.call-done = bf16[64,3136]{1,0:T(8,128)(2,1)} async-done(((bf16[512,3136]{1,0:T(8,128)(2,1)}), bf16[64,3136]{1,0:T(8,128)(2,1)}) %reduce-scatter.38.cloned.1.call-update) | async-done | bytes 401424
  (383 shorter events, 143.7 us)
Async XLA Ops:
  7.2 109.3 %all-gather.11.cloned.1.call-start = ((), (), s32[]{:S(2)}) async-start(), calls=%async_computation.17 | async-start | bytes 11354112 | tf_op jit(solution)/shard_map/all_gather | solution.py:358
  10.7 206.2 %all-gather.9.cloned.1.call-start = ((), (), s32[]{:S(2)}) async-start(), calls=%async_computation.16 | async-start | bytes 13516800 | tf_op jit(solution)/shard_map/all_gather | solution.py:357
  14.9 95.5 %copy-start.10 = (bf16[256,2048]{1,0:T(8,128)(2,1)S(1)}, bf16[256,2048]{1,0:T(8,128)(2,1)}, u32[]{:S(2)}) copy-start(bf16[256,2048]{1,0:T(8,128)(2,1)} %param.20) | copy-start | bytes 3145732
  14.9 96.8 %all-to-all-start = ((bf16[8,64,1024]{2,1,0:T(8,128)(2,1)}), bf16[8,64,1024]{2,1,0:T(8,128)(2,1)S(1)}, u32[]{:S(2)}, u32[]{:S(2)}) async-start(bf16[8,64,1024]{2,1,0:T(8,128)(2,1)} %reshape.411), calls=%async_computation | async-start | bytes 2097152 | tf_op jit(solution)/shard_map/all_to_all | solution.py:88
  21.4 320.6 %all-gather.15.cloned.1.call-start = ((), (), s32[]{:S(2)}) async-start(), calls=%async_computation.19 | async-start | bytes 5242880 | tf_op jit(solution)/shard_map/all_gather | solution.py:89
  108.8 122.0 %copy-start.38 = (f32[256,128]{1,0:T(8,128)}, f32[256,128]{1,0:T(8,128)S(1)}, u32[]{:S(2)}) copy-start(f32[256,128]{1,0:T(8,128)S(1)} %get-tuple-element.151) | copy-start | bytes 393220
  110.7 10.2 copy-start.81
  110.7 166.0 %copy-start.83 = (f32[256]{0:T(256)}, f32[256]{0:T(256)S(1)}, u32[]{:S(2)}) copy-start(f32[256]{0:T(256)S(1)} %add_rsqrt_fusion.8) | copy-start | bytes 3076
  110.7 118.9 %copy-start.73 = (f32[1,256]{1,0:T(1,128)}, f32[1,256]{1,0:T(1,128)S(1)}, u32[]{:S(2)}) copy-start(f32[1,256]{1,0:T(1,128)S(1)} %get-tuple-element.148) | copy-start | bytes 3076
  110.7 129.1 %copy-start.76 = (f32[1,256]{1,0:T(1,128)}, f32[1,256]{1,0:T(1,128)S(1)}, u32[]{:S(2)}) copy-start(f32[1,256]{1,0:T(1,128)S(1)} %get-tuple-element.147) | copy-start | bytes 3076
  112.7 270.9 %all-gather.13.cloned.1.call-start = ((), (), s32[]{:S(2)}) async-start(), calls=%async_computation.18 | async-start | bytes 9437184 | tf_op jit(solution)/shard_map/all_gather | solution.py:77
  120.8 155.8 %copy-start.60 = (f32[2048]{0:T(1024)}, f32[2048]{0:T(1024)S(1)}, u32[]{:S(2)}) copy-start(f32[2048]{0:T(1024)S(1)} %get-tuple-element.114) | copy-start | bytes 24580
  225.9 34.5 %copy-start = (f32[256,3136]{0,1:T(8,128)}, f32[256,3136]{0,1:T(8,128)S(1)}, u32[]{:S(2)}) copy-start(f32[256,3136]{0,1:T(8,128)S(1)} %fusion.95) | copy-start | bytes 9633796
  235.9 13.5 collective-permute-start
  239.9 15.0 copy-start.46
  239.9 15.0 copy-start.53
  249.4 14.6 collective-permute-start.1
  262.0 14.7 copy-start.2
  279.2 156.5 %all-gather.17.cloned.1.call-start = ((), (), s32[]{:S(2)}) async-start(), calls=%async_computation.20 | async-start | bytes 5242880 | tf_op jit(solution)/shard_map/all_gather | solution.py:89
  341.2 149.0 %all-gather.19.cloned.1.call-start = ((), (), s32[]{:S(2)}) async-start(), calls=%async_computation.21 | async-start | bytes 5242880 | tf_op jit(solution)/shard_map/all_gather | solution.py:141
  341.7 329.6 %reduce-scatter.22.cloned.1.call-start = ((), (), s32[]{:S(2)}) async-start(), calls=%async_computation.22 | async-start | bytes 9437184 | tf_op jit(solution)/shard_map/reduce_scatter | solution.py:81
  504.1 270.2 %all-gather.21.cloned.1.call-start = ((), (), s32[]{:S(2)}) async-start(), calls=%async_computation.23 | async-start | bytes 9437184 | tf_op jit(solution)/shard_map/all_gather | solution.py:77
  690.9 304.8 %reduce-scatter.24.cloned.1.call-start = ((), (), s32[]{:S(2)}) async-start(), calls=%async_computation.24 | async-start | bytes 9437184 | tf_op jit(solution)/shard_map/reduce_scatter | solution.py:81
  798.5 15.5 copy-start.90
  830.3 321.4 %reduce-scatter.36.cloned.1.call-start = ((), (), s32[]{:S(2)}) async-start(), calls=%async_computation.30 | async-start | bytes 81920 | tf_op jit(solution)/shard_map/reduce_scatter | solution.py:293
  1005.2 12.3 slice-start
  1023.1 15.1 collective-permute-start.2
  1029.3 10.6 copy-start.59
  1029.3 10.6 copy-start.57
  1038.4 14.7 collective-permute-start.3
  1061.2 11.4 copy-start.54
  1061.3 11.3 copy-start.86
  1061.3 12.3 copy-start.30
  1061.3 12.3 copy-start.31
  1061.3 12.3 copy-start.48
  1073.3 134.3 %reduce-scatter.28.cloned.1.call-start = ((), (), s32[]{:S(2)}) async-start(), calls=%async_computation.26 | async-start | bytes 13434880 | tf_op jit(solution)/shard_map/reduce_scatter | solution.py:293
  1093.8 240.0 %reduce-scatter.26.cloned.1.call-start = ((), (), s32[]{:S(2)}) async-start(), calls=%async_computation.25 | async-start | bytes 16056320 | tf_op jit(solution)/shard_map/reduce_scatter | solution.py:293
  1106.2 283.6 %reduce-scatter.30.cloned.1.call-start = ((), (), s32[]{:S(2)}) async-start(), calls=%async_computation.27 | async-start | bytes 5242880 | tf_op jit(solution)/shard_map/reduce_scatter | solution.py:95
  1121.6 323.8 %reduce-scatter.32.cloned.1.call-start = ((), (), s32[]{:S(2)}) async-start(), calls=%async_computation.28 | async-start | bytes 5242880 | tf_op jit(solution)/shard_map/reduce_scatter | solution.py:95
  1136.0 365.2 %reduce-scatter.34.cloned.1.call-start = ((), (), s32[]{:S(2)}) async-start(), calls=%async_computation.29 | async-start | bytes 5242880 | tf_op jit(solution)/shard_map/reduce_scatter | solution.py:229
  1150.6 377.1 %reduce-scatter.44.cloned.1.call-start = ((), (), s32[]{:S(2)}) async-start(), calls=%async_computation.34 | async-start | bytes 163840
  1151.6 411.4 %reduce-scatter.42.cloned.1.call-start = ((), (), s32[]{:S(2)}) async-start(), calls=%async_computation.33 | async-start | bytes 294912
  1153.3 471.8 %reduce-scatter.40.cloned.1.call-start = ((), (), s32[]{:S(2)}) async-start(), calls=%async_computation.32 | async-start | bytes 3096576
  1212.2 485.5 %reduce-scatter.38.cloned.1.call-start = ((), (), s32[]{:S(2)}) async-start(), calls=%async_computation.31 | async-start | bytes 3686400
  1389.8 61.1 %copy-start.91 = (u32[32]{0:T(128)S(1)}, u32[32]{0:T(128)}, u32[]{:S(2)}) copy-start(u32[32]{0:T(128)} %constant.78) | copy-start | bytes 388
  1389.8 55.5 %all-to-all-start.2 = ((bf16[8,64,1024]{2,1,0:T(8,128)(2,1)}), bf16[8,64,1024]{2,1,0:T(8,128)(2,1)S(1)}, u32[]{:S(2)}, u32[]{:S(2)}) async-start(bf16[8,64,1024]{2,1,0:T(8,128)(2,1)} %bitcast.270), calls=%async_computation.7 | async-start | bytes 2097152 | tf_op jit(solution)/shard_map/all_to_all | solution.py:98
  1445.3 55.8 %copy-start.25 = (bf16[8,64,1024]{2,1,0:T(8,128)(2,1)}, bf16[8,64,1024]{2,1,0:T(8,128)(2,1)S(1)}, u32[]{:S(2)}) copy-start(bf16[8,64,1024]{2,1,0:T(8,128)(2,1)S(1)} %all-to-all-done.2) | copy-start | bytes 3145732
  1445.3 64.4 %all-to-all-start.3 = ((bf16[8,64,1024]{2,1,0:T(8,128)(2,1)}), bf16[8,64,1024]{2,1,0:T(8,128)(2,1)}, u32[]{:S(2)}, u32[]{:S(2)}) async-start(bf16[8,64,1024]{2,1,0:T(8,128)(2,1)} %bitcast.269), calls=%async_computation.9 | async-start | bytes 2097152 | tf_op jit(solution)/shard_map/all_to_all | solution.py:98
  (75 other events, 208.8 us)
Sparse Core Ops, SparseCore 0:
  11.4 105.0 all-gather.10
  119.9 96.9 all-gather.8
  219.3 50.4 all-gather.14
  279.3 104.2 all-gather.12
  385.3 50.3 all-gather.16
  437.4 52.6 all-gather.18
  504.2 167.0 reduce-scatter.21
  691.0 83.2 all-gather.20
  830.4 165.2 reduce-scatter.23
  1073.4 24.5 reduce-scatter.35
  1101.4 106.1 reduce-scatter.27
  1210.9 122.8 reduce-scatter.25
  1337.0 52.6 reduce-scatter.29
  1392.6 52.6 reduce-scatter.31
  1448.4 52.6 reduce-scatter.33
  1504.3 23.3 reduce-scatter.43
  1530.4 32.4 reduce-scatter.41
  1565.1 59.8 reduce-scatter.39
  1627.4 70.2 reduce-scatter.37

commit v2 on v1

v2 whole, which is shorter than its diff:
```python
import jax
import jax.numpy as jnp
from jax import lax
from jax.experimental import pallas as pl
from jax.experimental.pallas import tpu as pltpu
from jax.sharding import Mesh, PartitionSpec as P

QUERY_HEADS = 8
KEY_VALUE_HEADS = 2
HEAD_SIZE = 256
WINDOW = 512
EPSILON = 1e-06
ROPE_BASE = 10000.0
HALF_ROOT = 0.7071067811865476
MASKED = -1e30
GELU_SCALE = 0.7978845608028654
GELU_CUBE = 0.044715
F32 = jnp.float32
BF16 = jnp.bfloat16


def dot(left, right, left_dim=1, right_dim=0):
    return lax.dot_general(
        left, right, (((left_dim,), (right_dim,)), ((), ())), preferred_element_type=F32
    )


def inverse_rms(value):
    return lax.rsqrt(jnp.mean(value * value, axis=-1, keepdims=True) + EPSILON)


def rms_back(value, inverse, gain, grad):
    scaled = grad * gain
    inner = jnp.mean(scaled * value, axis=-1, keepdims=True)
    unit = value * inverse
    return inverse * (scaled - unit * (inverse * inner)), grad * unit


def rope_tables(positions):
    half = HEAD_SIZE // 2
    rate = ROPE_BASE ** (-jnp.arange(half, dtype=F32) * 2.0 / HEAD_SIZE)
    angle = positions.astype(F32)[:, None] * rate[None, :]
    return jnp.cos(angle)[:, None, :], jnp.sin(angle)[:, None, :]


def rotate(value, cosine, sine):
    half = value.shape[-1] // 2
    first, second = value[..., :half], value[..., half:]
    return jnp.concatenate(
        [first * cosine - second * sine, second * cosine + first * sine], axis=-1
    )


def gelu_tanh(value):
    return jnp.tanh(GELU_SCALE * (value + GELU_CUBE * value * value * value))


def gelu(value):
    return 0.5 * value * (1.0 + gelu_tanh(value))


def gelu_slope(value):
    t = gelu_tanh(value)
    inner = GELU_SCALE * (1.0 + 3.0 * GELU_CUBE * value * value)
    return 0.5 * (1.0 + t) + 0.5 * value * (1.0 - t * t) * inner


AXES = ("y", "xc", "h", "l")
TEAM = ("xc", "l")
COPIES = ("y", "h")


class Sender:
    def __init__(self, send, recv):
        self.send, self.recv, self.count, self.started = send, recv, 0, []

    def go(self, source, target, peer):
        i = self.count
        self.count += 1
        copy = pltpu.make_async_remote_copy(
            src_ref=source,
            dst_ref=target,
            send_sem=self.send.at[i],
            recv_sem=self.recv.at[i],
            device_id=peer,
            device_id_type=pl.DeviceIdType.MESH,
        )
        copy.start()
        self.started.append(copy)
        return copy

    def finish(self):
        for copy in self.started:
            copy.wait_send()


def greet(peers):
    barrier = pltpu.get_barrier_semaphore()
    for peer in peers:
        pl.semaphore_signal(barrier, inc=1, device_id=peer, device_id_type=pl.DeviceIdType.MESH)
    pl.semaphore_wait(barrier, len(peers))


def plus(*parts):
    total = parts[0].astype(F32)
    for part in parts[1:]:
        total = total + part.astype(F32)
    return total


def remote_call(kernel, out, copies, identity, scratch=(), vmem=None, out_space=pl.ANY):
    return pl.pallas_call(
        kernel,
        out_shape=out,
        in_specs=[pl.BlockSpec(memory_space=pl.ANY)],
        out_specs=pl.BlockSpec(memory_space=out_space),
        scratch_shapes=[
            pltpu.SemaphoreType.DMA((copies,)),
            pltpu.SemaphoreType.DMA((copies,)),
            *scratch,
        ],
        compiler_params=pltpu.CompilerParams(
            collective_id=identity, has_side_effects=True, vmem_limit_bytes=vmem
        ),
    )


def team_places():
    xc, l = lax.axis_index("xc"), lax.axis_index("l")
    core = lax.rem(xc, 2)
    other = xc + 1 - 2 * core
    cross, side = lax.rem(xc + 2, 4), 1 - l
    own = {"O": xc * 2 + l, "X": cross * 2 + l, "L": xc * 2 + side, "D": cross * 2 + side}
    far = lax.rem(other + 2, 4)
    twin = {"O": other * 2 + l, "X": far * 2 + l, "L": other * 2 + side, "D": far * 2 + side}
    return own, twin, {"xc": other}, {"xc": cross}, {"l": side}


def team_gather_kernel(x_ref, o_ref, send, recv, local):
    own, _, core, cross, side = team_places()
    half = x_ref.shape[0] // 2
    top, low = pl.ds(0, half), pl.ds(half, half)
    keep = pltpu.make_async_copy(x_ref, o_ref.at[own["O"]], local)
    keep.start()
    greet([core, cross, side])
    out = Sender(send, recv)
    mine, from_side, from_cross = o_ref.at[own["O"]], o_ref.at[own["L"]], o_ref.at[own["X"]]
    diagonal = o_ref.at[own["D"]]
    side_top = out.go(x_ref.at[top], mine.at[top], side)
    cross_low = out.go(x_ref.at[low], mine.at[low], cross)
    side_low = out.go(x_ref.at[low], mine.at[low], side)
    cross_top = out.go(x_ref.at[top], mine.at[top], cross)
    twins = [out.go(x_ref, mine, core)]
    side_top.wait_recv()
    diagonal_top = out.go(from_side.at[top], from_side.at[top], cross)
    twins.append(out.go(from_side.at[top], from_side.at[top], core))
    cross_low.wait_recv()
    diagonal_low = out.go(from_cross.at[low], from_cross.at[low], side)
    twins.append(out.go(from_cross.at[low], from_cross.at[low], core))
    side_low.wait_recv()
    twins.append(out.go(from_side.at[low], from_side.at[low], core))
    cross_top.wait_recv()
    twins.append(out.go(from_cross.at[top], from_cross.at[top], core))
    diagonal_top.wait_recv()
    twins.append(out.go(diagonal.at[top], diagonal.at[top], core))
    diagonal_low.wait_recv()
    twins.append(out.go(diagonal.at[low], diagonal.at[low], core))
    for copy in twins:
        copy.wait_recv()
    out.finish()
    keep.wait()


def team_gather(block):
    rows, width = block.shape
    gathered = remote_call(
        team_gather_kernel,
        jax.ShapeDtypeStruct((8, rows, width), block.dtype),
        13,
        0,
        [pltpu.SemaphoreType.DMA],
    )(block)
    return gathered.reshape(8 * rows, width)


def team_scatter_kernel(p_ref, o_ref, send, recv, local, mine, twin_in, cross_in, side_in, bent_in):
    own, twin, core, cross, side = team_places()
    half = p_ref.shape[1] // 2
    top, low = pl.ds(0, half), pl.ds(half, half)
    loads = []
    for i, k in enumerate("DXLO"):
        loads.append(pltpu.make_async_copy(p_ref.at[own[k]], mine.at[i], local.at[i]))
        loads[-1].start()
    greet([core, cross, side])
    out = Sender(send, recv)
    swaps = [out.go(p_ref.at[twin[k]], twin_in.at[i], core) for i, k in enumerate("DXLO")]

    def join(i):
        loads[i].wait()
        swaps[i].wait_recv()
        mine[i] = plus(mine[i], twin_in[i]).astype(BF16)

    join(0)
    bent_cross = out.go(mine.at[0].at[top], bent_in.at[0], cross)
    bent_side = out.go(mine.at[0].at[low], bent_in.at[1], side)
    join(1)
    cross_top = out.go(mine.at[1].at[top], cross_in.at[top], cross)
    join(2)
    side_low = out.go(mine.at[2].at[low], side_in.at[low], side)
    bent_cross.wait_recv()
    mine[2, top] = plus(mine[2, top], bent_in[0]).astype(BF16)
    side_top = out.go(mine.at[2].at[top], side_in.at[top], side)
    bent_side.wait_recv()
    mine[1, low] = plus(mine[1, low], bent_in[1]).astype(BF16)
    cross_low = out.go(mine.at[1].at[low], cross_in.at[low], cross)
    loads[3].wait()
    swaps[3].wait_recv()
    o_ref[...] = plus(mine[3], twin_in[3])
    cross_top.wait_recv()
    side_low.wait_recv()
    o_ref[top] += cross_in[top].astype(F32)
    o_ref[low] += side_in[low].astype(F32)
    side_top.wait_recv()
    cross_low.wait_recv()
    o_ref[top] += side_in[top].astype(F32)
    o_ref[low] += cross_in[low].astype(F32)
    out.finish()


def team_scatter(partial_sum):
    rows, width = partial_sum.shape[0] // 8, partial_sum.shape[1]
    return remote_call(
        team_scatter_kernel,
        jax.ShapeDtypeStruct((rows, width), F32),
        10,
        1,
        [
            pltpu.SemaphoreType.DMA((4,)),
            pltpu.VMEM((4, rows, width), BF16),
            pltpu.VMEM((4, rows, width), BF16),
            pltpu.VMEM((rows, width), BF16),
            pltpu.VMEM((rows, width), BF16),
            pltpu.VMEM((2, rows // 2, width), BF16),
        ],
        40 * 2**20,
        pltpu.VMEM,
    )(partial_sum.reshape(8, rows, width))


def team_swap_kernel(x_ref, o_ref, send, recv, local):
    xc, l = lax.axis_index("xc"), lax.axis_index("l")
    me = xc * 2 + l
    keep = pltpu.make_async_copy(x_ref.at[me], o_ref.at[me], local)
    keep.start()
    places = []
    for i in range(1, 8):
        far, side = lax.rem(xc + i // 2, 4), lax.rem(l + i % 2, 2)
        back = lax.rem(xc + 4 - i // 2, 4)
        places.append((far * 2 + side, {"xc": far, "l": side}, back * 2 + side))
    greet([peer for _, peer, _ in places])
    out = Sender(send, recv)
    for rank, peer, _ in places:
        out.go(x_ref.at[rank], o_ref.at[me], peer)
    for copy in out.started:
        copy.wait_recv()
    out.finish()
    keep.wait()


def team_swap(blocks):
    return remote_call(
        team_swap_kernel,
        jax.ShapeDtypeStruct(blocks.shape, blocks.dtype),
        7,
        2,
        [pltpu.SemaphoreType.DMA],
    )(blocks)


def full_places():
    y, xc = lax.axis_index("y"), lax.axis_index("xc")
    h, l = lax.axis_index("h"), lax.axis_index("l")
    core = lax.rem(xc, 2)

    def rank(plane, depth, twin=False):
        b = xc + 1 - 2 * core if twin else xc
        b = lax.rem(b + 2, 4) if plane in "XD" else b
        a = 1 - y if plane in "YD" else y
        u = 1 - h if depth in ("H", "HL") else h
        v = 1 - l if depth in ("L", "HL") else l
        return ((a * 4 + b) * 2 + u) * 2 + v

    peers = {
        "C": {"xc": xc + 1 - 2 * core},
        "X": {"xc": lax.rem(xc + 2, 4)},
        "Y": {"y": 1 - y},
        "H": {"h": 1 - h},
        "L": {"l": 1 - l},
    }
    return rank, peers


DEPTHS = ("O", "L", "H", "HL")


def full_gather_kernel(x_ref, o_ref, send, recv, local):
    rank, peers = full_places()
    half = x_ref.shape[0] // 2
    top, low = pl.ds(0, half), pl.ds(half, half)

    def at(plane, depth):
        return o_ref.at[rank(plane, depth)]

    keep = pltpu.make_async_copy(x_ref, at("O", "O"), local)
    keep.start()
    greet(list(peers.values()))
    out = Sender(send, recv)
    twins = []
    to_h = out.go(x_ref, at("O", "O"), peers["H"])
    to_l = out.go(x_ref, at("O", "O"), peers["L"])
    direct, bent = {}, {}

    def begin(depth):
        source = x_ref if depth == "O" else at("O", depth)
        target = at("O", depth)
        y_top = out.go(source.at[top], target.at[top], peers["Y"])
        x_low = out.go(source.at[low], target.at[low], peers["X"])
        y_low = out.go(source.at[low], target.at[low], peers["Y"])
        x_top = out.go(source.at[top], target.at[top], peers["X"])
        twins.append(out.go(source, target, peers["C"]))
        direct[depth] = (y_top, x_low, y_low, x_top)

    def bend(depth):
        y_top, x_low, y_low, x_top = direct[depth]
        y_top.wait_recv()
        piece = at("Y", depth).at[top]
        bent_top = out.go(piece, piece, peers["X"])
        x_low.wait_recv()
        piece = at("X", depth).at[low]
        bent_low = out.go(piece, piece, peers["Y"])
        y_low.wait_recv()
        twins.append(out.go(at("Y", depth), at("Y", depth), peers["C"]))
        x_top.wait_recv()
        twins.append(out.go(at("X", depth), at("X", depth), peers["C"]))
        bent[depth] = (bent_top, bent_low)

    def close(depth):
        for copy in bent[depth]:
            copy.wait_recv()
        twins.append(out.go(at("D", depth), at("D", depth), peers["C"]))

    begin("O")
    to_h.wait_recv()
    to_hl = out.go(at("O", "H"), at("O", "H"), peers["L"])
    to_l.wait_recv()
    begin("L")
    bend("O")
    begin("H")
    bend("L")
    to_hl.wait_recv()
    begin("HL")
    bend("H")
    close("O")
    close("L")
    bend("HL")
    close("H")
    close("HL")
    for copy in twins:
        copy.wait_recv()
    out.finish()
    keep.wait()


def full_gather(block):
    rows, width = block.shape
    if lax.axis_size("y") != 2 or lax.axis_size("h") != 2:
        gathered = lax.all_gather(block, AXES, axis=0, tiled=False)
    else:
        gathered = remote_call(
            full_gather_kernel,
            jax.ShapeDtypeStruct((32, rows, width), block.dtype),
            43,
            3,
            [pltpu.SemaphoreType.DMA],
        )(block)
    return gathered.reshape(-1, width)


PLANES = ("D", "X", "Y", "O")
SUMS = ("HL", "L", "H", "O")


def full_scatter_kernel(
    p_ref, o_ref, send, recv, local, mine, twin_in, cross_in, lane_in, bent_in, depth_in
):
    rank, peers = full_places()
    half = p_ref.shape[1] // 2
    top, low = pl.ds(0, half), pl.ds(half, half)
    loads, swaps, flights = {}, {}, {}
    for t, depth in enumerate(SUMS):
        for k, plane in enumerate(PLANES):
            load = pltpu.make_async_copy(
                p_ref.at[rank(plane, depth)], mine.at[t, k], local.at[t * 4 + k]
            )
            load.start()
            loads[t, k] = load
    greet(list(peers.values()))
    out = Sender(send, recv)
    for t, depth in enumerate(SUMS):
        for k, plane in enumerate(PLANES):
            swaps[t, k] = out.go(
                p_ref.at[rank(plane, depth, True)], twin_in.at[t, k], peers["C"]
            )

    def join(t, k):
        loads[t, k].wait()
        swaps[t, k].wait_recv()
        mine[t, k] = plus(mine[t, k], twin_in[t, k]).astype(BF16)

    def begin(t):
        join(t, 0)
        bent_x = out.go(mine.at[t, 0].at[top], bent_in.at[t, 0], peers["X"])
        bent_y = out.go(mine.at[t, 0].at[low], bent_in.at[t, 1], peers["Y"])
        join(t, 1)
        x_top = out.go(mine.at[t, 1].at[top], cross_in.at[t].at[top], peers["X"])
        join(t, 2)
        y_low = out.go(mine.at[t, 2].at[low], lane_in.at[t].at[low], peers["Y"])
        join(t, 3)
        flights[t] = [bent_x, bent_y, x_top, y_low]

    def bend(t):
        bent_x, bent_y, x_top, y_low = flights[t]
        bent_x.wait_recv()
        mine[t, 2, top] = plus(mine[t, 2, top], bent_in[t, 0]).astype(BF16)
        y_top = out.go(mine.at[t, 2].at[top], lane_in.at[t].at[top], peers["Y"])
        bent_y.wait_recv()
        mine[t, 1, low] = plus(mine[t, 1, low], bent_in[t, 1]).astype(BF16)
        x_low = out.go(mine.at[t, 1].at[low], cross_in.at[t].at[low], peers["X"])
        flights[t] = [x_top, y_low, y_top, x_low]

    def close(t):
        for copy in flights[t]:
            copy.wait_recv()
        return plus(mine[t, 3], cross_in[t], lane_in[t])

    begin(0)
    begin(1)
    bend(0)
    begin(2)
    bend(1)
    mine[0, 3] = close(0).astype(BF16)
    to_hl = out.go(mine.at[0, 3], depth_in.at[0], peers["L"])
    begin(3)
    bend(2)
    mine[1, 3] = close(1).astype(BF16)
    to_l = out.go(mine.at[1, 3], depth_in.at[1], peers["L"])
    bend(3)
    total = close(2)
    to_hl.wait_recv()
    mine[2, 3] = plus(total, depth_in[0]).astype(BF16)
    to_h = out.go(mine.at[2, 3], depth_in.at[2], peers["H"])
    total = close(3)
    to_l.wait_recv()
    total = plus(total, depth_in[1])
    to_h.wait_recv()
    o_ref[...] = plus(total, depth_in[2])
    out.finish()


def full_scatter(partial_sum):
    shares = lax.axis_size("y") * lax.axis_size("h") * 8
    rows, width = partial_sum.shape[0] // shares, partial_sum.shape[1]
    blocks = partial_sum.reshape(shares, rows, width)
    if lax.axis_size("y") != 2 or lax.axis_size("h") != 2:
        return lax.psum_scatter(blocks, AXES, scatter_dimension=0, tiled=False).astype(F32)
    return remote_call(
        full_scatter_kernel,
        jax.ShapeDtypeStruct((rows, width), F32),
        43,
        4,
        [
            pltpu.SemaphoreType.DMA((16,)),
            pltpu.VMEM((4, 4, rows, width), BF16),
            pltpu.VMEM((4, 4, rows, width), BF16),
            pltpu.VMEM((4, rows, width), BF16),
            pltpu.VMEM((4, rows, width), BF16),
            pltpu.VMEM((4, 2, rows // 2, width), BF16),
            pltpu.VMEM((3, rows, width), BF16),
        ],
        56 * 2**20,
        pltpu.VMEM,
    )(blocks)


def shift(block, distance):
    pieces = lax.axis_size("h") * lax.axis_size("l")
    route = [(i, i + distance) for i in range(pieces) if 0 <= i + distance < pieces]
    return lax.ppermute(block, ("h", "l"), route)


def pull(block, axis, distance):
    size = lax.axis_size(axis)
    return lax.ppermute(block, axis, [(i, (i - distance) % size) for i in range(size)])


def copies_place(dy, dh):
    ys, hs = lax.axis_size("y"), lax.axis_size("h")
    y, h = lax.axis_index("y"), lax.axis_index("h")
    return lax.rem(y + dy, ys) * hs + lax.rem(h + dh, hs)


def copies_gather(block):
    ys, hs = lax.axis_size("y"), lax.axis_size("h")
    along = [block] + [pull(block, "h", k) for k in range(1, hs)]
    gathered = jnp.zeros((ys * hs * block.shape[0], block.shape[1]), block.dtype)
    for dy in range(ys):
        for dh in range(hs):
            piece = along[dh] if dy == 0 else pull(along[dh], "y", dy)
            start = copies_place(dy, dh) * block.shape[0]
            gathered = lax.dynamic_update_slice_in_dim(gathered, piece, start, axis=0)
    return gathered


def copies_scatter(partial_sum):
    ys, hs = lax.axis_size("y"), lax.axis_size("h")
    rows = partial_sum.shape[0] // (ys * hs)

    def piece(dy, dh):
        return lax.dynamic_slice_in_dim(partial_sum, copies_place(dy, dh) * rows, rows, axis=0)

    along = []
    for dh in range(hs):
        arrived = [pull(piece(dy, dh), "y", -dy) for dy in range(1, ys)]
        along.append((piece(0, dh), arrived))
    ready = [plus(own, *arrived).astype(BF16) for own, arrived in along[1:]]
    moved = [pull(ready[dh - 1], "h", -dh) for dh in range(1, hs)]
    return plus(along[0][0], *along[0][1], *moved)


def column_blocks(weight):
    ys, hs = lax.axis_size("y"), lax.axis_size("h")
    depth, width = weight.shape
    split = weight.reshape(depth, ys, 4, hs, 2, width // (ys * hs * 8))
    return split.transpose(2, 4, 0, 1, 3, 5).reshape(8, depth, width // 8)


def from_column_blocks(blocks):
    ys, hs = lax.axis_size("y"), lax.axis_size("h")
    depth, width = blocks.shape[1:]
    split = blocks.reshape(4, 2, depth, ys, hs, width // (ys * hs)).transpose(2, 3, 0, 4, 1, 5)
    return split.reshape(depth, 8 * width)


def depth_order(value):
    ys, hs = lax.axis_size("y"), lax.axis_size("h")
    rows, width = value.shape
    split = value.reshape(rows, ys, 4, hs, width // (4 * ys * hs))
    return split.transpose(0, 1, 3, 2, 4).reshape(rows, width)


def from_depth_order(value):
    ys, hs = lax.axis_size("y"), lax.axis_size("h")
    rows, width = value.shape
    split = value.reshape(rows, ys, hs, 4, width // (4 * ys * hs))
    return split.transpose(0, 1, 3, 2, 4).reshape(rows, width)


def layer(*args):
    (
        hidden_in,
        layer_input,
        seq_lengths,
        cotangent,
        query_weight,
        key_matrix,
        value_matrix,
        output_weight,
        laurel_left,
        laurel_right,
        input_gate,
        input_projection,
        gate_weight,
        up_weight,
        down_weight,
        norm_gains,
        head_gains,
    ) = args
    rows, width = hidden_in.shape
    hops = max(1, WINDOW // rows)
    groups = QUERY_HEADS // KEY_VALUE_HEADS
    piece = lax.axis_index(("h", "l"))
    places = piece * rows + jnp.arange(rows, dtype=jnp.int32)
    key_places = (piece - hops) * rows + jnp.arange((hops + 1) * rows, dtype=jnp.int32)
    live = (places < seq_lengths[0]).astype(F32)[:, None]

    head_width = QUERY_HEADS * HEAD_SIZE
    kv_width = KEY_VALUE_HEADS * HEAD_SIZE
    rank = laurel_left.shape[1]
    side = layer_input.shape[1]
    depth, head_part = query_weight.shape[0], head_gains.shape[1]
    columns = (
        query_weight,
        key_matrix,
        value_matrix,
        output_weight,
        input_gate,
        input_projection.T,
        laurel_left,
        laurel_right.T,
        norm_gains.T,
        jnp.pad(head_gains.T, ((0, depth - head_part), (0, 0))),
    )
    edges = [0]
    for column in columns:
        edges.append(edges[-1] + column.shape[1])
    full_width = -(-edges[-1] // 128) * 128
    swapped = team_swap(
        jnp.concatenate([column_blocks(gate_weight), column_blocks(up_weight)], axis=1)
    )
    gate_cols = copies_gather(swapped[:, :depth].reshape(8 * depth, -1))
    up_cols = copies_gather(swapped[:, depth:].reshape(8 * depth, -1))
    down_rows = copies_gather(down_weight)
    full = full_gather(
        jnp.pad(jnp.concatenate(columns, axis=1), ((0, 0), (0, full_width - edges[-1])))
    )
    first = full[:, : edges[3]]
    output_all, side_gate_all, projection_all, left_all, right_all = (
        full[:, edges[i] : edges[i + 1]] for i in range(3, 8)
    )
    gains = full[:, edges[8] : edges[9]].T.astype(F32)
    head_gain = (
        full[:, edges[9] : edges[10]].reshape(-1, depth, 2)[:, :head_part].reshape(-1, 2).T
    ).astype(F32)

    hidden = hidden_in.astype(F32)
    side_input = layer_input.astype(F32)
    cosine, sine = rope_tables(places)

    hidden_inv = inverse_rms(hidden)
    normed = hidden * hidden_inv * gains[0]
    normed_low = normed.astype(BF16)
    raw = dot(normed_low, first)
    query_raw = raw[:, :head_width].reshape(rows, QUERY_HEADS, HEAD_SIZE)
    key_raw = raw[:, head_width : head_width + kv_width].reshape(rows, KEY_VALUE_HEADS, HEAD_SIZE)
    value_raw = raw[:, head_width + kv_width :].reshape(
        rows, KEY_VALUE_HEADS, HEAD_SIZE
    )
    left_low = dot(normed_low, left_all).astype(BF16)
    query_inv = inverse_rms(query_raw)
    key_inv = inverse_rms(key_raw)
    value_inv = inverse_rms(value_raw)
    query_low = rotate(query_raw * query_inv * head_gain[0], cosine, sine).astype(BF16)
    key_low = rotate(key_raw * key_inv * head_gain[1], cosine, sine).astype(BF16)
    value_low = (value_raw * value_inv).astype(BF16)
    moving = jnp.stack([key_low, value_low])
    window = jnp.concatenate([shift(moving, hop) for hop in range(hops, 0, -1)] + [moving], axis=1)
    grouped = query_low.reshape(rows, KEY_VALUE_HEADS, groups, HEAD_SIZE)
    scores = jnp.einsum("qkgd,tkd->kgqt", grouped, window[0], preferred_element_type=F32)
    allowed = (
        (key_places[None, :] <= places[:, None])
        & (places[:, None] - key_places[None, :] < WINDOW)
        & (key_places[None, :] >= 0)
    )
    scores = jnp.where(allowed, scores, MASKED)
    weights = jnp.exp(scores - jnp.max(scores, axis=-1, keepdims=True))
    probs = weights / jnp.sum(weights, axis=-1, keepdims=True)
    probs_low = probs.astype(BF16)
    mixed = (
        jnp.einsum("kgqt,tkd->qkgd", probs_low, window[1], preferred_element_type=F32)
        .reshape(rows, head_width)
        .astype(BF16)
    )
    attention_raw = dot(mixed, output_all)
    attention_inv = inverse_rms(attention_raw)
    right_raw = dot(left_low, right_all, 1, 1)
    right_inv = inverse_rms(right_raw)
    merged = (
        hidden
        + attention_raw * attention_inv * gains[1]
        + normed
        + right_raw * right_inv * gains[2]
    ) * HALF_ROOT
    merged_inv = inverse_rms(merged)
    expand_low = (merged * merged_inv * gains[3]).astype(BF16)

    expand_all = team_gather(depth_order(expand_low))
    gate_raw = dot(expand_all, gate_cols)
    up_raw = dot(expand_all, up_cols)
    act_low = (gelu(gate_raw) * up_raw).astype(BF16)
    reduced_raw = team_scatter(dot(act_low, down_rows).astype(BF16))
    reduced_inv = inverse_rms(reduced_raw)
    after_feed = merged + reduced_raw * reduced_inv * gains[4]
    after_low = after_feed.astype(BF16)
    side_raw = dot(after_low, side_gate_all)
    side_low = (gelu(side_raw) * side_input).astype(BF16)
    side_out = dot(side_low, projection_all, 1, 1)
    side_inv = inverse_rms(side_out)
    block_out = (after_feed + side_out * side_inv * gains[5]) * live

    upstream = cotangent.astype(F32) * live
    grad_side, gain_five = rms_back(side_out, side_inv, gains[5], upstream)
    grad_side_low = grad_side.astype(BF16)
    grad_side_raw = (
        dot(grad_side_low, projection_all) * side_input * gelu_slope(side_raw)
    ).astype(BF16)
    grad_after = upstream + dot(grad_side_raw, side_gate_all, 1, 1)
    grad_reduced, gain_four = rms_back(reduced_raw, reduced_inv, gains[4], grad_after)
    grad_reduced_low = grad_reduced.astype(BF16)

    grad_reduced_all = team_gather(grad_reduced_low)
    grad_product = dot(grad_reduced_all, down_rows, 1, 1)
    grad_gate_low = (grad_product * up_raw * gelu_slope(gate_raw)).astype(BF16)
    grad_up_low = (grad_product * gelu(gate_raw)).astype(BF16)
    grad_down = copies_scatter(dot(act_low, grad_reduced_all, 0, 0).astype(BF16))
    part_low = (dot(grad_gate_low, gate_cols, 1, 1) + dot(grad_up_low, up_cols, 1, 1)).astype(BF16)
    mine_gate = copies_scatter(dot(expand_all, grad_gate_low, 0, 0).astype(BF16)).astype(BF16)
    mine_up = copies_scatter(dot(expand_all, grad_up_low, 0, 0).astype(BF16)).astype(BF16)
    part = from_depth_order(team_scatter(part_low))
    grad_merged, gain_three = rms_back(merged, merged_inv, gains[3], part)
    grad_sum = (grad_after + grad_merged) * HALF_ROOT
    grad_right, gain_two = rms_back(right_raw, right_inv, gains[2], grad_sum)
    grad_right_low = grad_right.astype(BF16)
    grad_left_low = dot(grad_right_low, right_all).astype(BF16)
    grad_attention, gain_one = rms_back(attention_raw, attention_inv, gains[1], grad_sum)
    grad_attention_low = grad_attention.astype(BF16)
    grad_mixed = (
        dot(grad_attention_low, output_all, 1, 1)
        .astype(BF16)
        .reshape(rows, KEY_VALUE_HEADS, groups, HEAD_SIZE)
    )
    grad_probs = jnp.einsum("qkgd,tkd->kgqt", grad_mixed, window[1], preferred_element_type=F32)
    inner = jnp.sum(probs * grad_probs, axis=-1, keepdims=True)
    grad_scores = (probs * (grad_probs - inner)).astype(BF16)
    grad_query_rot = jnp.einsum(
        "kgqt,tkd->qkgd", grad_scores, window[0], preferred_element_type=F32
    ).reshape(rows, QUERY_HEADS, HEAD_SIZE)
    grad_window = jnp.stack(
        [
            jnp.einsum("kgqt,qkgd->tkd", grad_scores, grouped, preferred_element_type=F32),
            jnp.einsum("kgqt,qkgd->tkd", probs_low, grad_mixed, preferred_element_type=F32),
        ]
    )
    carried = grad_window[:, hops * rows :]
    for hop in range(1, hops + 1):
        begin = (hops - hop) * rows
        carried = carried + shift(
            grad_window[:, begin : begin + rows].astype(BF16), -hop
        ).astype(F32)
    grad_query, head_zero = rms_back(
        query_raw, query_inv, head_gain[0], rotate(grad_query_rot, cosine, -sine)
    )
    grad_key, head_one = rms_back(
        key_raw, key_inv, head_gain[1], rotate(carried[0], cosine, -sine)
    )
    grad_value, _ = rms_back(value_raw, value_inv, 1.0, carried[1])
    grad_raw = jnp.concatenate(
        [
            grad_query.reshape(rows, head_width).astype(BF16),
            grad_key.reshape(rows, kv_width).astype(BF16),
            grad_value.reshape(rows, kv_width).astype(BF16),
        ],
        axis=1,
    )
    grad_normed = grad_sum + dot(grad_raw, first, 1, 1) + dot(grad_left_low, left_all, 1, 1)
    grad_input, gain_zero = rms_back(hidden, hidden_inv, gains[0], grad_normed)
    grad_hidden = grad_sum + grad_input

    gain_grads = jnp.stack(
        [
            jnp.sum(g, axis=0)
            for g in (gain_zero, gain_one, gain_two, gain_three, gain_four, gain_five)
        ]
    )
    head_grads = jnp.stack([jnp.sum(head_zero, axis=(0, 1)), jnp.sum(head_one, axis=(0, 1))])

    head_column = jnp.pad(
        head_grads.T.reshape(-1, head_part, 2), ((0, 0), (0, depth - head_part), (0, 0))
    ).reshape(-1, 2)
    small = jnp.concatenate(
        [
            dot(normed_low, grad_left_low, 0, 0),
            dot(grad_right_low, left_low, 0, 0),
            gain_grads.T,
            head_column,
            jnp.zeros((width, full_width - edges[-1]), F32),
        ],
        axis=1,
    )
    summed = full_scatter(
        jnp.concatenate(
            [
                dot(normed_low, grad_raw, 0, 0).astype(BF16),
                dot(mixed, grad_attention_low, 0, 0).astype(BF16),
                dot(after_low, grad_side_raw, 0, 0).astype(BF16),
                dot(grad_side_low, side_low, 0, 0).astype(BF16),
                small.astype(BF16),
            ],
            axis=1,
        )
    )
    (
        d_query,
        d_key,
        d_value,
        d_output,
        d_side_gate,
        d_projection,
        d_left,
        d_right,
        d_gains,
        d_heads,
    ) = (summed[:, edges[i] : edges[i + 1]] for i in range(10))
    d_right, d_projection, d_gains = d_right.T, d_projection.T, d_gains.T
    d_heads = d_heads[:head_part].T
    back = team_swap(
        jnp.concatenate(
            [mine_gate.reshape(8, depth, -1), mine_up.reshape(8, depth, -1)], axis=1
        )
    )
    grad_gate = from_column_blocks(back[:, :depth]).astype(F32)
    grad_up = from_column_blocks(back[:, depth:]).astype(F32)
    return (
        block_out,
        grad_hidden,
        d_query,
        d_key,
        d_value,
        d_output,
        d_left,
        d_right,
        d_side_gate,
        d_projection,
        grad_gate,
        grad_up,
        grad_down,
        d_gains,
        d_heads,
    )


def solution(mesh):
    dp, seq = mesh.shape["dp"], mesh.shape["seq"]
    grid = Mesh(mesh.devices.reshape(dp // 4, 4, seq // 2, 2), AXES)
    row, column = P(AXES, None), P(None, AXES)
    return jax.shard_map(
        layer,
        mesh=grid,
        in_specs=(row, row, P(("y", "xc")))
        + (row,) * 6
        + (column, row, column)
        + (row,) * 3
        + (column,) * 2,
        out_specs=(row,) * 7 + (column, row, column) + (row,) * 3 + (column,) * 2,
        check_vma=False,
    )
```

time: 1720 us -> 1190 us (0.69)
  waiting for transfers between devices: 1130 us -> 166 us
  Pallas kernels: 0 us -> 518 us
  blocking collectives: 163 us -> 0 us
  local copies, waits for them, and re-layouts: 81.3 us -> 189 us
    reduce_scatter x8 -> x0, waiting for transfers between devices: 650 us -> none  [the longest x2 325 us: group_scatter(): return lax.psum_scatter(partial, 'g', scatter_dimension=0, tiled=True)]
    pallas_call x0 -> x8, Pallas kernels: none -> 518 us  [the longest x1 129 us: full_scatter(): remote_call(full_scatter_kernel, jax.ShapeDtypeStruct((rows, width), F32)...]
    all_gather x7 -> x0, waiting for transfers between devices: 299 us -> none  [the longest x2 125 us: group_gather(): return lax.all_gather(block, 'g', axis=0, tiled=True)]
    unnamed x23 -> x0, waiting for transfers between devices: 156 us -> none
    ppermute x4 -> x22, waiting for transfers between devices: 25.8 us -> 166 us  [the longest x18 150 us: pull(): lax.ppermute(block, axis, [(i, (i - distance) % size) for i in range(size)])]
    all_gather x1 -> x0, blocking collectives: 85.9 us -> none  [gather_weights(): lax.all_gather(head_gains, both, axis=1, tiled=True)]
    all_to_all x1 -> x0, blocking collectives: 59.6 us -> none  [column_chunks(): lax.all_to_all(split.reshape(ranks, depth, planes * part), 'g', 0, 0)]
    concatenate x1 -> x2, local copies, waits for them, and re-layouts: 1.8 us -> 37.5 us  [the longest x1 36.2 us: layer(): jnp.concatenate([dot(normed_low, grad_raw, 0, 0).astype(BF16), dot(mixed,...]
  transfers between devices with their start and end apart: 26 -> 22, of which waited for: 21 -> 7; matrix products, arithmetic and copies ran while one was open for 12% -> 22% of each run, Pallas kernels for 0% -> 23%
where the time goes in v2:
time: 1190 us; the launch traced here: 1180 us
  Pallas kernels  518 us (44%)
  matrix products  210 us (18%)
  local copies, waits for them, and re-layouts  189 us (16%)
  waiting for transfers between devices  166 us (14%)
  other arithmetic  67.5 us (6%)
  starting transfers between devices  29.5 us (2%)
    dot_general x27, matrix products, dot(): lax.dot_general(left, right, (((left_dim,), (right_dim,)), ((), ())), pre...  198 us
    ppermute x18, waiting for transfers between devices, pull(): lax.ppermute(block, axis, [(i, (i - distance) % size) for i in range(size)])  150 us
    pallas_call x1, Pallas kernels, full_scatter(): remote_call(full_scatter_kernel, jax.ShapeDtypeStruct((rows, width), F32)...  129 us
    pallas_call x1, Pallas kernels, full_gather(): remote_call(full_gather_kernel, jax.ShapeDtypeStruct((32, rows, width), b...  124 us
    pallas_call x2, Pallas kernels, team_gather(): remote_call(team_gather_kernel, jax.ShapeDtypeStruct((8, rows, width), bl...  114 us
    pallas_call x2, Pallas kernels, team_scatter(): remote_call(team_scatter_kernel, jax.ShapeDtypeStruct((rows, width), F32)...  80.5 us
    pallas_call x2, Pallas kernels, team_swap(): remote_call(team_swap_kernel, jax.ShapeDtypeStruct(blocks.shape, blocks.d...  70.2 us
    concatenate x1, local copies, waits for them, and re-layouts, layer(): jnp.concatenate([dot(normed_low, grad_raw, 0, 0).astype(BF16), dot(mixed,...  36.2 us
  transfers between devices with their start and end apart: 22, of which 7 were waited for; matrix products, arithmetic and copies ran while one was open for 22% of the time, Pallas kernels for 23%

profile of v2, /device:TPU:1, one launch (start us, length us, event | category | flops | bytes accessed | tf_op | source)
XLA Modules:
  0.0 1183.7 jit_solution(3994855886127457240)
XLA Ops:
  5.2 124.2 %shard_map.280 = bf16[32,64,5888]{2,1,0:T(8,128)(2,1)} custom-call(bf16[64,5888]{1,0:T(8,128)(2,1)} %pad.14.x_ref), custom_call_target="tpu_custom_call" | custom-call | tf_op jit(solution)/shard_map/pallas_call | solution.py:379
  133.9 6.6 fusion.3
  150.4 3.9 collective-permute-start
  154.3 4.8 collective-permute-start.1
  170.4 28.5 %shard_map.282 = bf16[8,128,1024]{2,1,0:T(8,128)(2,1)} custom-call(bf16[8,128,1024]{2,1,0:T(8,128)(2,1)} %pad_maximum_fusion.1.x_ref), custom_call_target="tpu_custom_call" | custom-call | tf_op jit(solution)/shard_map/pallas_call | solution.py:271
  198.9 3.3 fusion.106
  202.2 3.4 collective-permute-start.2
  226.5 3.0 broadcast.382.clone.1
  252.8 3.1 fusion.112
  258.7 6.2 multiply_reduce_fusion.16
  267.2 28.8 %collective-permute-done.2 = bf16[512,1024]{1,0:T(8,128)(2,1)} collective-permute-done((bf16[512,1024]{1,0:T(8,128)(2,1)}, bf16[512,1024]{1,0:T(8,128)(2,1)}, u32[]{:S(2)}, u32[]{:S(2)}) %collective-permute-start.2) | collective-permute-done | bytes 1048608 | tf_op jit(solution)/shard_map/ppermute | solution.py:503
  304.2 73.9 %shard_map.281 = bf16[8,256,2048]{2,1,0:T(8,128)(2,1)} custom-call(bf16[256,2048]{1,0:T(8,128)(2,1)} %reshape.453.x_ref), custom_call_target="tpu_custom_call" | custom-call | tf_op jit(solution)/shard_map/pallas_call | solution.py:176
  395.5 7.5 collective-permute-done.4
  404.0 12.8 %fusion.113 = f32[2048,1024]{1,0:T(8,128)} fusion(bf16[2048,2048]{1,0:T(8,128)(2,1)S(1)} %bitcast.227, bf16[2048,1024]{1,0:T(8,128)(2,1)} %constant_dynamic-update-slice_fusion.8), kind=kOutput, calls=%fused_computation.257 | convolution fusion | flops 8589934592 | bytes 20971520 | tf_op jit(solution)/shard_map/dot_general | solution.py:23
  416.8 8.6 collective-permute-done.7
  426.5 16.2 %multiply_convert_fusion.1 = (bf16[2048,1024]{1,0:T(8,128)(2,1)S(1)}, f32[2048,1024]{1,0:T(8,128)}) fusion(f32[2048,1024]{1,0:T(8,128)} %fusion.113, bf16[2048,2048]{1,0:T(8,128)(2,1)S(1)} %bitcast.228, bf16[2048,1024]{1,0:T(8,128)(2,1)} %constant_dynamic-update-slice_fusion.4), kind=kOutput, calls=%fused_computation.18 | convolution fusion | flops 8610906112 | bytes 33554432 | tf_op jit(solution)/shard_map/dot_general | solution.py:23
  442.7 5.2 collective-permute-done.10
  449.0 10.8 convolution_convert_fusion.2
  459.8 40.8 %shard_map.283 = f32[256,2048]{1,0:T(8,128)S(1)} custom-call(bf16[8,256,2048]{2,1,0:T(8,128)(2,1)S(1)} %bitcast.205), custom_call_target="tpu_custom_call" | custom-call | tf_op jit(solution)/shard_map/pallas_call | solution.py:232
  517.3 39.9 %shard_map.284 = bf16[8,256,2048]{2,1,0:T(8,128)(2,1)} custom-call(bf16[256,2048]{1,0:T(8,128)(2,1)} %multiply_convert_fusion.5.x_ref), custom_call_target="tpu_custom_call" | custom-call | tf_op jit(solution)/shard_map/pallas_call | solution.py:176
  557.2 14.0 %convolution_convert_fusion.3 = bf16[1024,2048]{1,0:T(8,128)(2,1)} fusion(bf16[2048,1024]{1,0:T(8,128)(2,1)} %copy-done.141, bf16[2048,2048]{1,0:T(8,128)(2,1)} %bitcast.232), kind=kOutput, calls=%fused_computation.34 | convolution fusion | flops 8592031744 | bytes 16777216 | tf_op jit(solution)/shard_map/dot_general | solution.py:23
  571.2 23.8 %fusion.12 = (bf16[2048,1024]{1,0:T(8,128)(2,1)S(1)}, bf16[2048,1024]{1,0:T(8,128)(2,1)}) fusion(f32[2048,1024]{1,0:T(8,128)} %fusion.113, f32[2048,1024]{1,0:T(8,128)} %get-tuple-element.221, bf16[2048,2048]{1,0:T(8,128)(2,1)} %bitcast.233, bf16[1024,2048]{1,0:T(8,128)(2,1)} %constant_dynamic-update-slice_fusion), kind=kOutput, calls=%fused_computation.16 | convolution fusion | flops 8638169088 | bytes 37748736 | tf_op jit(solution)/shard_map/dot_general | solution.py:23
  595.0 15.6 %convolution_convert_fusion.4 = bf16[2048,1024]{1,0:T(8,128)(2,1)} fusion(bf16[2048,2048]{1,0:T(8,128)(2,1)} %bitcast.226, bf16[2048,1024]{1,0:T(8,128)(2,1)} %get-tuple-element.153), kind=kOutput, calls=%fused_computation.35 | convolution fusion | flops 8592031744 | bytes 16777216 | tf_op jit(solution)/shard_map/dot_general | solution.py:23
  610.6 14.3 %fusion.114 = f32[2048,2048]{1,0:T(8,128)} fusion(bf16[2048,1024]{1,0:T(8,128)(2,1)S(1)} %copy-done.143, bf16[2048,1024]{1,0:T(8,128)(2,1)} %constant_dynamic-update-slice_fusion.4), kind=kOutput, calls=%fused_computation.258 | convolution fusion | flops 8589934592 | bytes 25165824 | tf_op jit(solution)/shard_map/dot_general | solution.py:23
  624.9 10.7 convolution_convert_fusion.5
  635.6 14.6 %add_convert_fusion = bf16[2048,2048]{1,0:T(8,128)(2,1)S(1)} fusion(f32[2048,2048]{1,0:T(8,128)} %fusion.114, bf16[2048,1024]{1,0:T(8,128)(2,1)} %copy-done.142, bf16[2048,1024]{1,0:T(8,128)(2,1)} %constant_dynamic-update-slice_fusion.8), kind=kOutput, calls=%fused_computation.1 | convolution fusion | flops 8598323200 | bytes 33554432 | tf_op jit(solution)/shard_map/dot_general | solution.py:23
  650.2 39.7 %shard_map.285 = f32[256,2048]{1,0:T(8,128)S(1)} custom-call(bf16[8,256,2048]{2,1,0:T(8,128)(2,1)S(1)} %bitcast.204), custom_call_target="tpu_custom_call" | custom-call | tf_op jit(solution)/shard_map/pallas_call | solution.py:232
  696.3 4.1 reshape.465
  703.4 4.2 multiply_reduce_fusion.4
  709.8 6.9 fusion.30
  719.4 4.5 fusion.17
  767.1 5.6 convolution_convert_fusion.1
  773.3 16.4 %collective-permute-done.12 = bf16[2,256,2,256]{3,1,2,0:T(8,128)(2,1)} collective-permute-done((bf16[2,256,2,256]{3,1,2,0:T(8,128)(2,1)}, bf16[2,256,2,256]{3,1,2,0:T(8,128)(2,1)}, u32[]{:S(2)}, u32[]{:S(2)}) %collective-permute-start.12) | collective-permute-done | bytes 524320 | tf_op jit(solution)/shard_map/ppermute | solution.py:498
  798.9 9.5 fusion.27
  808.3 6.8 convolution_convert_fusion
  815.4 3.9 fusion.39
  822.3 36.2 %concatenate.69 = bf16[2048,5888]{1,0:T(8,128)(2,1)} concatenate(bf16[2048,3072]{1,0:T(8,128)(2,1)} %convolution_convert_fusion, bf16[2048,2048]{1,0:T(8,128)(2,1)} %convolution_convert_fusion.1, bf16[2048,256]{1,0:T(8,128)(2,1)} %convolution_convert_fusion.7, bf16[2048,256]{1,0:T(8,128)(2,1)} %convolution_convert_fusion.6, bf16[2048,64]{1,0:T(8,128)(2,1)} %copy.414, ...), dimensions={1} | concatenate | bytes 48234496 | tf_op jit(solution)/shard_map/concatenate | solution.py:790
  858.5 129.2 %shard_map.286 = f32[64,5888]{1,0:T(8,128)} custom-call(bf16[32,64,5888]{2,1,0:T(8,128)(2,1)} %bitcast.206), custom_call_target="tpu_custom_call" | custom-call | tf_op jit(solution)/shard_map/pallas_call | solution.py:476
  995.1 3.0 add_convert_fusion.3
  1008.0 79.1 %collective-permute-done.15 = bf16[512,1024]{1,0:T(8,128)(2,1)S(1)} collective-permute-done((bf16[512,1024]{1,0:T(8,128)(2,1)}, bf16[512,1024]{1,0:T(8,128)(2,1)S(1)}, u32[]{:S(2)}, u32[]{:S(2)}) %collective-permute-start.15) | collective-permute-done | bytes 1048608 | tf_op jit(solution)/shard_map/ppermute | solution.py:503
  1089.3 20.3 %collective-permute-done.18 = bf16[512,1024]{1,0:T(8,128)(2,1)S(1)} collective-permute-done((bf16[512,1024]{1,0:T(8,128)(2,1)}, bf16[512,1024]{1,0:T(8,128)(2,1)S(1)}, u32[]{:S(2)}, u32[]{:S(2)}) %collective-permute-start.18) | collective-permute-done | bytes 1048608 | tf_op jit(solution)/shard_map/ppermute | solution.py:503
  1113.2 41.7 %shard_map.287 = bf16[8,128,1024]{2,1,0:T(8,128)(2,1)} custom-call(bf16[8,128,1024]{2,1,0:T(8,128)(2,1)} %pad_maximum_fusion.3.x_ref), custom_call_target="tpu_custom_call" | custom-call | tf_op jit(solution)/shard_map/pallas_call | solution.py:271
  1155.0 3.3 slice_convert_fusion
  1158.3 4.2 reshape.476
  1162.5 4.5 copy.416
  1167.0 3.9 reshape.473
  1173.7 3.2 copy.417
  1179.6 3.7 convert_add_fusion.1
  (529 shorter events, 221.8 us)
Async XLA Ops:
  133.5 131.9 %copy-start.73 = (f32[1,2048]{1,0:T(1,128)}, f32[1,2048]{1,0:T(1,128)S(1)}, u32[]{:S(2)}) copy-start(f32[1,2048]{1,0:T(1,128)S(1)} %get-tuple-element.206) | copy-start | bytes 24580
  133.5 163.7 %copy-start.75 = (f32[1,2048]{1,0:T(1,128)}, f32[1,2048]{1,0:T(1,128)S(1)}, u32[]{:S(2)}) copy-start(f32[1,2048]{1,0:T(1,128)S(1)} %get-tuple-element.203) | copy-start | bytes 24580
  148.0 75.4 %copy-start.44 = (f32[256,128]{1,0:T(8,128)}, f32[256,128]{1,0:T(8,128)S(1)}, u32[]{:S(2)}) copy-start(f32[256,128]{1,0:T(8,128)S(1)} %get-tuple-element.211) | copy-start | bytes 393220
  150.4 97.3 %collective-permute-start = (bf16[2,256,2,256]{3,1,2,0:T(8,128)(2,1)}, bf16[2,256,2,256]{3,1,2,0:T(8,128)(2,1)}, u32[]{:S(2)}, u32[]{:S(2)}) collective-permute-start(bf16[2,256,2,256]{3,1,2,0:T(8,128)(2,1)} %pad_maximum_fusion.10), channel_id=1, source_target_pairs={{0,2},{1,3},{4,6},{5,7},{8,10},{9,11},{12,14},{13,15},{16,18},{17,... | collective-permute-start | bytes 1572872 | tf_op jit(solution)/shard_map/ppermute | solution.py:498
  154.3 93.8 %collective-permute-start.1 = (bf16[2,256,2,256]{3,1,2,0:T(8,128)(2,1)}, bf16[2,256,2,256]{3,1,2,0:T(8,128)(2,1)}, u32[]{:S(2)}, u32[]{:S(2)}) collective-permute-start(bf16[2,256,2,256]{3,1,2,0:T(8,128)(2,1)} %pad_maximum_fusion.10), channel_id=1, source_target_pairs={{0,1},{1,2},{2,3},{4,5},{5,6},{6,7},{8,9},{9,10},{10,11},{12,13},{... | collective-permute-start | bytes 1572872 | tf_op jit(solution)/shard_map/ppermute | solution.py:498
  202.2 93.8 %collective-permute-start.2 = (bf16[512,1024]{1,0:T(8,128)(2,1)}, bf16[512,1024]{1,0:T(8,128)(2,1)}, u32[]{:S(2)}, u32[]{:S(2)}) collective-permute-start(bf16[512,1024]{1,0:T(8,128)(2,1)} %bitcast.30), channel_id=1, source_target_pairs={{0,2},{2,0},{1,3},{3,1},{4,6},{6,4},{5,7},{7,5},{8,10},{10,8},{9,1... | collective-permute-start | bytes 3145736 | tf_op jit(solution)/shard_map/ppermute | solution.py:503
  205.6 178.4 %collective-permute-start.3 = (bf16[512,1024]{1,0:T(8,128)(2,1)}, bf16[512,1024]{1,0:T(8,128)(2,1)}, u32[]{:S(2)}, u32[]{:S(2)}) collective-permute-start(bf16[512,1024]{1,0:T(8,128)(2,1)} %bitcast.30), channel_id=1, source_target_pairs={{0,16},{16,0},{1,17},{17,1},{2,18},{18,2},{3,19},{19,3},{4,20},{20... | collective-permute-start | bytes 3145736 | tf_op jit(solution)/shard_map/ppermute | solution.py:503
  206.8 171.3 %collective-permute-start.5 = (bf16[512,1024]{1,0:T(8,128)(2,1)}, bf16[512,1024]{1,0:T(8,128)(2,1)}, u32[]{:S(2)}, u32[]{:S(2)}) collective-permute-start(bf16[512,1024]{1,0:T(8,128)(2,1)} %bitcast.31), channel_id=1, source_target_pairs={{0,2},{2,0},{1,3},{3,1},{4,6},{6,4},{5,7},{7,5},{8,10},{10,8},{9,1... | collective-permute-start | bytes 3145736 | tf_op jit(solution)/shard_map/ppermute | solution.py:503
  239.4 12.3 %copy-start.46 = (bf16[256,8,128]{2,0,1:T(8,128)(2,1)}, bf16[256,8,128]{2,0,1:T(8,128)(2,1)S(1)}, u32[]{:S(2)}) copy-start(bf16[256,8,128]{2,0,1:T(8,128)(2,1)S(1)} %copy.380) | copy-start | bytes 1572868
  239.5 12.2 %copy-start.48 = (bf16[256,8,128]{2,0,1:T(8,128)(2,1)}, bf16[256,8,128]{2,0,1:T(8,128)(2,1)S(1)}, u32[]{:S(2)}) copy-start(bf16[256,8,128]{2,0,1:T(8,128)(2,1)S(1)} %copy.381) | copy-start | bytes 1572868
  247.7 17.2 %copy-start.127 = (f32[256]{0:T(256)}, f32[256]{0:T(256)S(1)}, u32[]{:S(2)}) copy-start(f32[256]{0:T(256)S(1)} %get-tuple-element.214) | copy-start | bytes 3076
  247.7 17.7 %copy-start.5 = (f32[256,2048]{1,0:T(8,128)}, f32[256,2048]{1,0:T(8,128)S(1)}, u32[]{:S(2)}) copy-start(f32[256,2048]{1,0:T(8,128)S(1)} %get-tuple-element.215) | copy-start | bytes 6291460
  247.7 140.1 %collective-permute-start.6 = (bf16[512,1024]{1,0:T(8,128)(2,1)}, bf16[512,1024]{1,0:T(8,128)(2,1)}, u32[]{:S(2)}, u32[]{:S(2)}) collective-permute-start(bf16[512,1024]{1,0:T(8,128)(2,1)} %bitcast.31), channel_id=1, source_target_pairs={{0,16},{16,0},{1,17},{17,1},{2,18},{18,2},{3,19},{19,3},{4,20},{20... | collective-permute-start | bytes 3145736 | tf_op jit(solution)/shard_map/ppermute | solution.py:503
  248.0 136.2 %collective-permute-start.8 = (bf16[256,2048]{1,0:T(8,128)(2,1)}, bf16[256,2048]{1,0:T(8,128)(2,1)}, u32[]{:S(2)}, u32[]{:S(2)}) collective-permute-start(bf16[256,2048]{1,0:T(8,128)(2,1)} %param.31), channel_id=1, source_target_pairs={{0,2},{2,0},{1,3},{3,1},{4,6},{6,4},{5,7},{7,5},{8,10},{10,8},{9,1... | collective-permute-start | bytes 3145736 | tf_op jit(solution)/shard_map/ppermute | solution.py:503
  266.6 111.5 %copy-start.131 = (f32[256]{0:T(256)}, f32[256]{0:T(256)S(1)}, u32[]{:S(2)}) copy-start(f32[256]{0:T(256)S(1)} %get-tuple-element.150) | copy-start | bytes 3076
  266.6 234.3 %copy-start.1 = (f32[256,2048]{1,0:T(8,128)}, f32[256,2048]{1,0:T(8,128)S(1)}, u32[]{:S(2)}) copy-start(f32[256,2048]{1,0:T(8,128)S(1)} %get-tuple-element.151) | copy-start | bytes 6291460
  267.2 30.0 %copy-start.114 = (f32[256]{0:T(256)}, f32[256]{0:T(256)S(1)}, u32[]{:S(2)}) copy-start(f32[256]{0:T(256)S(1)} %get-tuple-element.213) | copy-start | bytes 3076
  296.0 97.2 %collective-permute-start.9 = (bf16[256,2048]{1,0:T(8,128)(2,1)}, bf16[256,2048]{1,0:T(8,128)(2,1)}, u32[]{:S(2)}, u32[]{:S(2)}) collective-permute-start(bf16[256,2048]{1,0:T(8,128)(2,1)} %param.31), channel_id=1, source_target_pairs={{0,16},{16,0},{1,17},{17,1},{2,18},{18,2},{3,19},{19,3},{4,20},{20... | collective-permute-start | bytes 3145736 | tf_op jit(solution)/shard_map/ppermute | solution.py:503
  378.1 24.9 %collective-permute-start.4 = (bf16[512,1024]{1,0:T(8,128)(2,1)}, bf16[512,1024]{1,0:T(8,128)(2,1)S(1)}, u32[]{:S(2)}, u32[]{:S(2)}) collective-permute-start(bf16[512,1024]{1,0:T(8,128)(2,1)} %collective-permute-done.2), channel_id=1, source_target_pairs={{0,16},{16,0},{1,17},{17,1},{2,18},{18,2},{3,19},{19,3},{4,20},{20... | collective-permute-start | bytes 3145736 | tf_op jit(solution)/shard_map/ppermute | solution.py:503
  384.0 41.4 %collective-permute-start.7 = (bf16[512,1024]{1,0:T(8,128)(2,1)}, bf16[512,1024]{1,0:T(8,128)(2,1)S(1)}, u32[]{:S(2)}, u32[]{:S(2)}) collective-permute-start(bf16[512,1024]{1,0:T(8,128)(2,1)} %collective-permute-done.5), channel_id=1, source_target_pairs={{0,16},{16,0},{1,17},{17,1},{2,18},{18,2},{3,19},{19,3},{4,20},{20... | collective-permute-start | bytes 3145736 | tf_op jit(solution)/shard_map/ppermute | solution.py:503
  384.2 63.7 %collective-permute-start.10 = (bf16[256,2048]{1,0:T(8,128)(2,1)}, bf16[256,2048]{1,0:T(8,128)(2,1)S(1)}, u32[]{:S(2)}, u32[]{:S(2)}) collective-permute-start(bf16[256,2048]{1,0:T(8,128)(2,1)} %collective-permute-done.8), channel_id=1, source_target_pairs={{0,16},{16,0},{1,17},{17,1},{2,18},{18,2},{3,19},{19,3},{4,20},{20... | collective-permute-start | bytes 3145736 | tf_op jit(solution)/shard_map/ppermute | solution.py:503
  387.8 16.2 %copy-start.23 = (bf16[8,256,2048]{2,1,0:T(8,128)(2,1)S(1)}, bf16[8,256,2048]{2,1,0:T(8,128)(2,1)}, u32[]{:S(2)}) copy-start(bf16[8,256,2048]{2,1,0:T(8,128)(2,1)} %shard_map.281) | copy-start | bytes 25165828
  442.7 17.1 %copy-start.141 = (bf16[2048,1024]{1,0:T(8,128)(2,1)}, bf16[2048,1024]{1,0:T(8,128)(2,1)S(1)}, u32[]{:S(2)}) copy-start(bf16[2048,1024]{1,0:T(8,128)(2,1)S(1)} %get-tuple-element.220) | copy-start | bytes 12582916
  595.0 29.9 %copy-start.142 = (bf16[2048,1024]{1,0:T(8,128)(2,1)}, bf16[2048,1024]{1,0:T(8,128)(2,1)S(1)}, u32[]{:S(2)}) copy-start(bf16[2048,1024]{1,0:T(8,128)(2,1)S(1)} %get-tuple-element.152) | copy-start | bytes 12582916
  595.0 15.6 %copy-start.143 = (bf16[2048,1024]{1,0:T(8,128)(2,1)S(1)}, bf16[2048,1024]{1,0:T(8,128)(2,1)}, u32[]{:S(2)}) copy-start(bf16[2048,1024]{1,0:T(8,128)(2,1)} %get-tuple-element.153) | copy-start | bytes 12582916
  595.0 29.9 %slice-start.2 = ((s8[8388608]{0:T(1024)(128)(4,1)}), s8[4194304]{0:T(1024)(128)(4,1)S(1)}, s32[]{:S(2)}) async-start(s8[8388608]{0:T(1024)(128)(4,1)} %bitcast.229), calls=%async_computation.2 | async-start | bytes 8388608
  610.6 14.3 %slice-start.3 = ((s8[8388608]{0:T(1024)(128)(4,1)}), s8[4194304]{0:T(1024)(128)(4,1)S(1)}, s32[]{:S(2)}) async-start(s8[8388608]{0:T(1024)(128)(4,1)} %bitcast.229), calls=%async_computation.3 | async-start | bytes 8388608
  693.9 8.9 copy-start.132
  709.8 14.1 %slice-start = ((s8[6291456]{0:T(1024)(128)(4,1)}), s8[2097152]{0:T(1024)(128)(4,1)S(1)}, s32[]{:S(2)}) async-start(s8[6291456]{0:T(1024)(128)(4,1)} %bitcast.223), calls=%async_computation | async-start | bytes 4194304
  736.2 18.0 %copy-start.78 = (bf16[256,64]{0,1:T(8,128)(2,1)}, bf16[256,64]{0,1:T(8,128)(2,1)S(1)}, u32[]{:S(2)}) copy-start(bf16[256,64]{0,1:T(8,128)(2,1)S(1)} %convolution_convert_fusion.10) | copy-start | bytes 98308
  738.7 265.4 %collective-permute-start.20 = (bf16[256,2048]{1,0:T(8,128)(2,1)}, bf16[256,2048]{1,0:T(8,128)(2,1)}, u32[]{:S(2)}, u32[]{:S(2)}) collective-permute-start(bf16[256,2048]{1,0:T(8,128)(2,1)} %get-tuple-element.157), channel_id=1, source_target_pairs={{0,16},{16,0},{1,17},{17,1},{2,18},{18,2},{3,19},{19,3},{4,20},{20... | collective-permute-start | bytes 3145736 | tf_op jit(solution)/shard_map/ppermute | solution.py:503
  741.7 250.5 %collective-permute-start.14 = (bf16[512,1024]{1,0:T(8,128)(2,1)}, bf16[512,1024]{1,0:T(8,128)(2,1)}, u32[]{:S(2)}, u32[]{:S(2)}) collective-permute-start(bf16[512,1024]{1,0:T(8,128)(2,1)} %get-tuple-element.159), channel_id=1, source_target_pairs={{0,16},{16,0},{1,17},{17,1},{2,18},{18,2},{3,19},{19,3},{4,20},{20... | collective-permute-start | bytes 3145736 | tf_op jit(solution)/shard_map/ppermute | solution.py:503
  742.2 265.7 %collective-permute-start.13 = (bf16[512,1024]{1,0:T(8,128)(2,1)}, bf16[512,1024]{1,0:T(8,128)(2,1)}, u32[]{:S(2)}, u32[]{:S(2)}) collective-permute-start(bf16[512,1024]{1,0:T(8,128)(2,1)} %get-tuple-element.158), channel_id=1, source_target_pairs={{0,16},{16,0},{1,17},{17,1},{2,18},{18,2},{3,19},{19,3},{4,20},{20... | collective-permute-start | bytes 3145736 | tf_op jit(solution)/shard_map/ppermute | solution.py:503
  751.2 21.6 %collective-permute-start.11 = (bf16[2,256,2,256]{3,1,2,0:T(8,128)(2,1)}, bf16[2,256,2,256]{3,1,2,0:T(8,128)(2,1)}, u32[]{:S(2)}, u32[]{:S(2)}) collective-permute-start(bf16[2,256,2,256]{3,1,2,0:T(8,128)(2,1)} %get-tuple-element.183), channel_id=1, source_target_pairs={{1,0},{2,1},{3,2},{5,4},{6,5},{7,6},{9,8},{10,9},{11,10},{13,12},{... | collective-permute-start | bytes 1572872 | tf_op jit(solution)/shard_map/ppermute | solution.py:498
  752.8 37.0 %collective-permute-start.12 = (bf16[2,256,2,256]{3,1,2,0:T(8,128)(2,1)}, bf16[2,256,2,256]{3,1,2,0:T(8,128)(2,1)}, u32[]{:S(2)}, u32[]{:S(2)}) collective-permute-start(bf16[2,256,2,256]{3,1,2,0:T(8,128)(2,1)} %get-tuple-element.184), channel_id=1, source_target_pairs={{2,0},{3,1},{6,4},{7,5},{10,8},{11,9},{14,12},{15,13},{18,16},{19,... | collective-permute-start | bytes 1572872 | tf_op jit(solution)/shard_map/ppermute | solution.py:498
  758.0 9.1 copy-start.43
  758.0 9.1 copy-start.56
  767.1 23.5 %copy-start.30 = (f32[1,768,2,256]{3,1,2,0:T(8,128)S(1)}, f32[1,768,2,256]{3,1,2,0:T(8,128)}, u32[]{:S(2)}) copy-start(f32[1,768,2,256]{3,1,2,0:T(8,128)} %fusion.50) | copy-start | bytes 4718596
  767.1 23.5 %copy-start.32 = (f32[1,768,2,256]{3,1,2,0:T(8,128)S(1)}, f32[1,768,2,256]{3,1,2,0:T(8,128)}, u32[]{:S(2)}) copy-start(f32[1,768,2,256]{3,1,2,0:T(8,128)} %convolution_bitcast_fusion) | copy-start | bytes 4718596
  772.8 222.3 %collective-permute-start.17 = (bf16[512,1024]{1,0:T(8,128)(2,1)}, bf16[512,1024]{1,0:T(8,128)(2,1)}, u32[]{:S(2)}, u32[]{:S(2)}) collective-permute-start(bf16[512,1024]{1,0:T(8,128)(2,1)} %get-tuple-element.161), channel_id=1, source_target_pairs={{0,16},{16,0},{1,17},{17,1},{2,18},{18,2},{3,19},{19,3},{4,20},{20... | collective-permute-start | bytes 3145736 | tf_op jit(solution)/shard_map/ppermute | solution.py:503
  789.7 299.5 %collective-permute-start.16 = (bf16[512,1024]{1,0:T(8,128)(2,1)}, bf16[512,1024]{1,0:T(8,128)(2,1)}, u32[]{:S(2)}, u32[]{:S(2)}) collective-permute-start(bf16[512,1024]{1,0:T(8,128)(2,1)} %get-tuple-element.160), channel_id=1, source_target_pairs={{0,16},{16,0},{1,17},{17,1},{2,18},{18,2},{3,19},{19,3},{4,20},{20... | collective-permute-start | bytes 3145736 | tf_op jit(solution)/shard_map/ppermute | solution.py:503
  858.5 129.3 %copy-start.130 = (f32[256]{0:T(256)S(1)}, f32[256]{0:T(256)}, u32[]{:S(2)}) copy-start(f32[256]{0:T(256)} %copy-done.129) | copy-start | bytes 3076
  858.5 129.3 %copy-start.22 = (f32[256,2048]{1,0:T(8,128)S(1)}, f32[256,2048]{1,0:T(8,128)}, u32[]{:S(2)}) copy-start(f32[256,2048]{1,0:T(8,128)} %get-tuple-element.227) | copy-start | bytes 6291460
  995.0 9.0 copy-start.65
  995.1 92.0 %collective-permute-start.15 = (bf16[512,1024]{1,0:T(8,128)(2,1)}, bf16[512,1024]{1,0:T(8,128)(2,1)S(1)}, u32[]{:S(2)}, u32[]{:S(2)}) collective-permute-start(bf16[512,1024]{1,0:T(8,128)(2,1)} %add_convert_fusion.5), channel_id=1, source_target_pairs={{0,2},{2,0},{1,3},{3,1},{4,6},{6,4},{5,7},{7,5},{8,10},{10,8},{9,1... | collective-permute-start | bytes 3145736 | tf_op jit(solution)/shard_map/ppermute | solution.py:503
  998.1 111.5 %collective-permute-start.18 = (bf16[512,1024]{1,0:T(8,128)(2,1)}, bf16[512,1024]{1,0:T(8,128)(2,1)S(1)}, u32[]{:S(2)}, u32[]{:S(2)}) collective-permute-start(bf16[512,1024]{1,0:T(8,128)(2,1)} %add_convert_fusion.3), channel_id=1, source_target_pairs={{0,2},{2,0},{1,3},{3,1},{4,6},{6,4},{5,7},{7,5},{8,10},{10,8},{9,1... | collective-permute-start | bytes 3145736 | tf_op jit(solution)/shard_map/ppermute | solution.py:503
  1004.1 175.5 %collective-permute-start.19 = (bf16[256,2048]{1,0:T(8,128)(2,1)S(1)}, bf16[256,2048]{1,0:T(8,128)(2,1)}, u32[]{:S(2)}, u32[]{:S(2)}) collective-permute-start(bf16[256,2048]{1,0:T(8,128)(2,1)S(1)} %copy-done.65), channel_id=1, source_target_pairs={{0,16},{16,0},{1,17},{17,1},{2,18},{18,2},{3,19},{19,3},{4,20},{20... | collective-permute-start | bytes 3145736 | tf_op jit(solution)/shard_map/ppermute | solution.py:503
  1007.9 171.7 %collective-permute-start.21 = (bf16[256,2048]{1,0:T(8,128)(2,1)}, bf16[256,2048]{1,0:T(8,128)(2,1)}, u32[]{:S(2)}, u32[]{:S(2)}) collective-permute-start(bf16[256,2048]{1,0:T(8,128)(2,1)} %add_convert_fusion.1), channel_id=1, source_target_pairs={{0,2},{2,0},{1,3},{3,1},{4,6},{6,4},{5,7},{7,5},{8,10},{10,8},{9,1... | collective-permute-start | bytes 3145736 | tf_op jit(solution)/shard_map/ppermute | solution.py:503
  (122 other events, 403.3 us)

commit v3 on v2

--- a/solution.py
+++ b/solution.py
@@ -1,3 +1,5 @@
+from functools import partial
+
 import jax
 import jax.numpy as jnp
 from jax import lax
@@ -108,12 +110,15 @@
     return total
 
 
-def remote_call(kernel, out, copies, identity, scratch=(), vmem=None, out_space=pl.ANY):
+def remote_call(kernel, out, copies, identity, scratch=(), vmem=None, spaces=pl.ANY, inputs=1):
+    places = [pl.BlockSpec(memory_space=space) for space in spaces] if isinstance(
+        spaces, (list, tuple)
+    ) else pl.BlockSpec(memory_space=spaces)
     return pl.pallas_call(
         kernel,
         out_shape=out,
-        in_specs=[pl.BlockSpec(memory_space=pl.ANY)],
-        out_specs=pl.BlockSpec(memory_space=out_space),
+        in_specs=[pl.BlockSpec(memory_space=pl.ANY)] * inputs,
+        out_specs=places,
         scratch_shapes=[
             pltpu.SemaphoreType.DMA((copies,)),
             pltpu.SemaphoreType.DMA((copies,)),
@@ -247,34 +252,13 @@
     )(partial_sum.reshape(8, rows, width))
 
 
-def team_swap_kernel(x_ref, o_ref, send, recv, local):
+def team_peers():
     xc, l = lax.axis_index("xc"), lax.axis_index("l")
-    me = xc * 2 + l
-    keep = pltpu.make_async_copy(x_ref.at[me], o_ref.at[me], local)
-    keep.start()
-    places = []
+    peers = []
     for i in range(1, 8):
         far, side = lax.rem(xc + i // 2, 4), lax.rem(l + i % 2, 2)
-        back = lax.rem(xc + 4 - i // 2, 4)
-        places.append((far * 2 + side, {"xc": far, "l": side}, back * 2 + side))
-    greet([peer for _, peer, _ in places])
-    out = Sender(send, recv)
-    for rank, peer, _ in places:
-        out.go(x_ref.at[rank], o_ref.at[me], peer)
-    for copy in out.started:
-        copy.wait_recv()
-    out.finish()
-    keep.wait()
-
-
-def team_swap(blocks):
-    return remote_call(
-        team_swap_kernel,
-        jax.ShapeDtypeStruct(blocks.shape, blocks.dtype),
-        7,
-        2,
-        [pltpu.SemaphoreType.DMA],
-    )(blocks)
+        peers.append((far * 2 + side, {"xc": far, "l": side}))
+    return xc * 2 + l, peers
 
 
 def full_places():
@@ -303,238 +287,340 @@
 DEPTHS = ("O", "L", "H", "HL")
 
 
-def full_gather_kernel(x_ref, o_ref, send, recv, local):
+def copy_places():
+    y, h = lax.axis_index("y"), lax.axis_index("h")
+    return {
+        "O": y * 2 + h,
+        "Y": (1 - y) * 2 + h,
+        "H": y * 2 + 1 - h,
+        "D": (1 - y) * 2 + 1 - h,
+    }
+
+
+def weights_in_kernel(
+    x_ref, gate_ref, up_ref, down_ref, o_ref, gates_ref, ups_ref, downs_ref, send, recv, local
+):
     rank, peers = full_places()
-    half = x_ref.shape[0] // 2
-    top, low = pl.ds(0, half), pl.ds(half, half)
+    me, team = team_peers()
+    spot = copy_places()
 
     def at(plane, depth):
         return o_ref.at[rank(plane, depth)]
 
-    keep = pltpu.make_async_copy(x_ref, at("O", "O"), local)
-    keep.start()
-    greet(list(peers.values()))
+    keeps = [
+        pltpu.make_async_copy(x_ref, at("O", "O"), local.at[0]),
+        pltpu.make_async_copy(down_ref, downs_ref.at[spot["O"]], local.at[1]),
+        pltpu.make_async_copy(gate_ref.at[me], gates_ref.at[spot["O"], me], local.at[2]),
+        pltpu.make_async_copy(up_ref.at[me], ups_ref.at[spot["O"], me], local.at[3]),
+    ]
+    for keep in keeps:
+        keep.start()
+    greet([peer for _, peer in team] + [peers["Y"], peers["H"]])
     out = Sender(send, recv)
-    twins = []
+    swaps, twins = [], []
     to_h = out.go(x_ref, at("O", "O"), peers["H"])
     to_l = out.go(x_ref, at("O", "O"), peers["L"])
+    for place, peer in team:
+        swaps.append(out.go(gate_ref.at[place], gates_ref.at[spot["O"], me], peer))
+        swaps.append(out.go(up_ref.at[place], ups_ref.at[spot["O"], me], peer))
     direct, bent = {}, {}
 
     def begin(depth):
         source = x_ref if depth == "O" else at("O", depth)
         target = at("O", depth)
-        y_top = out.go(source.at[top], target.at[top], peers["Y"])
-        x_low = out.go(source.at[low], target.at[low], peers["X"])
-        y_low = out.go(source.at[low], target.at[low], peers["Y"])
-        x_top = out.go(source.at[top], target.at[top], peers["X"])
+        to_y = out.go(source, target, peers["Y"])
+        to_x = out.go(source, target, peers["X"])
         twins.append(out.go(source, target, peers["C"]))
-        direct[depth] = (y_top, x_low, y_low, x_top)
+        direct[depth] = (to_y, to_x)
 
     def bend(depth):
-        y_top, x_low, y_low, x_top = direct[depth]
-        y_top.wait_recv()
-        piece = at("Y", depth).at[top]
-        bent_top = out.go(piece, piece, peers["X"])
-        x_low.wait_recv()
-        piece = at("X", depth).at[low]
-        bent_low = out.go(piece, piece, peers["Y"])
-        y_low.wait_recv()
+        to_y, to_x = direct[depth]
+        to_y.wait_recv()
+        bent[depth] = out.go(at("Y", depth), at("Y", depth), peers["X"])
         twins.append(out.go(at("Y", depth), at("Y", depth), peers["C"]))
-        x_top.wait_recv()
+        to_x.wait_recv()
         twins.append(out.go(at("X", depth), at("X", depth), peers["C"]))
-        bent[depth] = (bent_top, bent_low)
 
     def close(depth):
-        for copy in bent[depth]:
-            copy.wait_recv()
+        bent[depth].wait_recv()
         twins.append(out.go(at("D", depth), at("D", depth), peers["C"]))
 
+    blocks = {"gate": gates_ref, "up": ups_ref, "down": downs_ref}
+    flats, arrivals = {}, []
+
+    def spread(name):
+        block = blocks[name]
+        source = down_ref if name == "down" else block.at[spot["O"]]
+        flats[name] = out.go(source, block.at[spot["O"]], peers["H"])
+        arrivals.append(out.go(source, block.at[spot["O"]], peers["Y"]))
+
+    def corner(name):
+        flats[name].wait_recv()
+        piece = blocks[name].at[spot["H"]]
+        arrivals.append(out.go(piece, piece, peers["Y"]))
+
+    spread("down")
     begin("O")
+    for swap in swaps:
+        swap.wait_recv()
+    keeps[2].wait()
+    keeps[3].wait()
+    spread("gate")
     to_h.wait_recv()
     to_hl = out.go(at("O", "H"), at("O", "H"), peers["L"])
     to_l.wait_recv()
     begin("L")
+    begin("H")
+    corner("down")
     bend("O")
-    begin("H")
-    bend("L")
+    spread("up")
     to_hl.wait_recv()
     begin("HL")
+    bend("L")
+    corner("gate")
     bend("H")
     close("O")
     close("L")
     bend("HL")
+    corner("up")
     close("H")
     close("HL")
-    for copy in twins:
+    for copy in twins + arrivals:
         copy.wait_recv()
     out.finish()
-    keep.wait()
-
-
-def full_gather(block):
-    rows, width = block.shape
+    keeps[0].wait()
+    keeps[1].wait()
+
+
+def weights_in(columns, gate_blocks, up_blocks, down):
+    rows, width = columns.shape
+    ranks, depth, part = gate_blocks.shape
     if lax.axis_size("y") != 2 or lax.axis_size("h") != 2:
-        gathered = lax.all_gather(block, AXES, axis=0, tiled=False)
+        full = lax.all_gather(columns, AXES, axis=0, tiled=False)
+        gates, ups = (
+            lax.all_gather(lax.all_to_all(b, TEAM, 0, 0), COPIES, axis=0, tiled=False)
+            for b in (gate_blocks, up_blocks)
+        )
+        downs = lax.all_gather(down, COPIES, axis=0, tiled=False)
     else:
-        gathered = remote_call(
-            full_gather_kernel,
-            jax.ShapeDtypeStruct((32, rows, width), block.dtype),
-            43,
+        full, gates, ups, downs = remote_call(
+            weights_in_kernel,
+            (
+                jax.ShapeDtypeStruct((32, rows, width), BF16),
+                jax.ShapeDtypeStruct((4, ranks, depth, part), BF16),
+                jax.ShapeDtypeStruct((4, ranks, depth, part), BF16),
+                jax.ShapeDtypeStruct((4, *down.shape), BF16),
+            ),
+            14 + 3 + 28 + 9,
             3,
-            [pltpu.SemaphoreType.DMA],
-        )(block)
-    return gathered.reshape(-1, width)
+            [pltpu.SemaphoreType.DMA((4,))],
+            spaces=[pl.ANY] * 4,
+            inputs=4,
+        )(columns, gate_blocks, up_blocks, down)
+    return (
+        full.reshape(-1, width),
+        gates.reshape(-1, part),
+        ups.reshape(-1, part),
+        downs.reshape(-1, down.shape[1]),
+    )
 
 
 PLANES = ("D", "X", "Y", "O")
 SUMS = ("HL", "L", "H", "O")
 
 
-def full_scatter_kernel(
-    p_ref, o_ref, send, recv, local, mine, twin_in, cross_in, lane_in, bent_in, depth_in
-):
+def grads_out_kernel(edges, *refs):
+    n = len(edges)
+    parts, sums = refs[:n], refs[n : n + 3]
+    o_ref, gate_ref, up_ref, down_ref, send, recv, local = refs[n + 3 : n + 10]
+    mine, twin_in, cross_in, lane_in, bent_in, depth_in = refs[n + 10 : n + 16]
+    flat, flat_y, flat_h = refs[n + 16 : n + 19], refs[n + 19 : n + 22], refs[n + 22 : n + 25]
     rank, peers = full_places()
-    half = p_ref.shape[1] // 2
-    top, low = pl.ds(0, half), pl.ds(half, half)
+    me, team = team_peers()
+    spot = copy_places()
     loads, swaps, flights = {}, {}, {}
+    count = 0
+
+    def load(source, target):
+        nonlocal count
+        copy = pltpu.make_async_copy(source, target, local.at[count])
+        count += 1
+        copy.start()
+        return copy
+
     for t, depth in enumerate(SUMS):
         for k, plane in enumerate(PLANES):
-            load = pltpu.make_async_copy(
-                p_ref.at[rank(plane, depth)], mine.at[t, k], local.at[t * 4 + k]
-            )
-            load.start()
-            loads[t, k] = load
-    greet(list(peers.values()))
+            place = rank(plane, depth)
+            loads[t, k] = [
+                load(part.at[place], mine.at[t, k, :, pl.ds(begin, part.shape[2])])
+                for part, begin in zip(parts, edges)
+            ]
+    own_loads = [
+        [load(total.at[spot[k]], buffer.at[j]) for j, k in enumerate("HO")]
+        for total, buffer in zip(sums, flat)
+    ]
+    greet([peer for _, peer in team] + [peers["Y"], peers["H"]])
     out = Sender(send, recv)
-    for t, depth in enumerate(SUMS):
+
+    def swap(t):
         for k, plane in enumerate(PLANES):
-            swaps[t, k] = out.go(
-                p_ref.at[rank(plane, depth, True)], twin_in.at[t, k], peers["C"]
-            )
+            place = rank(plane, SUMS[t], True)
+            swaps[t, k] = [
+                out.go(
+                    part.at[place], twin_in.at[t, k, :, pl.ds(begin, part.shape[2])], peers["C"]
+                )
+                for part, begin in zip(parts, edges)
+            ]
 
     def join(t, k):
-        loads[t, k].wait()
-        swaps[t, k].wait_recv()
+        for copy in loads[t, k]:
+            copy.wait()
+        for copy in swaps[t, k]:
+            copy.wait_recv()
         mine[t, k] = plus(mine[t, k], twin_in[t, k]).astype(BF16)
 
     def begin(t):
         join(t, 0)
-        bent_x = out.go(mine.at[t, 0].at[top], bent_in.at[t, 0], peers["X"])
-        bent_y = out.go(mine.at[t, 0].at[low], bent_in.at[t, 1], peers["Y"])
+        to_bend = out.go(mine.at[t, 0], bent_in.at[t], peers["X"])
         join(t, 1)
-        x_top = out.go(mine.at[t, 1].at[top], cross_in.at[t].at[top], peers["X"])
+        to_x = out.go(mine.at[t, 1], cross_in.at[t], peers["X"])
         join(t, 2)
-        y_low = out.go(mine.at[t, 2].at[low], lane_in.at[t].at[low], peers["Y"])
         join(t, 3)
-        flights[t] = [bent_x, bent_y, x_top, y_low]
+        flights[t] = [to_bend, to_x]
 
     def bend(t):
-        bent_x, bent_y, x_top, y_low = flights[t]
-        bent_x.wait_recv()
-        mine[t, 2, top] = plus(mine[t, 2, top], bent_in[t, 0]).astype(BF16)
-        y_top = out.go(mine.at[t, 2].at[top], lane_in.at[t].at[top], peers["Y"])
-        bent_y.wait_recv()
-        mine[t, 1, low] = plus(mine[t, 1, low], bent_in[t, 1]).astype(BF16)
-        x_low = out.go(mine.at[t, 1].at[low], cross_in.at[t].at[low], peers["X"])
-        flights[t] = [x_top, y_low, y_top, x_low]
+        to_bend, to_x = flights[t]
+        to_bend.wait_recv()
+        mine[t, 2] = plus(mine[t, 2], bent_in[t]).astype(BF16)
+        flights[t] = [to_x, out.go(mine.at[t, 2], lane_in.at[t], peers["Y"])]
 
     def close(t):
         for copy in flights[t]:
             copy.wait_recv()
         return plus(mine[t, 3], cross_in[t], lane_in[t])
 
+    y_side, h_side = {}, {}
+
+    def lane(i, j):
+        y_side[i, j] = out.go(sums[i].at[spot["DY"[j]]], flat_y[i].at[j], peers["Y"])
+
+    def along(i):
+        own_loads[i][0].wait()
+        y_side[i, 0].wait_recv()
+        flat[i][0] = plus(flat[i][0], flat_y[i][0]).astype(BF16)
+        h_side[i] = out.go(flat[i].at[0], flat_h[i], peers["H"])
+
+    swap(0)
+    lane(2, 0)
+    swap(1)
+    swap(2)
+    swap(3)
     begin(0)
     begin(1)
+    along(2)
+    lane(0, 0)
     bend(0)
     begin(2)
+    begin(3)
+    along(0)
+    lane(1, 0)
     bend(1)
     mine[0, 3] = close(0).astype(BF16)
     to_hl = out.go(mine.at[0, 3], depth_in.at[0], peers["L"])
-    begin(3)
+    along(1)
+    lane(0, 1)
+    lane(1, 1)
     bend(2)
     mine[1, 3] = close(1).astype(BF16)
     to_l = out.go(mine.at[1, 3], depth_in.at[1], peers["L"])
+    lane(2, 1)
     bend(3)
     total = close(2)
     to_hl.wait_recv()
     mine[2, 3] = plus(total, depth_in[0]).astype(BF16)
     to_h = out.go(mine.at[2, 3], depth_in.at[2], peers["H"])
+    returns = []
+    for i, target in enumerate((gate_ref, up_ref)):
+        own_loads[i][1].wait()
+        y_side[i, 1].wait_recv()
+        h_side[i].wait_recv()
+        flat[i][1] = plus(flat[i][1], flat_y[i][1], flat_h[i][...]).astype(BF16)
+        keep = load(flat[i].at[1, me], target.at[me])
+        returns.append(keep)
+        for place, peer in team:
+            returns.append(out.go(flat[i].at[1, place], target.at[me], peer))
     total = close(3)
     to_l.wait_recv()
     total = plus(total, depth_in[1])
     to_h.wait_recv()
     o_ref[...] = plus(total, depth_in[2])
+    own_loads[2][1].wait()
+    y_side[2, 1].wait_recv()
+    h_side[2].wait_recv()
+    down_ref[...] = plus(flat[2][1], flat_y[2][1], flat_h[2][...])
+    for i, copy in enumerate(returns):
+        if i % 8 == 0:
+            copy.wait()
+        else:
+            copy.wait_recv()
     out.finish()
 
 
-def full_scatter(partial_sum):
-    shares = lax.axis_size("y") * lax.axis_size("h") * 8
-    rows, width = partial_sum.shape[0] // shares, partial_sum.shape[1]
-    blocks = partial_sum.reshape(shares, rows, width)
-    if lax.axis_size("y") != 2 or lax.axis_size("h") != 2:
-        return lax.psum_scatter(blocks, AXES, scatter_dimension=0, tiled=False).astype(F32)
+def grads_out(parts, gate, up, down):
+    ys, hs = lax.axis_size("y"), lax.axis_size("h")
+    shares = ys * hs * 8
+    rows = parts[0].shape[0] // shares
+    blocks = [part.reshape(shares, rows, part.shape[1]) for part in parts]
+    sums = [
+        gate.reshape(ys * hs, 8, -1, gate.shape[1]),
+        up.reshape(ys * hs, 8, -1, up.shape[1]),
+        down.reshape(ys * hs, -1, down.shape[1]),
+    ]
+    if ys != 2 or hs != 2:
+        block = jnp.concatenate(blocks, axis=2)
+        total = lax.psum_scatter(block, AXES, scatter_dimension=0, tiled=False).astype(F32)
+        gate, up, down = (
+            lax.psum_scatter(value, COPIES, scatter_dimension=0, tiled=False) for value in sums
+        )
+        gate, up = (lax.all_to_all(value, TEAM, 0, 0) for value in (gate, up))
+        return total, gate, up, down.astype(F32)
+    edges = [0]
+    for part in parts:
+        edges.append(edges[-1] + part.shape[1])
+    width = edges.pop()
+    flats = [pltpu.VMEM((2, *value.shape[1:]), BF16) for value in sums]
     return remote_call(
-        full_scatter_kernel,
-        jax.ShapeDtypeStruct((rows, width), F32),
-        43,
+        partial(grads_out_kernel, tuple(edges)),
+        (
+            jax.ShapeDtypeStruct((rows, width), F32),
+            jax.ShapeDtypeStruct(sums[0].shape[1:], BF16),
+            jax.ShapeDtypeStruct(sums[1].shape[1:], BF16),
+            jax.ShapeDtypeStruct(sums[2].shape[1:], F32),
+        ),
+        16 * len(parts) + 12 + 3 + 6 + 3 + 14,
         4,
         [
-            pltpu.SemaphoreType.DMA((16,)),
+            pltpu.SemaphoreType.DMA((16 * len(parts) + 6 + 2,)),
             pltpu.VMEM((4, 4, rows, width), BF16),
             pltpu.VMEM((4, 4, rows, width), BF16),
             pltpu.VMEM((4, rows, width), BF16),
             pltpu.VMEM((4, rows, width), BF16),
-            pltpu.VMEM((4, 2, rows // 2, width), BF16),
+            pltpu.VMEM((4, rows, width), BF16),
             pltpu.VMEM((3, rows, width), BF16),
+            *flats,
+            *flats,
+            *[pltpu.VMEM(value.shape[1:], BF16) for value in sums],
         ],
-        56 * 2**20,
-        pltpu.VMEM,
-    )(blocks)
+        60 * 2**20,
+        [pltpu.VMEM, pl.ANY, pl.ANY, pltpu.VMEM],
+        len(parts) + 3,
+    )(*blocks, *sums)
 
 
 def shift(block, distance):
     pieces = lax.axis_size("h") * lax.axis_size("l")
     route = [(i, i + distance) for i in range(pieces) if 0 <= i + distance < pieces]
     return lax.ppermute(block, ("h", "l"), route)
-
-
-def pull(block, axis, distance):
-    size = lax.axis_size(axis)
-    return lax.ppermute(block, axis, [(i, (i - distance) % size) for i in range(size)])
-
-
-def copies_place(dy, dh):
-    ys, hs = lax.axis_size("y"), lax.axis_size("h")
-    y, h = lax.axis_index("y"), lax.axis_index("h")
-    return lax.rem(y + dy, ys) * hs + lax.rem(h + dh, hs)
-
-
-def copies_gather(block):
-    ys, hs = lax.axis_size("y"), lax.axis_size("h")
-    along = [block] + [pull(block, "h", k) for k in range(1, hs)]
-    gathered = jnp.zeros((ys * hs * block.shape[0], block.shape[1]), block.dtype)
-    for dy in range(ys):
-        for dh in range(hs):
-            piece = along[dh] if dy == 0 else pull(along[dh], "y", dy)
-            start = copies_place(dy, dh) * block.shape[0]
-            gathered = lax.dynamic_update_slice_in_dim(gathered, piece, start, axis=0)
-    return gathered
-
-
-def copies_scatter(partial_sum):
-    ys, hs = lax.axis_size("y"), lax.axis_size("h")
-    rows = partial_sum.shape[0] // (ys * hs)
-
-    def piece(dy, dh):
-        return lax.dynamic_slice_in_dim(partial_sum, copies_place(dy, dh) * rows, rows, axis=0)
-
-    along = []
-    for dh in range(hs):
-        arrived = [pull(piece(dy, dh), "y", -dy) for dy in range(1, ys)]
-        along.append((piece(0, dh), arrived))
-    ready = [plus(own, *arrived).astype(BF16) for own, arrived in along[1:]]
-    moved = [pull(ready[dh - 1], "h", -dh) for dh in range(1, hs)]
-    return plus(along[0][0], *along[0][1], *moved)
 
 
 def column_blocks(weight):
@@ -614,14 +700,11 @@
     for column in columns:
         edges.append(edges[-1] + column.shape[1])
     full_width = -(-edges[-1] // 128) * 128
-    swapped = team_swap(
-        jnp.concatenate([column_blocks(gate_weight), column_blocks(up_weight)], axis=1)
-    )
-    gate_cols = copies_gather(swapped[:, :depth].reshape(8 * depth, -1))
-    up_cols = copies_gather(swapped[:, depth:].reshape(8 * depth, -1))
-    down_rows = copies_gather(down_weight)
-    full = full_gather(
-        jnp.pad(jnp.concatenate(columns, axis=1), ((0, 0), (0, full_width - edges[-1])))
+    local_columns = jnp.pad(
+        jnp.concatenate(columns, axis=1), ((0, 0), (0, full_width - edges[-1]))
+    )
+    full, gate_cols, up_cols, down_rows = weights_in(
+        local_columns, column_blocks(gate_weight), column_blocks(up_weight), down_weight
     )
     first = full[:, : edges[3]]
     output_all, side_gate_all, projection_all, left_all, right_all = (
@@ -711,10 +794,10 @@
     grad_product = dot(grad_reduced_all, down_rows, 1, 1)
     grad_gate_low = (grad_product * up_raw * gelu_slope(gate_raw)).astype(BF16)
     grad_up_low = (grad_product * gelu(gate_raw)).astype(BF16)
-    grad_down = copies_scatter(dot(act_low, grad_reduced_all, 0, 0).astype(BF16))
+    part_down = dot(act_low, grad_reduced_all, 0, 0).astype(BF16)
     part_low = (dot(grad_gate_low, gate_cols, 1, 1) + dot(grad_up_low, up_cols, 1, 1)).astype(BF16)
-    mine_gate = copies_scatter(dot(expand_all, grad_gate_low, 0, 0).astype(BF16)).astype(BF16)
-    mine_up = copies_scatter(dot(expand_all, grad_up_low, 0, 0).astype(BF16)).astype(BF16)
+    part_gate = dot(expand_all, grad_gate_low, 0, 0).astype(BF16)
+    part_up = dot(expand_all, grad_up_low, 0, 0).astype(BF16)
     part = from_depth_order(team_scatter(part_low))
     grad_merged, gain_three = rms_back(merged, merged_inv, gains[3], part)
     grad_sum = (grad_after + grad_merged) * HALF_ROOT
@@ -776,28 +859,23 @@
     head_column = jnp.pad(
         head_grads.T.reshape(-1, head_part, 2), ((0, 0), (0, depth - head_part), (0, 0))
     ).reshape(-1, 2)
-    small = jnp.concatenate(
-        [
-            dot(normed_low, grad_left_low, 0, 0),
-            dot(grad_right_low, left_low, 0, 0),
-            gain_grads.T,
-            head_column,
-            jnp.zeros((width, full_width - edges[-1]), F32),
-        ],
-        axis=1,
-    )
-    summed = full_scatter(
-        jnp.concatenate(
-            [
-                dot(normed_low, grad_raw, 0, 0).astype(BF16),
-                dot(mixed, grad_attention_low, 0, 0).astype(BF16),
-                dot(after_low, grad_side_raw, 0, 0).astype(BF16),
-                dot(grad_side_low, side_low, 0, 0).astype(BF16),
-                small.astype(BF16),
-            ],
-            axis=1,
-        )
-    )
+    tail = full_width - edges[6]
+    small = (
+        dot(normed_low, jnp.pad(grad_left_low, ((0, 0), (0, tail - rank))), 0, 0)
+        + dot(grad_right_low, jnp.pad(left_low, ((0, 0), (rank, tail - 2 * rank))), 0, 0)
+        + jnp.pad(gain_grads.T, ((0, 0), (2 * rank, tail - 2 * rank - 6)))
+        + jnp.pad(head_column, ((0, 0), (2 * rank + 6, tail - 2 * rank - 8)))
+    )
+    weight_grads = (
+        dot(normed_low, grad_raw, 0, 0).astype(BF16),
+        dot(mixed, grad_attention_low, 0, 0).astype(BF16),
+        dot(after_low, grad_side_raw, 0, 0).astype(BF16),
+        dot(grad_side_low, side_low, 0, 0).astype(BF16),
+        small.astype(BF16),
+    )
+    summed, back_gate, back_up, grad_down = grads_out(weight_grads, part_gate, part_up, part_down)
+    grad_gate = from_column_blocks(back_gate).astype(F32)
+    grad_up = from_column_blocks(back_up).astype(F32)
     (
         d_query,
         d_key,
@@ -812,13 +890,6 @@
     ) = (summed[:, edges[i] : edges[i + 1]] for i in range(10))
     d_right, d_projection, d_gains = d_right.T, d_projection.T, d_gains.T
     d_heads = d_heads[:head_part].T
-    back = team_swap(
-        jnp.concatenate(
-            [mine_gate.reshape(8, depth, -1), mine_up.reshape(8, depth, -1)], axis=1
-        )
-    )
-    grad_gate = from_column_blocks(back[:, :depth]).astype(F32)
-    grad_up = from_column_blocks(back[:, depth:]).astype(F32)
     return (
         block_out,
         grad_hidden,

time: 1190 us -> 1040 us (0.87)
  waiting for transfers between devices: 166 us -> 2.39 us
  Pallas kernels: 518 us -> 633 us
  local copies, waits for them, and re-layouts: 189 us -> 119 us
  starting transfers between devices: 29.5 us -> 11.1 us
  other arithmetic: 67.5 us -> 50.3 us
    pallas_call x4 -> x2, Pallas kernels: 324 us -> 474 us  [the longest x1 247 us: weights_in(): remote_call(weights_in_kernel, (jax.ShapeDtypeStruct((32, rows, width), B...]
    ppermute x18 -> x0, waiting for transfers between devices: 150 us -> none  [pull(): lax.ppermute(block, axis, [(i, (i - distance) % size) for i in range(size)])]
    concatenate x1 -> x0, local copies, waits for them, and re-layouts: 36.2 us -> none  [layer(): jnp.concatenate([dot(normed_low, grad_raw, 0, 0).astype(BF16), dot(mixed,...]
    pallas_call x2, Pallas kernels: 114 us -> 79.7 us  [team_gather(): remote_call(team_gather_kernel, jax.ShapeDtypeStruct((8, rows, width), bl...]
    dynamic_update_slice x12 -> x0, local copies, waits for them, and re-layouts: 23.9 us -> none  [copies_gather(): gathered = lax.dynamic_update_slice_in_dim(gathered, piece, start, axis=0)]
    ppermute x18 -> x0, starting transfers between devices: 17.9 us -> none  [pull(): lax.ppermute(block, axis, [(i, (i - distance) % size) for i in range(size)])]
    convert_element_type x6 -> x0, other arithmetic: 16.5 us -> none  [the longest x3 8.83 us: copies_scatter(): ready = [plus(own, *arrived).astype(BF16) for own, arrived in along[1:]]]
    ppermute x4, waiting for transfers between devices: 16.5 us -> 2.39 us  [shift(): return lax.ppermute(block, ('h', 'l'), route)]
  transfers between devices with their start and end apart: 22 -> 4, of which waited for: 7 -> 1; matrix products, arithmetic and copies ran while one was open for 22% -> 5% of each run, Pallas kernels for 23% -> 0%
where the time goes in v3:
time: 1040 us; the launch traced here: 1030 us
  Pallas kernels  633 us (61%)
  matrix products  209 us (20%)
  local copies, waits for them, and re-layouts  119 us (11%)
  other arithmetic  50.3 us (5%)
  starting transfers between devices  11.1 us (1%)
    pallas_call x1, Pallas kernels, weights_in(): remote_call(weights_in_kernel, (jax.ShapeDtypeStruct((32, rows, width), B...  247 us
    pallas_call x1, Pallas kernels, grads_out(): remote_call(partial(grads_out_kernel, tuple(edges)), (jax.ShapeDtypeStruc...  227 us
    dot_general x27, matrix products, dot(): lax.dot_general(left, right, (((left_dim,), (right_dim,)), ((), ())), pre...  194 us
    pallas_call x2, Pallas kernels, team_gather(): remote_call(team_gather_kernel, jax.ShapeDtypeStruct((8, rows, width), bl...  79.7 us
    pallas_call x2, Pallas kernels, team_scatter(): remote_call(team_scatter_kernel, jax.ShapeDtypeStruct((rows, width), F32)...  79.4 us
    unnamed x282, local copies, waits for them, and re-layouts  36.5 us
  transfers between devices with their start and end apart: 4, of which 1 were waited for; matrix products, arithmetic and copies ran while one was open for 5% of the time, Pallas kernels for 0%

profile of v3, /device:TPU:1, one launch (start us, length us, event | category | flops | bytes accessed | tf_op | source)
XLA Modules:
  0.0 1027.3 jit_solution(18249341094268440524)
XLA Ops:
  11.7 247.3 %shard_map.280 = (bf16[32,64,5888]{2,1,0:T(8,128)(2,1)}, bf16[4,8,64,1024]{3,2,1,0:T(8,128)(2,1)}, bf16[4,8,64,1024]{3,2,1,0:T(8,128)(2,1)}, bf16[4,256,2048]{2,1,0:T(8,128)(2,1)}) custom-call(bf16[64,5888]{1,0:T(8,128)(2,1)} %pad.29.x_ref, bf16[8,64,1024]{2,1,0:T(8,128)(2,1)} %reshape.463.gate_ref, bf16[8,64,1024]{2,1,0:T(8,128)(2,1)} %reshape.465.up_ref, ...), custom_call_target="tpu_custom_call" | custom-call | tf_op jit(solution)/shard_map/pallas_call | solution.py:406
  261.8 6.5 fusion.3
  284.0 5.9 collective-permute-start
  295.9 2.5 copy.411
  316.4 2.4 copy.412
  324.5 2.9 fusion.119
  330.2 6.2 multiply_reduce_fusion.16
  342.8 2.6 reshape.473.x_ref
  345.4 39.8 %shard_map.281 = bf16[8,256,2048]{2,1,0:T(8,128)(2,1)} custom-call(bf16[256,2048]{1,0:T(8,128)(2,1)} %reshape.473.x_ref), custom_call_target="tpu_custom_call" | custom-call | tf_op jit(solution)/shard_map/pallas_call | solution.py:181
  385.2 14.5 %fusion.120 = f32[2048,1024]{1,0:T(8,128)} fusion(bf16[2048,2048]{1,0:T(8,128)(2,1)} %bitcast.225, bf16[2048,1024]{1,0:T(8,128)(2,1)} %bitcast.336), kind=kOutput, calls=%fused_computation.235 | convolution fusion | flops 8589934592 | bytes 20971520 | tf_op jit(solution)/shard_map/dot_general | solution.py:25
  399.8 14.8 %multiply_convert_fusion.1 = (bf16[2048,1024]{1,0:T(8,128)(2,1)}, f32[2048,1024]{1,0:T(8,128)}) fusion(f32[2048,1024]{1,0:T(8,128)} %fusion.120, bf16[2048,2048]{1,0:T(8,128)(2,1)S(1)} %bitcast.226, bf16[2048,1024]{1,0:T(8,128)(2,1)S(1)} %bitcast.335), kind=kOutput, calls=%fused_computation.18 | convolution fusion | flops 8610906112 | bytes 33554432 | tf_op jit(solution)/shard_map/dot_general | solution.py:25
  414.6 10.7 %convolution_convert_fusion.2 = bf16[2048,2048]{1,0:T(8,128)(2,1)S(1)} fusion(bf16[2048,1024]{1,0:T(8,128)(2,1)} %get-tuple-element.226, bf16[1024,2048]{1,0:T(8,128)(2,1)S(1)} %bitcast.339), kind=kOutput, calls=%fused_computation.21 | convolution fusion | flops 8594128896 | bytes 16777216 | tf_op jit(solution)/shard_map/dot_general | solution.py:25
  425.2 39.7 %shard_map.282 = f32[256,2048]{1,0:T(8,128)S(1)} custom-call(bf16[8,256,2048]{2,1,0:T(8,128)(2,1)S(1)} %bitcast.217), custom_call_target="tpu_custom_call" | custom-call | tf_op jit(solution)/shard_map/pallas_call | solution.py:237
  465.6 2.4 fusion.65
  475.5 2.7 multiply_reduce_fusion.2
  481.0 39.9 %shard_map.283 = bf16[8,256,2048]{2,1,0:T(8,128)(2,1)} custom-call(bf16[256,2048]{1,0:T(8,128)(2,1)} %multiply_convert_fusion.5.x_ref), custom_call_target="tpu_custom_call" | custom-call | tf_op jit(solution)/shard_map/pallas_call | solution.py:181
  520.9 24.4 %multiply_convert_fusion = (bf16[2048,1024]{1,0:T(8,128)(2,1)}, bf16[2048,1024]{1,0:T(8,128)(2,1)}) fusion(f32[2048,1024]{1,0:T(8,128)} %fusion.120, f32[2048,1024]{1,0:T(8,128)} %get-tuple-element.227, bf16[2048,2048]{1,0:T(8,128)(2,1)} %bitcast.231, bf16[1024,2048]{1,0:T(8,128)(2,1)} %bitcast.338), kind=kOutput, calls=%fused_computation.17 | convolution fusion | flops 8638169088 | bytes 37748736 | tf_op jit(solution)/shard_map/dot_general | solution.py:25
  545.3 13.9 %fusion.121 = f32[2048,2048]{1,0:T(8,128)} fusion(bf16[2048,1024]{1,0:T(8,128)(2,1)} %get-tuple-element.169, bf16[2048,1024]{1,0:T(8,128)(2,1)S(1)} %bitcast.337), kind=kOutput, calls=%fused_computation.236 | convolution fusion | flops 8589934592 | bytes 25165824 | tf_op jit(solution)/shard_map/dot_general | solution.py:25
  559.3 14.7 %add_convert_fusion = bf16[2048,2048]{1,0:T(8,128)(2,1)S(1)} fusion(f32[2048,2048]{1,0:T(8,128)} %fusion.121, bf16[2048,1024]{1,0:T(8,128)(2,1)} %get-tuple-element.168, bf16[2048,1024]{1,0:T(8,128)(2,1)} %bitcast.334), kind=kOutput, calls=%fused_computation.1 | convolution fusion | flops 8598323200 | bytes 33554432 | tf_op jit(solution)/shard_map/dot_general | solution.py:25
  574.0 39.7 %shard_map.284 = f32[256,2048]{1,0:T(8,128)S(1)} custom-call(bf16[8,256,2048]{2,1,0:T(8,128)(2,1)S(1)} %bitcast.216), custom_call_target="tpu_custom_call" | custom-call | tf_op jit(solution)/shard_map/pallas_call | solution.py:237
  615.0 2.7 reshape.481
  617.7 2.4 copy.352
  620.1 4.1 reshape.482
  624.3 2.3 multiply_reduce_fusion.3
  627.1 4.6 multiply_reduce_fusion.4
  634.0 6.9 fusion.33
  640.9 2.3 copy.407
  643.1 7.2 fusion.17
  652.6 3.9 fusion.19
  656.5 2.3 convolution_bitcast_fusion
  662.6 11.1 %convolution_convert_fusion.5 = bf16[2048,1024]{1,0:T(8,128)(2,1)} fusion(bf16[2048,2048]{1,0:T(8,128)(2,1)S(1)} %bitcast.229, bf16[2048,1024]{1,0:T(8,128)(2,1)S(1)} %copy-done.121), kind=kOutput, calls=%fused_computation.36 | convolution fusion | flops 8592031744 | bytes 16777216 | tf_op jit(solution)/shard_map/dot_general | solution.py:25
  673.6 12.7 %convolution_convert_fusion.4 = bf16[2048,1024]{1,0:T(8,128)(2,1)} fusion(bf16[2048,2048]{1,0:T(8,128)(2,1)S(1)} %bitcast.230, bf16[2048,1024]{1,0:T(8,128)(2,1)} %get-tuple-element.168), kind=kOutput, calls=%fused_computation.35 | convolution fusion | flops 8592031744 | bytes 16777216 | tf_op jit(solution)/shard_map/dot_general | solution.py:25
  686.3 11.0 %convolution_convert_fusion.3 = bf16[1024,2048]{1,0:T(8,128)(2,1)} fusion(bf16[2048,1024]{1,0:T(8,128)(2,1)S(1)} %copy-done.120, bf16[2048,2048]{1,0:T(8,128)(2,1)S(1)} %bitcast.234), kind=kOutput, calls=%fused_computation.34 | convolution fusion | flops 8592031744 | bytes 16777216 | tf_op jit(solution)/shard_map/dot_general | solution.py:25
  718.4 5.5 convolution_convert_fusion.1
  724.0 2.4 collective-permute-done.3
  733.2 2.6 multiply_reduce_fusion.18
  736.1 6.6 fusion.29
  742.7 6.8 convolution_convert_fusion
  749.6 3.2 fusion.42
  755.5 4.2 fusion.32
  759.7 226.7 %shard_map.285 = (f32[64,5888]{1,0:T(8,128)}, bf16[8,64,1024]{2,1,0:T(8,128)(2,1)}, bf16[8,64,1024]{2,1,0:T(8,128)(2,1)}, f32[256,2048]{1,0:T(8,128)}) custom-call(bf16[32,64,3072]{2,1,0:T(8,128)(2,1)} %bitcast.218, bf16[32,64,2048]{2,1,0:T(8,128)(2,1)} %bitcast.219, bf16[32,64,256]{2,1,0:T(8,128)(2,1)} %bitcast.251, bf16[32,64,256]{2,1,0:T(8,128)(2,1)} %bitcast.289, ...), custom_call_target="tpu_custom_call" | custom-call | tf_op jit(solution)/shard_map/pallas_call | solution.py:592
  995.6 4.3 reshape.498
  999.8 4.5 copy.376
  1004.4 3.9 reshape.495
  1008.3 4.1 reshape.499
  1012.3 4.5 copy.377
  1016.9 3.9 reshape.496
  1022.1 3.7 fusion.41
  (413 shorter events, 130.1 us)
Async XLA Ops:
  11.7 249.2 %copy-start.3 = (bf16[256,2048]{1,0:T(8,128)(2,1)S(1)}, bf16[256,2048]{1,0:T(8,128)(2,1)}, u32[]{:S(2)}) copy-start(bf16[256,2048]{1,0:T(8,128)(2,1)} %param.17) | copy-start | bytes 3145732
  260.9 75.6 %copy-start.61 = (f32[1,2048]{1,0:T(1,128)}, f32[1,2048]{1,0:T(1,128)S(1)}, u32[]{:S(2)}) copy-start(f32[1,2048]{1,0:T(1,128)S(1)} %get-tuple-element.212) | copy-start | bytes 24580
  270.0 6.4 copy-start.24
  270.0 10.0 copy-start.26
  277.4 12.5 %copy-start.78 = (f32[256]{0:T(256)S(1)}, f32[256]{0:T(256)}, u32[]{:S(2)}) copy-start(f32[256]{0:T(256)} %copy-done.77) | copy-start | bytes 3076
  280.1 12.0 %copy-start.52 = (f32[256,128]{1,0:T(8,128)}, f32[256,128]{1,0:T(8,128)S(1)}, u32[]{:S(2)}) copy-start(f32[256,128]{1,0:T(8,128)S(1)} %get-tuple-element.216) | copy-start | bytes 393220
  280.1 26.4 %copy-start.39 = (f32[256,128]{1,0:T(8,128)}, f32[256,128]{1,0:T(8,128)S(1)}, u32[]{:S(2)}) copy-start(f32[256,128]{1,0:T(8,128)S(1)} %get-tuple-element.217) | copy-start | bytes 393220
  280.8 11.3 %copy-start.19 = (f32[256,3072]{1,0:T(8,128)S(1)}, f32[256,3072]{1,0:T(8,128)}, u32[]{:S(2)}) copy-start(f32[256,3072]{1,0:T(8,128)} %copy-done.18) | copy-start | bytes 9437188
  280.9 12.6 %copy-start.48 = (bf16[1,256,2,128]{3,1,2,0:T(8,128)(2,1)}, bf16[1,256,2,128]{3,1,2,0:T(8,128)(2,1)S(1)}, u32[]{:S(2)}) copy-start(bf16[1,256,2,128]{3,1,2,0:T(8,128)(2,1)S(1)} %get-tuple-element.203) | copy-start | bytes 393220
  280.9 12.6 %copy-start.50 = (bf16[1,256,2,128]{3,1,2,0:T(8,128)(2,1)}, bf16[1,256,2,128]{3,1,2,0:T(8,128)(2,1)S(1)}, u32[]{:S(2)}) copy-start(bf16[1,256,2,128]{3,1,2,0:T(8,128)(2,1)S(1)} %get-tuple-element.204) | copy-start | bytes 393220
  281.8 39.6 %collective-permute-start.1 = (bf16[2,256,2,256]{3,1,2,0:T(8,128)(2,1)}, bf16[2,256,2,256]{3,1,2,0:T(8,128)(2,1)}, u32[]{:S(2)}, u32[]{:S(2)}) collective-permute-start(bf16[2,256,2,256]{3,1,2,0:T(8,128)(2,1)} %pad_maximum_fusion.8), channel_id=1, source_target_pairs={{0,1},{1,2},{2,3},{4,5},{5,6},{6,7},{8,9},{9,10},{10,11},{12,13},{... | collective-permute-start | bytes 1572872 | tf_op jit(solution)/shard_map/ppermute | solution.py:623
  284.0 37.4 %collective-permute-start = (bf16[2,256,2,256]{3,1,2,0:T(8,128)(2,1)}, bf16[2,256,2,256]{3,1,2,0:T(8,128)(2,1)}, u32[]{:S(2)}, u32[]{:S(2)}) collective-permute-start(bf16[2,256,2,256]{3,1,2,0:T(8,128)(2,1)} %pad_maximum_fusion.8), channel_id=1, source_target_pairs={{0,2},{1,3},{4,6},{5,7},{8,10},{9,11},{12,14},{13,15},{16,18},{17,... | collective-permute-start | bytes 1572872 | tf_op jit(solution)/shard_map/ppermute | solution.py:623
  298.3 8.2 copy-start.5
  307.8 6.5 copy-start.111
  309.1 162.2 %copy-start.92 = (f32[256]{0:T(256)}, f32[256]{0:T(256)S(1)}, u32[]{:S(2)}) copy-start(f32[256]{0:T(256)S(1)} %compare_convert_fusion) | copy-start | bytes 3076
  311.7 11.7 %copy-start.41 = (bf16[256,8,128]{2,0,1:T(8,128)(2,1)}, bf16[256,8,128]{2,0,1:T(8,128)(2,1)S(1)}, u32[]{:S(2)}) copy-start(bf16[256,8,128]{2,0,1:T(8,128)(2,1)S(1)} %copy.348) | copy-start | bytes 1572868
  313.1 10.4 %copy-start.42 = (bf16[256,8,128]{2,0,1:T(8,128)(2,1)}, bf16[256,8,128]{2,0,1:T(8,128)(2,1)S(1)}, u32[]{:S(2)}) copy-start(bf16[256,8,128]{2,0,1:T(8,128)(2,1)S(1)} %copy.347) | copy-start | bytes 1572868
  321.4 15.1 %copy-start.104 = (f32[256]{0:T(256)}, f32[256]{0:T(256)S(1)}, u32[]{:S(2)}) copy-start(f32[256]{0:T(256)S(1)} %get-tuple-element.220) | copy-start | bytes 3076
  321.4 15.2 %copy-start.7 = (f32[256,2048]{1,0:T(8,128)}, f32[256,2048]{1,0:T(8,128)S(1)}, u32[]{:S(2)}) copy-start(f32[256,2048]{1,0:T(8,128)S(1)} %get-tuple-element.221) | copy-start | bytes 6291460
  330.2 6.2 copy-start.44
  330.2 6.3 copy-start.72
  330.2 6.3 copy-start.74
  330.2 6.4 copy-start.79
  337.8 127.4 %copy-start.1 = (f32[256,2048]{1,0:T(8,128)}, f32[256,2048]{1,0:T(8,128)S(1)}, u32[]{:S(2)}) copy-start(f32[256,2048]{1,0:T(8,128)S(1)} %get-tuple-element.167) | copy-start | bytes 6291460
  385.2 14.6 %copy-start.23 = (bf16[8,256,2048]{2,1,0:T(8,128)(2,1)S(1)}, bf16[8,256,2048]{2,1,0:T(8,128)(2,1)}, u32[]{:S(2)}) copy-start(bf16[8,256,2048]{2,1,0:T(8,128)(2,1)} %shard_map.281) | copy-start | bytes 25165828
  385.2 14.5 %copy-start.117 = (bf16[4,8,64,1024]{3,2,1,0:T(8,128)(2,1)S(1)}, bf16[4,8,64,1024]{3,2,1,0:T(8,128)(2,1)}, u32[]{:S(2)}) copy-start(bf16[4,8,64,1024]{3,2,1,0:T(8,128)(2,1)} %get-tuple-element.25) | copy-start | bytes 12582916
  399.8 14.8 %copy-start.119 = (bf16[4,256,2048]{2,1,0:T(8,128)(2,1)S(1)}, bf16[4,256,2048]{2,1,0:T(8,128)(2,1)}, u32[]{:S(2)}) copy-start(bf16[4,256,2048]{2,1,0:T(8,128)(2,1)} %get-tuple-element.26) | copy-start | bytes 12582916
  465.6 5.7 copy-start.9
  468.0 5.4 copy-start.59
  520.9 24.4 %copy-start.118 = (bf16[4,8,64,1024]{3,2,1,0:T(8,128)(2,1)S(1)}, bf16[4,8,64,1024]{3,2,1,0:T(8,128)(2,1)}, u32[]{:S(2)}) copy-start(bf16[4,8,64,1024]{3,2,1,0:T(8,128)(2,1)} %get-tuple-element.24) | copy-start | bytes 12582916
  633.0 77.6 %copy-start.22 = (bf16[256,2048]{1,0:T(8,128)(2,1)}, bf16[256,2048]{1,0:T(8,128)(2,1)S(1)}, u32[]{:S(2)}) copy-start(bf16[256,2048]{1,0:T(8,128)(2,1)S(1)} %get-tuple-element.183) | copy-start | bytes 3145732
  634.0 16.3 %slice-start = ((s8[6291456]{0:T(1024)(128)(4,1)}), s8[2097152]{0:T(1024)(128)(4,1)S(1)}, s32[]{:S(2)}) async-start(s8[6291456]{0:T(1024)(128)(4,1)} %bitcast.222), calls=%async_computation | async-start | bytes 4194304
  643.1 7.2 slice-start.1
  643.1 7.2 copy-start.56
  650.4 12.2 %slice-start.2 = ((s8[8388608]{0:T(1024)(128)(4,1)}), s8[4194304]{0:T(1024)(128)(4,1)S(1)}, s32[]{:S(2)}) async-start(s8[8388608]{0:T(1024)(128)(4,1)} %bitcast.227), calls=%async_computation.2 | async-start | bytes 8388608
  652.6 10.0 slice-start.3
  658.9 38.5 %copy-start.32 = (f32[1,768,2,256]{3,1,2,0:T(8,128)}, f32[1,768,2,256]{3,1,2,0:T(8,128)S(1)}, u32[]{:S(2)}) copy-start(f32[1,768,2,256]{3,1,2,0:T(8,128)S(1)} %convolution_bitcast_fusion) | copy-start | bytes 4718596
  662.5 23.8 %slice-start.4 = ((s8[8388608]{0:T(1024)(128)(4,1)}), s8[4194304]{0:T(1024)(128)(4,1)S(1)}, s32[]{:S(2)}) async-start(s8[8388608]{0:T(1024)(128)(4,1)} %bitcast.232), calls=%async_computation.4 | async-start | bytes 8388608
  673.6 12.7 %slice-start.5 = ((s8[8388608]{0:T(1024)(128)(4,1)}), s8[4194304]{0:T(1024)(128)(4,1)S(1)}, s32[]{:S(2)}) async-start(s8[8388608]{0:T(1024)(128)(4,1)} %bitcast.232), calls=%async_computation.5 | async-start | bytes 8388608
  673.6 12.7 %copy-start.120 = (bf16[2048,1024]{1,0:T(8,128)(2,1)S(1)}, bf16[2048,1024]{1,0:T(8,128)(2,1)}, u32[]{:S(2)}) copy-start(bf16[2048,1024]{1,0:T(8,128)(2,1)} %get-tuple-element.226) | copy-start | bytes 12582916
  686.3 11.0 %copy-start.30 = (f32[1,768,2,256]{3,1,2,0:T(8,128)S(1)}, f32[1,768,2,256]{3,1,2,0:T(8,128)}, u32[]{:S(2)}) copy-start(f32[1,768,2,256]{3,1,2,0:T(8,128)} %fusion.53) | copy-start | bytes 4718596
  698.6 27.7 %collective-permute-start.3 = (bf16[2,256,2,256]{3,1,2,0:T(8,128)(2,1)}, bf16[2,256,2,256]{3,1,2,0:T(8,128)(2,1)}, u32[]{:S(2)}, u32[]{:S(2)}) collective-permute-start(bf16[2,256,2,256]{3,1,2,0:T(8,128)(2,1)} %get-tuple-element.190), channel_id=1, source_target_pairs={{2,0},{3,1},{6,4},{7,5},{10,8},{11,9},{14,12},{15,13},{18,16},{19,... | collective-permute-start | bytes 1572872 | tf_op jit(solution)/shard_map/ppermute | solution.py:623
  699.9 26.4 %collective-permute-start.2 = (bf16[2,256,2,256]{3,1,2,0:T(8,128)(2,1)}, bf16[2,256,2,256]{3,1,2,0:T(8,128)(2,1)}, u32[]{:S(2)}, u32[]{:S(2)}) collective-permute-start(bf16[2,256,2,256]{3,1,2,0:T(8,128)(2,1)} %get-tuple-element.189), channel_id=1, source_target_pairs={{1,0},{2,1},{3,2},{5,4},{6,5},{7,6},{9,8},{10,9},{11,10},{13,12},{... | collective-permute-start | bytes 1572872 | tf_op jit(solution)/shard_map/ppermute | solution.py:623
  709.7 5.1 copy-start.28
  709.7 5.1 copy-start.29
  718.4 7.9 copy-start.31
  718.4 7.9 copy-start.33
  986.4 8.5 copy-start.107
  (84 other events, 219.1 us)

commit v4 on v3

--- a/solution.py
+++ b/solution.py
@@ -108,6 +108,28 @@
     for part in parts[1:]:
         total = total + part.astype(F32)
     return total
+
+
+def strips(ref):
+    if len(ref.shape) == 3:
+        return [ref.at[i] for i in range(ref.shape[0])]
+    step = min(16, ref.shape[0])
+    return [ref.at[pl.ds(i, step)] for i in range(0, ref.shape[0], step)]
+
+
+def add_into(target, *sources):
+    for strip, *others in zip(strips(target), *[strips(source) for source in sources]):
+        total = strip[...]
+        if len(others) > 1:
+            total = plus(total, *[other[...] for other in others])
+        else:
+            total = total + others[0][...].astype(total.dtype)
+        strip[...] = total.astype(target.dtype)
+
+
+def add_to(target, *sources):
+    for strip, *others in zip(strips(target), *[strips(source) for source in sources]):
+        strip[...] = plus(*[other[...] for other in others]).astype(target.dtype)
 
 
 def remote_call(kernel, out, copies, identity, scratch=(), vmem=None, spaces=pl.ANY, inputs=1):
@@ -141,21 +163,33 @@
     return own, twin, {"xc": other}, {"xc": cross}, {"l": side}
 
 
-def team_gather_kernel(x_ref, o_ref, send, recv, local):
+def team_gather_kernel(extra, *refs):
+    if extra:
+        x_ref, near_ref, far_ref, o_ref, blocks_ref, send, recv, local = refs
+    else:
+        x_ref, o_ref, send, recv, local = refs
     own, _, core, cross, side = team_places()
     half = x_ref.shape[0] // 2
     top, low = pl.ds(0, half), pl.ds(half, half)
-    keep = pltpu.make_async_copy(x_ref, o_ref.at[own["O"]], local)
-    keep.start()
-    greet([core, cross, side])
+    keeps = [pltpu.make_async_copy(x_ref, o_ref.at[own["O"]], local.at[0])]
+    lane = {"y": 1 - lax.axis_index("y")} if extra else None
+    if extra:
+        spot = copy_places()
+        near, far = blocks_ref.at[spot["O"]], blocks_ref.at[spot["H"]]
+        keeps.append(pltpu.make_async_copy(near_ref, near, local.at[1]))
+        keeps.append(pltpu.make_async_copy(far_ref, far, local.at[2]))
+    for keep in keeps:
+        keep.start()
+    greet([core, cross, side] + ([lane] if extra else []))
     out = Sender(send, recv)
+    twins = [out.go(near_ref, near, lane), out.go(far_ref, far, lane)] if extra else []
     mine, from_side, from_cross = o_ref.at[own["O"]], o_ref.at[own["L"]], o_ref.at[own["X"]]
     diagonal = o_ref.at[own["D"]]
     side_top = out.go(x_ref.at[top], mine.at[top], side)
     cross_low = out.go(x_ref.at[low], mine.at[low], cross)
     side_low = out.go(x_ref.at[low], mine.at[low], side)
     cross_top = out.go(x_ref.at[top], mine.at[top], cross)
-    twins = [out.go(x_ref, mine, core)]
+    twins.append(out.go(x_ref, mine, core))
     side_top.wait_recv()
     diagonal_top = out.go(from_side.at[top], from_side.at[top], cross)
     twins.append(out.go(from_side.at[top], from_side.at[top], core))
@@ -173,22 +207,51 @@
     for copy in twins:
         copy.wait_recv()
     out.finish()
-    keep.wait()
+    for keep in keeps:
+        keep.wait()
 
 
 def team_gather(block):
     rows, width = block.shape
     gathered = remote_call(
-        team_gather_kernel,
+        partial(team_gather_kernel, False),
         jax.ShapeDtypeStruct((8, rows, width), block.dtype),
         13,
         0,
-        [pltpu.SemaphoreType.DMA],
+        [pltpu.SemaphoreType.DMA((1,))],
+        40 * 2**20,
+        pltpu.VMEM,
     )(block)
     return gathered.reshape(8 * rows, width)
 
 
-def team_scatter_kernel(p_ref, o_ref, send, recv, local, mine, twin_in, cross_in, side_in, bent_in):
+def team_gather_with(block, near, far):
+    rows, width = block.shape
+    if far is None:
+        return team_gather(block), lax.all_gather(near, COPIES, axis=0, tiled=True)
+    gathered, blocks = remote_call(
+        partial(team_gather_kernel, True),
+        (
+            jax.ShapeDtypeStruct((8, rows, width), block.dtype),
+            jax.ShapeDtypeStruct((4, *near.shape), near.dtype),
+        ),
+        15,
+        2,
+        [pltpu.SemaphoreType.DMA((3,))],
+        vmem=40 * 2**20,
+        spaces=[pltpu.VMEM] * 2,
+        inputs=3,
+    )(block, near, far)
+    return gathered.reshape(8 * rows, width), blocks.reshape(-1, near.shape[1])
+
+
+def team_scatter_kernel(extra, *refs):
+    if extra:
+        p_ref, f_ref, o_ref, sum_ref, send, recv, local = refs[:7]
+        lane_mine, lane_in = refs[12:]
+    else:
+        p_ref, o_ref, send, recv, local = refs[:5]
+    mine, twin_in, cross_in, side_in, bent_in = refs[7:12] if extra else refs[5:]
     own, twin, core, cross, side = team_places()
     half = p_ref.shape[1] // 2
     top, low = pl.ds(0, half), pl.ds(half, half)
@@ -196,14 +259,25 @@
     for i, k in enumerate("DXLO"):
         loads.append(pltpu.make_async_copy(p_ref.at[own[k]], mine.at[i], local.at[i]))
         loads[-1].start()
-    greet([core, cross, side])
+    lane = {"y": 1 - lax.axis_index("y")} if extra else None
+    if extra:
+        spot = copy_places()
+        for j, k in enumerate("HO"):
+            loads.append(
+                pltpu.make_async_copy(f_ref.at[spot[k]], lane_mine.at[j], local.at[4 + j])
+            )
+            loads[-1].start()
+    greet([core, cross, side] + ([lane] if extra else []))
     out = Sender(send, recv)
+    lanes = []
+    if extra:
+        lanes = [out.go(f_ref.at[spot[k]], lane_in.at[j], lane) for j, k in enumerate("DY")]
     swaps = [out.go(p_ref.at[twin[k]], twin_in.at[i], core) for i, k in enumerate("DXLO")]
 
     def join(i):
         loads[i].wait()
         swaps[i].wait_recv()
-        mine[i] = plus(mine[i], twin_in[i]).astype(BF16)
+        add_into(mine.at[i], twin_in.at[i])
 
     join(0)
     bent_cross = out.go(mine.at[0].at[top], bent_in.at[0], cross)
@@ -213,43 +287,60 @@
     join(2)
     side_low = out.go(mine.at[2].at[low], side_in.at[low], side)
     bent_cross.wait_recv()
-    mine[2, top] = plus(mine[2, top], bent_in[0]).astype(BF16)
+    add_into(mine.at[2, top], bent_in.at[0])
     side_top = out.go(mine.at[2].at[top], side_in.at[top], side)
     bent_side.wait_recv()
-    mine[1, low] = plus(mine[1, low], bent_in[1]).astype(BF16)
+    add_into(mine.at[1, low], bent_in.at[1])
     cross_low = out.go(mine.at[1].at[low], cross_in.at[low], cross)
     loads[3].wait()
     swaps[3].wait_recv()
-    o_ref[...] = plus(mine[3], twin_in[3])
     cross_top.wait_recv()
     side_low.wait_recv()
-    o_ref[top] += cross_in[top].astype(F32)
-    o_ref[low] += side_in[low].astype(F32)
+    add_to(o_ref.at[top], mine.at[3, top], twin_in.at[3, top], cross_in.at[top])
+    add_to(o_ref.at[low], mine.at[3, low], twin_in.at[3, low], side_in.at[low])
     side_top.wait_recv()
     cross_low.wait_recv()
-    o_ref[top] += side_in[top].astype(F32)
-    o_ref[low] += cross_in[low].astype(F32)
+    add_into(o_ref.at[top], side_in.at[top])
+    add_into(o_ref.at[low], cross_in.at[low])
+    for j, copy in enumerate(lanes):
+        loads[4 + j].wait()
+        copy.wait_recv()
+        add_to(sum_ref.at[j], lane_mine.at[j], lane_in.at[j])
     out.finish()
 
 
-def team_scatter(partial_sum):
+def team_scatter(partial_sum, lane_sum=None):
     rows, width = partial_sum.shape[0] // 8, partial_sum.shape[1]
+    scratch = [
+        pltpu.VMEM((4, rows, width), BF16),
+        pltpu.VMEM((4, rows, width), BF16),
+        pltpu.VMEM((rows, width), BF16),
+        pltpu.VMEM((rows, width), BF16),
+        pltpu.VMEM((2, rows // 2, width), BF16),
+    ]
+    total = jax.ShapeDtypeStruct((rows, width), F32)
+    blocks = partial_sum.reshape(8, rows, width)
+    if lane_sum is None:
+        return remote_call(
+            partial(team_scatter_kernel, False),
+            total,
+            10,
+            1,
+            [pltpu.SemaphoreType.DMA((4,)), *scratch],
+            40 * 2**20,
+            pltpu.VMEM,
+        )(blocks)
+    pair = (2, *lane_sum.shape[1:])
     return remote_call(
-        team_scatter_kernel,
-        jax.ShapeDtypeStruct((rows, width), F32),
-        10,
-        1,
-        [
-            pltpu.SemaphoreType.DMA((4,)),
-            pltpu.VMEM((4, rows, width), BF16),
-            pltpu.VMEM((4, rows, width), BF16),
-            pltpu.VMEM((rows, width), BF16),
-            pltpu.VMEM((rows, width), BF16),
-            pltpu.VMEM((2, rows // 2, width), BF16),
-        ],
-        40 * 2**20,
-        pltpu.VMEM,
-    )(partial_sum.reshape(8, rows, width))
+        partial(team_scatter_kernel, True),
+        (total, jax.ShapeDtypeStruct(pair, BF16)),
+        12,
+        5,
+        [pltpu.SemaphoreType.DMA((6,)), *scratch, pltpu.VMEM(pair, BF16), pltpu.VMEM(pair, BF16)],
+        48 * 2**20,
+        [pltpu.VMEM] * 2,
+        2,
+    )(blocks, lane_sum)
 
 
 def team_peers():
@@ -298,7 +389,8 @@
 
 
 def weights_in_kernel(
-    x_ref, gate_ref, up_ref, down_ref, o_ref, gates_ref, ups_ref, downs_ref, send, recv, local
+    x_ref, gate_in, up_in, down_ref, o_ref, gates_ref, ups_ref, far_ref, send, recv, local, split,
+    gate_ref, up_ref,
 ):
     rank, peers = full_places()
     me, team = team_peers()
@@ -307,19 +399,36 @@
     def at(plane, depth):
         return o_ref.at[rank(plane, depth)]
 
+    pieces = []
+    for source, target in ((gate_in, gate_ref), (up_in, up_ref)):
+        width = source.shape[1] // 32
+        for r in range(8):
+            for c in range(4):
+                begin = ((c // 2 * 4 + r // 2) * 2 + c % 2) * 2 + r % 2
+                pieces.append(
+                    pltpu.make_async_copy(
+                        source.at[:, pl.ds(begin * width, width)],
+                        target.at[r, :, pl.ds(c * width, width)],
+                        split.at[len(pieces)],
+                    )
+                )
+    for piece in pieces:
+        piece.start()
     keeps = [
         pltpu.make_async_copy(x_ref, at("O", "O"), local.at[0]),
-        pltpu.make_async_copy(down_ref, downs_ref.at[spot["O"]], local.at[1]),
-        pltpu.make_async_copy(gate_ref.at[me], gates_ref.at[spot["O"], me], local.at[2]),
-        pltpu.make_async_copy(up_ref.at[me], ups_ref.at[spot["O"], me], local.at[3]),
+        pltpu.make_async_copy(gate_ref.at[me], gates_ref.at[spot["O"], me], local.at[1]),
+        pltpu.make_async_copy(up_ref.at[me], ups_ref.at[spot["O"], me], local.at[2]),
     ]
-    for keep in keeps:
-        keep.start()
+    keeps[0].start()
     greet([peer for _, peer in team] + [peers["Y"], peers["H"]])
     out = Sender(send, recv)
     swaps, twins = [], []
     to_h = out.go(x_ref, at("O", "O"), peers["H"])
     to_l = out.go(x_ref, at("O", "O"), peers["L"])
+    for piece in pieces:
+        piece.wait()
+    keeps[1].start()
+    keeps[2].start()
     for place, peer in team:
         swaps.append(out.go(gate_ref.at[place], gates_ref.at[spot["O"], me], peer))
         swaps.append(out.go(up_ref.at[place], ups_ref.at[spot["O"], me], peer))
@@ -345,39 +454,37 @@
         bent[depth].wait_recv()
         twins.append(out.go(at("D", depth), at("D", depth), peers["C"]))
 
-    blocks = {"gate": gates_ref, "up": ups_ref, "down": downs_ref}
+    blocks = {"gate": gates_ref, "up": ups_ref}
     flats, arrivals = {}, []
 
     def spread(name):
-        block = blocks[name]
-        source = down_ref if name == "down" else block.at[spot["O"]]
-        flats[name] = out.go(source, block.at[spot["O"]], peers["H"])
-        arrivals.append(out.go(source, block.at[spot["O"]], peers["Y"]))
+        mine = blocks[name].at[spot["O"]]
+        flats[name] = out.go(mine, mine, peers["H"])
+        arrivals.append(out.go(mine, mine, peers["Y"]))
 
     def corner(name):
         flats[name].wait_recv()
         piece = blocks[name].at[spot["H"]]
         arrivals.append(out.go(piece, piece, peers["Y"]))
 
-    spread("down")
     begin("O")
     for swap in swaps:
         swap.wait_recv()
+    keeps[1].wait()
     keeps[2].wait()
-    keeps[3].wait()
     spread("gate")
     to_h.wait_recv()
     to_hl = out.go(at("O", "H"), at("O", "H"), peers["L"])
     to_l.wait_recv()
     begin("L")
     begin("H")
-    corner("down")
     bend("O")
     spread("up")
     to_hl.wait_recv()
     begin("HL")
     bend("L")
     corner("gate")
+    arrivals.append(out.go(down_ref, far_ref, peers["H"]))
     bend("H")
     close("O")
     close("L")
@@ -389,40 +496,39 @@
         copy.wait_recv()
     out.finish()
     keeps[0].wait()
-    keeps[1].wait()
-
-
-def weights_in(columns, gate_blocks, up_blocks, down):
+
+
+def weights_in(columns, gate, up, down):
     rows, width = columns.shape
-    ranks, depth, part = gate_blocks.shape
-    if lax.axis_size("y") != 2 or lax.axis_size("h") != 2:
+    ranks, depth, part = 8, gate.shape[0], gate.shape[1] // 8
+    if not small_grid():
         full = lax.all_gather(columns, AXES, axis=0, tiled=False)
         gates, ups = (
             lax.all_gather(lax.all_to_all(b, TEAM, 0, 0), COPIES, axis=0, tiled=False)
-            for b in (gate_blocks, up_blocks)
+            for b in (column_blocks(gate), column_blocks(up))
         )
-        downs = lax.all_gather(down, COPIES, axis=0, tiled=False)
+        far = None
     else:
-        full, gates, ups, downs = remote_call(
+        full, gates, ups, far = remote_call(
             weights_in_kernel,
             (
                 jax.ShapeDtypeStruct((32, rows, width), BF16),
                 jax.ShapeDtypeStruct((4, ranks, depth, part), BF16),
                 jax.ShapeDtypeStruct((4, ranks, depth, part), BF16),
-                jax.ShapeDtypeStruct((4, *down.shape), BF16),
+                jax.ShapeDtypeStruct(down.shape, BF16),
             ),
-            14 + 3 + 28 + 9,
+            14 + 3 + 28 + 7,
             3,
-            [pltpu.SemaphoreType.DMA((4,))],
+            [
+                pltpu.SemaphoreType.DMA((3,)),
+                pltpu.SemaphoreType.DMA((64,)),
+                pltpu.VMEM((ranks, depth, part), BF16),
+                pltpu.VMEM((ranks, depth, part), BF16),
+            ],
             spaces=[pl.ANY] * 4,
             inputs=4,
-        )(columns, gate_blocks, up_blocks, down)
-    return (
-        full.reshape(-1, width),
-        gates.reshape(-1, part),
-        ups.reshape(-1, part),
-        downs.reshape(-1, down.shape[1]),
-    )
+        )(columns, gate, up, down)
+    return full.reshape(-1, width), gates.reshape(-1, part), ups.reshape(-1, part), far
 
 
 PLANES = ("D", "X", "Y", "O")
@@ -431,13 +537,16 @@
 
 def grads_out_kernel(edges, *refs):
     n = len(edges)
-    parts, sums = refs[:n], refs[n : n + 3]
-    o_ref, gate_ref, up_ref, down_ref, send, recv, local = refs[n + 3 : n + 10]
-    mine, twin_in, cross_in, lane_in, bent_in, depth_in = refs[n + 10 : n + 16]
-    flat, flat_y, flat_h = refs[n + 16 : n + 19], refs[n + 19 : n + 22], refs[n + 22 : n + 25]
+    parts, (far_ref, near_ref, raw_ref) = refs[:n], refs[n : n + 3]
+    o_ref, gate_ref, up_ref, send, recv, local = refs[n + 3 : n + 9]
+    mine, twin_in, cross_in, lane_in, bent_in, depth_in = refs[n + 9 : n + 15]
+    flat, flat_h, back_in = refs[n + 15 : n + 17], refs[n + 17 : n + 19], refs[n + 19 : n + 21]
+    flat_far, flat_y = refs[n + 21], refs[n + 22 :]
     rank, peers = full_places()
     me, team = team_peers()
     spot = copy_places()
+    half = mine.shape[2] // 2
+    top, low = pl.ds(0, half), pl.ds(half, half)
     loads, swaps, flights = {}, {}, {}
     count = 0
 
@@ -455,10 +564,8 @@
                 load(part.at[place], mine.at[t, k, :, pl.ds(begin, part.shape[2])])
                 for part, begin in zip(parts, edges)
             ]
-    own_loads = [
-        [load(total.at[spot[k]], buffer.at[j]) for j, k in enumerate("HO")]
-        for total, buffer in zip(sums, flat)
-    ]
+    own_loads = [load(near_ref, flat[0]), load(raw_ref.at[spot["O"]], flat[1])]
+    far_load = load(raw_ref.at[spot["H"]], flat_far)
     greet([peer for _, peer in team] + [peers["Y"], peers["H"]])
     out = Sender(send, recv)
 
@@ -477,144 +584,160 @@
             copy.wait()
         for copy in swaps[t, k]:
             copy.wait_recv()
-        mine[t, k] = plus(mine[t, k], twin_in[t, k]).astype(BF16)
-
-    def begin(t):
-        join(t, 0)
-        to_bend = out.go(mine.at[t, 0], bent_in.at[t], peers["X"])
-        join(t, 1)
-        to_x = out.go(mine.at[t, 1], cross_in.at[t], peers["X"])
-        join(t, 2)
-        join(t, 3)
-        flights[t] = [to_bend, to_x]
+        add_into(mine.at[t, k], twin_in.at[t, k])
+
+    def diagonal(t):
+        flights[t] = [
+            out.go(mine.at[t, 0, top], bent_in.at[t, top], peers["X"]),
+            out.go(mine.at[t, 0, low], bent_in.at[t, low], peers["Y"]),
+        ]
+
+    def straight(t):
+        flights[t].append(out.go(mine.at[t, 1, top], cross_in.at[t, top], peers["X"]))
+        flights[t].append(out.go(mine.at[t, 2, low], lane_in.at[t, low], peers["Y"]))
 
     def bend(t):
-        to_bend, to_x = flights[t]
-        to_bend.wait_recv()
-        mine[t, 2] = plus(mine[t, 2], bent_in[t]).astype(BF16)
-        flights[t] = [to_x, out.go(mine.at[t, 2], lane_in.at[t], peers["Y"])]
+        flights[t][0].wait_recv()
+        add_into(mine.at[t, 2, top], bent_in.at[t, top])
+        flights[t].append(out.go(mine.at[t, 2, top], lane_in.at[t, top], peers["Y"]))
+        flights[t][1].wait_recv()
+        add_into(mine.at[t, 1, low], bent_in.at[t, low])
+        flights[t].append(out.go(mine.at[t, 1, low], cross_in.at[t, low], peers["X"]))
 
     def close(t):
-        for copy in flights[t]:
+        for copy in flights[t][2:]:
             copy.wait_recv()
-        return plus(mine[t, 3], cross_in[t], lane_in[t])
-
-    y_side, h_side = {}, {}
-
-    def lane(i, j):
-        y_side[i, j] = out.go(sums[i].at[spot["DY"[j]]], flat_y[i].at[j], peers["Y"])
-
-    def along(i):
-        own_loads[i][0].wait()
-        y_side[i, 0].wait_recv()
-        flat[i][0] = plus(flat[i][0], flat_y[i][0]).astype(BF16)
-        h_side[i] = out.go(flat[i].at[0], flat_h[i], peers["H"])
+        return (cross_in.at[t], lane_in.at[t])
 
     swap(0)
-    lane(2, 0)
+    h_side = [out.go(far_ref, flat_h[0], peers["H"])]
+    y_side = [out.go(raw_ref.at[spot["D"]], flat_y[0], peers["Y"])]
     swap(1)
     swap(2)
     swap(3)
-    begin(0)
-    begin(1)
-    along(2)
-    lane(0, 0)
+    for t in (0, 1):
+        for k in (0, 1, 2):
+            join(t, k)
+        diagonal(t)
+        straight(t)
+    join(0, 3)
+    join(1, 3)
+    far_load.wait()
+    y_side[0].wait_recv()
+    add_into(flat_far, flat_y[0])
+    h_side.append(out.go(flat_far, flat_h[1], peers["H"]))
+    y_side.append(out.go(raw_ref.at[spot["Y"]], flat_y[1], peers["Y"]))
     bend(0)
-    begin(2)
-    begin(3)
-    along(0)
-    lane(1, 0)
+    for k in (0, 1, 2):
+        join(2, k)
+    diagonal(2)
+    straight(2)
     bend(1)
-    mine[0, 3] = close(0).astype(BF16)
+    for k in (0, 1, 2):
+        join(3, k)
+    diagonal(3)
+    straight(3)
+    join(2, 3)
+    join(3, 3)
+    add_into(mine.at[0, 3], *close(0))
     to_hl = out.go(mine.at[0, 3], depth_in.at[0], peers["L"])
-    along(1)
-    lane(0, 1)
-    lane(1, 1)
     bend(2)
-    mine[1, 3] = close(1).astype(BF16)
+    add_into(mine.at[1, 3], *close(1))
     to_l = out.go(mine.at[1, 3], depth_in.at[1], peers["L"])
-    lane(2, 1)
     bend(3)
-    total = close(2)
+    ready = close(2)
     to_hl.wait_recv()
-    mine[2, 3] = plus(total, depth_in[0]).astype(BF16)
+    add_into(mine.at[2, 3], *ready, depth_in.at[0])
     to_h = out.go(mine.at[2, 3], depth_in.at[2], peers["H"])
     returns = []
+    for i in range(2):
+        own_loads[i].wait()
+        h_side[i].wait_recv()
+        arrived = [flat_h[i]]
+        if i == 1:
+            y_side[1].wait_recv()
+            arrived.append(flat_y[1])
+        add_into(flat[i], *arrived)
+        returns.append([load(flat[i].at[me], back_in[i].at[me])])
+        for place, peer in team:
+            returns[i].append(out.go(flat[i].at[place], back_in[i].at[me], peer))
+    ready = close(3)
+    to_l.wait_recv()
+    add_to(o_ref, mine.at[3, 3], *ready, depth_in.at[1])
+    to_h.wait_recv()
+    add_into(o_ref, depth_in.at[2])
     for i, target in enumerate((gate_ref, up_ref)):
-        own_loads[i][1].wait()
-        y_side[i, 1].wait_recv()
-        h_side[i].wait_recv()
-        flat[i][1] = plus(flat[i][1], flat_y[i][1], flat_h[i][...]).astype(BF16)
-        keep = load(flat[i].at[1, me], target.at[me])
-        returns.append(keep)
-        for place, peer in team:
-            returns.append(out.go(flat[i].at[1, place], target.at[me], peer))
-    total = close(3)
-    to_l.wait_recv()
-    total = plus(total, depth_in[1])
-    to_h.wait_recv()
-    o_ref[...] = plus(total, depth_in[2])
-    own_loads[2][1].wait()
-    y_side[2, 1].wait_recv()
-    h_side[2].wait_recv()
-    down_ref[...] = plus(flat[2][1], flat_y[2][1], flat_h[2][...])
-    for i, copy in enumerate(returns):
-        if i % 8 == 0:
-            copy.wait()
-        else:
+        returns[i][0].wait()
+        for copy in returns[i][1:]:
             copy.wait_recv()
+        width = target.shape[1] // 32
+        for r in range(8):
+            for c in range(4):
+                begin = ((c // 2 * 4 + r // 2) * 2 + c % 2) * 2 + r % 2
+                target[:, pl.ds(begin * width, width)] = back_in[i][
+                    r, :, pl.ds(c * width, width)
+                ].astype(F32)
     out.finish()
 
 
-def grads_out(parts, gate, up, down):
-    ys, hs = lax.axis_size("y"), lax.axis_size("h")
-    shares = ys * hs * 8
+def grads_out(parts, gate, up):
+    shares = lax.axis_size("y") * lax.axis_size("h") * 8
     rows = parts[0].shape[0] // shares
     blocks = [part.reshape(shares, rows, part.shape[1]) for part in parts]
-    sums = [
-        gate.reshape(ys * hs, 8, -1, gate.shape[1]),
-        up.reshape(ys * hs, 8, -1, up.shape[1]),
-        down.reshape(ys * hs, -1, down.shape[1]),
-    ]
-    if ys != 2 or hs != 2:
+    if not small_grid():
         block = jnp.concatenate(blocks, axis=2)
         total = lax.psum_scatter(block, AXES, scatter_dimension=0, tiled=False).astype(F32)
-        gate, up, down = (
-            lax.psum_scatter(value, COPIES, scatter_dimension=0, tiled=False) for value in sums
+        up = lax.psum_scatter(up, COPIES, scatter_dimension=0, tiled=False)
+        gate, up = (
+            from_column_blocks(lax.all_to_all(value, TEAM, 0, 0)).astype(F32)
+            for value in (gate, up)
         )
-        gate, up = (lax.all_to_all(value, TEAM, 0, 0) for value in (gate, up))
-        return total, gate, up, down.astype(F32)
+        return total, gate, up
     edges = [0]
     for part in parts:
         edges.append(edges[-1] + part.shape[1])
     width = edges.pop()
-    flats = [pltpu.VMEM((2, *value.shape[1:]), BF16) for value in sums]
+    flat = gate[0].shape
     return remote_call(
         partial(grads_out_kernel, tuple(edges)),
         (
             jax.ShapeDtypeStruct((rows, width), F32),
-            jax.ShapeDtypeStruct(sums[0].shape[1:], BF16),
-            jax.ShapeDtypeStruct(sums[1].shape[1:], BF16),
-            jax.ShapeDtypeStruct(sums[2].shape[1:], F32),
+            jax.ShapeDtypeStruct((flat[1], 8 * flat[2]), F32),
+            jax.ShapeDtypeStruct((flat[1], 8 * flat[2]), F32),
         ),
-        16 * len(parts) + 12 + 3 + 6 + 3 + 14,
+        16 * len(parts) + 24 + 3 + 4 + 14,
         4,
         [
-            pltpu.SemaphoreType.DMA((16 * len(parts) + 6 + 2,)),
+            pltpu.SemaphoreType.DMA((16 * len(parts) + 3 + 2,)),
             pltpu.VMEM((4, 4, rows, width), BF16),
             pltpu.VMEM((4, 4, rows, width), BF16),
             pltpu.VMEM((4, rows, width), BF16),
             pltpu.VMEM((4, rows, width), BF16),
             pltpu.VMEM((4, rows, width), BF16),
             pltpu.VMEM((3, rows, width), BF16),
-            *flats,
-            *flats,
-            *[pltpu.VMEM(value.shape[1:], BF16) for value in sums],
+            *[pltpu.VMEM(flat, BF16)] * 9,
         ],
-        60 * 2**20,
-        [pltpu.VMEM, pl.ANY, pl.ANY, pltpu.VMEM],
+        56 * 2**20,
+        [pltpu.VMEM] * 3,
         len(parts) + 3,
-    )(*blocks, *sums)
+    )(*blocks, *gate, up)
+
+
+def small_grid():
+    return lax.axis_size("y") == 2 and lax.axis_size("h") == 2
+
+
+def lane_sums(value):
+    if not small_grid():
+        return lax.psum_scatter(value, COPIES, scatter_dimension=0, tiled=False)
+    spot = copy_places()
+
+    def piece(k):
+        return lax.dynamic_index_in_dim(value, spot[k], axis=0, keepdims=False)
+
+    sent = jnp.stack([piece("D"), piece("Y")])
+    arrived = lax.ppermute(sent, "y", [(0, 1), (1, 0)])
+    return [plus(piece(k), arrived[j]).astype(BF16) for j, k in enumerate("HO")]
 
 
 def shift(block, distance):
@@ -703,8 +826,8 @@
     local_columns = jnp.pad(
         jnp.concatenate(columns, axis=1), ((0, 0), (0, full_width - edges[-1]))
     )
-    full, gate_cols, up_cols, down_rows = weights_in(
-        local_columns, column_blocks(gate_weight), column_blocks(up_weight), down_weight
+    full, gate_cols, up_cols, far_down = weights_in(
+        local_columns, gate_weight, up_weight, down_weight
     )
     first = full[:, : edges[3]]
     output_all, side_gate_all, projection_all, left_all, right_all = (
@@ -766,7 +889,7 @@
     merged_inv = inverse_rms(merged)
     expand_low = (merged * merged_inv * gains[3]).astype(BF16)
 
-    expand_all = team_gather(depth_order(expand_low))
+    expand_all, down_rows = team_gather_with(depth_order(expand_low), down_weight, far_down)
     gate_raw = dot(expand_all, gate_cols)
     up_raw = dot(expand_all, up_cols)
     act_low = (gelu(gate_raw) * up_raw).astype(BF16)
@@ -798,7 +921,19 @@
     part_low = (dot(grad_gate_low, gate_cols, 1, 1) + dot(grad_up_low, up_cols, 1, 1)).astype(BF16)
     part_gate = dot(expand_all, grad_gate_low, 0, 0).astype(BF16)
     part_up = dot(expand_all, grad_up_low, 0, 0).astype(BF16)
-    part = from_depth_order(team_scatter(part_low))
+    down_blocks = part_down.reshape(-1, *down_weight.shape)
+    part_gate, part_up = (
+        value.reshape(-1, 8, depth, value.shape[1]) for value in (part_gate, part_up)
+    )
+    part_low, part_gate, part_up = lax.optimization_barrier((part_low, part_gate, part_up))
+    if small_grid():
+        part, down_sums = team_scatter(part_low, down_blocks)
+        grad_down = plus(down_sums[1], lax.ppermute(down_sums[0], "h", [(0, 1), (1, 0)]))
+    else:
+        part = team_scatter(part_low)
+        grad_down = lax.psum_scatter(down_blocks, COPIES, scatter_dimension=0).astype(F32)
+    sums_gate = lane_sums(part_gate)
+    part = from_depth_order(part)
     grad_merged, gain_three = rms_back(merged, merged_inv, gains[3], part)
     grad_sum = (grad_after + grad_merged) * HALF_ROOT
     grad_right, gain_two = rms_back(right_raw, right_inv, gains[2], grad_sum)
@@ -873,9 +1008,7 @@
         dot(grad_side_low, side_low, 0, 0).astype(BF16),
         small.astype(BF16),
     )
-    summed, back_gate, back_up, grad_down = grads_out(weight_grads, part_gate, part_up, part_down)
-    grad_gate = from_column_blocks(back_gate).astype(F32)
-    grad_up = from_column_blocks(back_up).astype(F32)
+    summed, grad_gate, grad_up = grads_out(weight_grads, sums_gate, part_up)
     (
         d_query,
         d_key,

time: 1040 us -> 981 us (0.943)
  Pallas kernels: 633 us -> 581 us
  local copies, waits for them, and re-layouts: 119 us -> 96.6 us
  waiting for transfers between devices: 2.39 us -> 14.8 us
    pallas_call x1, Pallas kernels: 247 us -> 202 us  [weights_in(): remote_call(weights_in_kernel, (jax.ShapeDtypeStruct((32, rows, width), B...]
    pallas_call x1, Pallas kernels: 227 us -> 200 us  [grads_out(): remote_call(partial(grads_out_kernel, tuple(edges)), (jax.ShapeDtypeStruc...]
    convert_element_type x6 -> x0, local copies, waits for them, and re-layouts: 25.2 us -> none  [the longest x3 12.7 us: layer(): grad_gate = from_column_blocks(back_gate).astype(F32)]
    pallas_call x4, Pallas kernels: 159 us -> 178 us  [the longest x1 50 us: team_gather_with(): remote_call(partial(team_gather_kernel, True), (jax.ShapeDtypeStruct((8,...]
    ppermute x0 -> x2, waiting for transfers between devices: none -> 14.8 us  [the longest x1 14.8 us: layer(): lax.ppermute(down_sums[0], 'h', [(0, 1), (1, 0)])]
    unnamed x282 -> x297, local copies, waits for them, and re-layouts: 36.5 us -> 42.2 us
  transfers between devices with their start and end apart: 4 -> 6, of which waited for: 1 -> 1; matrix products, arithmetic and copies ran while one was open for 5% -> 9% of each run, Pallas kernels for 0% -> 0%
where the time goes in v4:
time: 981 us; the launch traced here: 974 us
  Pallas kernels  581 us (59%)
  matrix products  207 us (21%)
  local copies, waits for them, and re-layouts  96.6 us (10%)
  other arithmetic  54.3 us (6%)
  starting transfers between devices  17.3 us (2%)
  waiting for transfers between devices  14.8 us (2%)
    pallas_call x1, Pallas kernels, weights_in(): remote_call(weights_in_kernel, (jax.ShapeDtypeStruct((32, rows, width), B...  202 us
    pallas_call x1, Pallas kernels, grads_out(): remote_call(partial(grads_out_kernel, tuple(edges)), (jax.ShapeDtypeStruc...  200 us
    dot_general x27, matrix products, dot(): lax.dot_general(left, right, (((left_dim,), (right_dim,)), ((), ())), pre...  197 us
    pallas_call x1, Pallas kernels, team_gather_with(): remote_call(partial(team_gather_kernel, True), (jax.ShapeDtypeStruct((8,...  50 us
    pallas_call x1, Pallas kernels, team_scatter(): remote_call(partial(team_scatter_kernel, True), (total, jax.ShapeDtypeStr...  48 us
    unnamed x297, local copies, waits for them, and re-layouts  42.2 us
    pallas_call x1, Pallas kernels, team_scatter(): remote_call(partial(team_scatter_kernel, False), total, 10, 1, [pltpu.Sem...  40.9 us
    pallas_call x1, Pallas kernels, team_gather(): remote_call(partial(team_gather_kernel, False), jax.ShapeDtypeStruct((8,...  39.4 us
  transfers between devices with their start and end apart: 6, of which 1 were waited for; matrix products, arithmetic and copies ran while one was open for 9% of the time, Pallas kernels for 0%

profile of v4, /device:TPU:1, one launch (start us, length us, event | category | flops | bytes accessed | tf_op | source)
XLA Modules:
  0.0 973.6 jit_solution(10034618419911984103)
XLA Ops:
  5.2 202.2 %shard_map.280 = (bf16[32,64,5888]{2,1,0:T(8,128)(2,1)}, bf16[4,8,64,1024]{3,2,1,0:T(8,128)(2,1)}, bf16[4,8,64,1024]{3,2,1,0:T(8,128)(2,1)}, bf16[256,2048]{1,0:T(8,128)(2,1)}) custom-call(bf16[64,5888]{1,0:T(8,128)(2,1)} %pad.29.x_ref, bf16[64,8192]{1,0:T(8,128)(2,1)} %gate_in.1, bf16[64,8192]{1,0:T(8,128)(2,1)} %up_in.1, bf16[256,2048]{1,0:T(8,128)(2,1)} %refs_1_.1), custom_call_target="tpu_custom_call" | custom-call | tf_op jit(solution)/shard_map/pallas_call | solution.py:512
  210.3 6.6 fusion.3
  219.4 2.0 slice.214
  230.6 4.8 collective-permute-start.1
  235.4 4.5 collective-permute-start
  239.9 2.2 convolution_convert_fusion.9
  245.8 2.5 copy.379
  266.4 2.3 copy.380
  274.5 2.9 fusion.121
  280.1 6.2 multiply_reduce_fusion.16
  293.7 50.0 %shard_map.281 = (bf16[8,256,2048]{2,1,0:T(8,128)(2,1)}, bf16[4,256,2048]{2,1,0:T(8,128)(2,1)S(1)}) custom-call(bf16[256,2048]{1,0:T(8,128)(2,1)S(1)} %reshape.455.refs_0_, bf16[256,2048]{1,0:T(8,128)(2,1)S(1)} %copy-done.1, bf16[256,2048]{1,0:T(8,128)(2,1)S(1)} %copy-done.4), custom_call_target="tpu_custom_call" | custom-call | tf_op jit(solution)/shard_map/pallas_call | solution.py:232
  343.7 16.0 %fusion.122 = f32[2048,1024]{1,0:T(8,128)} fusion(bf16[2048,2048]{1,0:T(8,128)(2,1)} %bitcast.328, bf16[2048,1024]{1,0:T(8,128)(2,1)} %bitcast.336), kind=kOutput, calls=%fused_computation.242 | convolution fusion | flops 8589934592 | bytes 20971520 | tf_op jit(solution)/shard_map/dot_general | solution.py:25
  359.7 14.4 %multiply_convert_fusion.1 = (bf16[2048,1024]{1,0:T(8,128)(2,1)}, f32[2048,1024]{1,0:T(8,128)}) fusion(f32[2048,1024]{1,0:T(8,128)} %fusion.122, bf16[2048,2048]{1,0:T(8,128)(2,1)S(1)} %bitcast.330, bf16[2048,1024]{1,0:T(8,128)(2,1)S(1)} %bitcast.334), kind=kOutput, calls=%fused_computation.18 | convolution fusion | flops 8610906112 | bytes 33554432 | tf_op jit(solution)/shard_map/dot_general | solution.py:25
  374.1 10.6 %convolution_convert_fusion.2 = bf16[2048,2048]{1,0:T(8,128)(2,1)S(1)} fusion(bf16[2048,1024]{1,0:T(8,128)(2,1)} %get-tuple-element.242, bf16[1024,2048]{1,0:T(8,128)(2,1)S(1)} %bitcast.222), kind=kOutput, calls=%fused_computation.21 | convolution fusion | flops 8594128896 | bytes 16777216 | tf_op jit(solution)/shard_map/dot_general | solution.py:25
  384.7 40.9 %shard_map.282 = f32[256,2048]{1,0:T(8,128)S(1)} custom-call(bf16[8,256,2048]{2,1,0:T(8,128)(2,1)S(1)} %bitcast.217), custom_call_target="tpu_custom_call" | custom-call | tf_op jit(solution)/shard_map/pallas_call | solution.py:324
  427.6 2.4 fusion.67
  433.3 2.1 multiply_convert_fusion.6
  435.4 2.1 fusion.57
  437.5 2.8 multiply_reduce_fusion.2
  442.2 39.4 %shard_map.283 = bf16[8,256,2048]{2,1,0:T(8,128)(2,1)S(1)} custom-call(bf16[256,2048]{1,0:T(8,128)(2,1)S(1)} %multiply_convert_fusion.5.refs_0_), custom_call_target="tpu_custom_call" | custom-call | tf_op jit(solution)/shard_map/pallas_call | solution.py:216
  481.5 3.2 copy-done
  484.8 24.7 %multiply_convert_fusion = (bf16[2048,1024]{1,0:T(8,128)(2,1)}, bf16[2048,1024]{1,0:T(8,128)(2,1)}) fusion(f32[2048,1024]{1,0:T(8,128)} %fusion.122, f32[2048,1024]{1,0:T(8,128)} %get-tuple-element.243, bf16[2048,2048]{1,0:T(8,128)(2,1)} %bitcast.218, bf16[1024,2048]{1,0:T(8,128)(2,1)} %bitcast.223), kind=kOutput, calls=%fused_computation.17 | convolution fusion | flops 8638169088 | bytes 37748736 | tf_op jit(solution)/shard_map/dot_general | solution.py:25
  509.5 15.6 %fusion.123 = f32[2048,2048]{1,0:T(8,128)} fusion(bf16[2048,1024]{1,0:T(8,128)(2,1)} %get-tuple-element.181, bf16[2048,1024]{1,0:T(8,128)(2,1)} %bitcast.337), kind=kOutput, calls=%fused_computation.243 | convolution fusion | flops 8589934592 | bytes 25165824 | tf_op jit(solution)/shard_map/dot_general | solution.py:25
  525.1 13.1 %convolution_convert_fusion.5 = bf16[2048,1024]{1,0:T(8,128)(2,1)} fusion(bf16[2048,2048]{1,0:T(8,128)(2,1)} %bitcast.329, bf16[2048,1024]{1,0:T(8,128)(2,1)S(1)} %copy-done.128), kind=kOutput, calls=%fused_computation.36 | convolution fusion | flops 8592031744 | bytes 16777216 | tf_op jit(solution)/shard_map/dot_general | solution.py:25
  538.2 10.8 %convolution_convert_fusion.3 = bf16[1024,2048]{1,0:T(8,128)(2,1)} fusion(bf16[2048,1024]{1,0:T(8,128)(2,1)S(1)} %copy-done.125, bf16[2048,2048]{1,0:T(8,128)(2,1)S(1)} %bitcast.221), kind=kOutput, calls=%fused_computation.34 | convolution fusion | flops 8592031744 | bytes 16777216 | tf_op jit(solution)/shard_map/dot_general | solution.py:25
  549.1 10.8 %convolution_convert_fusion.4 = bf16[2048,1024]{1,0:T(8,128)(2,1)} fusion(bf16[2048,2048]{1,0:T(8,128)(2,1)S(1)} %bitcast.333, bf16[2048,1024]{1,0:T(8,128)(2,1)S(1)} %copy-done.126), kind=kOutput, calls=%fused_computation.35 | convolution fusion | flops 8592031744 | bytes 16777216 | tf_op jit(solution)/shard_map/dot_general | solution.py:25
  559.8 14.1 %add_convert_fusion = bf16[2048,2048]{1,0:T(8,128)(2,1)} fusion(f32[2048,2048]{1,0:T(8,128)} %fusion.123, bf16[2048,1024]{1,0:T(8,128)(2,1)S(1)} %copy-done.127, bf16[2048,1024]{1,0:T(8,128)(2,1)S(1)} %bitcast.335), kind=kOutput, calls=%fused_computation.1 | convolution fusion | flops 8598323200 | bytes 33554432 | tf_op jit(solution)/shard_map/dot_general | solution.py:25
  573.9 48.0 %shard_map.284 = (f32[256,2048]{1,0:T(8,128)S(1)}, bf16[2,256,2048]{2,1,0:T(8,128)(2,1)S(1)}) custom-call(bf16[8,256,2048]{2,1,0:T(8,128)(2,1)} %bitcast.231, bf16[4,256,2048]{2,1,0:T(8,128)(2,1)} %bitcast.243), custom_call_target="tpu_custom_call" | custom-call | tf_op jit(solution)/shard_map/pallas_call | solution.py:334
  623.2 2.5 reshape.466
  625.7 4.0 copy.322
  629.7 4.5 reshape.467
  634.3 2.9 multiply_reduce_fusion.3
  637.3 4.8 multiply_reduce_fusion.4
  645.0 6.9 fusion.33
  653.4 4.2 fusion.17
  687.9 4.4 collective-permute-start.5
  692.4 7.3 convolution_convert_fusion.1
  707.9 2.6 multiply_reduce_fusion.18
  711.2 6.8 fusion.29
  718.1 2.6 fusion.42
  720.7 2.1 fusion.41
  726.2 4.3 fusion.32
  730.5 6.9 convolution_convert_fusion
  737.4 14.8 %collective-permute-done.5 = bf16[256,2048]{1,0:T(8,128)(2,1)} collective-permute-done((bf16[256,2048]{1,0:T(8,128)(2,1)}, bf16[256,2048]{1,0:T(8,128)(2,1)}, u32[]{:S(2)}, u32[]{:S(2)}) %collective-permute-start.5) | collective-permute-done | bytes 1048608 | tf_op jit(solution)/shard_map/ppermute | solution.py:931
  752.2 2.9 convert_add_fusion.1
  755.1 3.9 fusion.59
  758.9 200.1 %shard_map.285 = (f32[64,5888]{1,0:T(8,128)}, f32[64,8192]{1,0:T(8,128)}, f32[64,8192]{1,0:T(8,128)}) custom-call(bf16[32,64,3072]{2,1,0:T(8,128)(2,1)} %bitcast.224, bf16[32,64,2048]{2,1,0:T(8,128)(2,1)} %bitcast.225, bf16[32,64,256]{2,1,0:T(8,128)(2,1)} %bitcast.250, bf16[32,64,256]{2,1,0:T(8,128)(2,1)} %bitcast.285, bf16[32,64,256]{2,1,0:T(8,128)(2,1)} %bitcast.251, ...), custom_call_target="tpu_custom_call" | custom-call | tf_op jit(solution)/shard_map/pallas_call | solution.py:701
  959.1 2.4 fusion.117
  (425 shorter events, 122.3 us)
Async XLA Ops:
  5.2 204.2 %copy-start.9 = (bf16[256,2048]{1,0:T(8,128)(2,1)S(1)}, bf16[256,2048]{1,0:T(8,128)(2,1)}, u32[]{:S(2)}) copy-start(bf16[256,2048]{1,0:T(8,128)(2,1)} %param.17) | copy-start | bytes 3145732
  209.4 77.5 %copy-start.71 = (f32[1,2048]{1,0:T(1,128)}, f32[1,2048]{1,0:T(1,128)S(1)}, u32[]{:S(2)}) copy-start(f32[1,2048]{1,0:T(1,128)S(1)} %get-tuple-element.228) | copy-start | bytes 24580
  218.7 6.4 copy-start.29
  218.7 10.1 %copy-start.31 = (f32[256,512]{1,0:T(8,128)}, f32[256,512]{1,0:T(8,128)S(1)}, u32[]{:S(2)}) copy-start(f32[256,512]{1,0:T(8,128)S(1)} %get-tuple-element.191) | copy-start | bytes 1572868
  225.6 5.0 copy-start.94
  226.1 13.8 %copy-start.87 = (f32[256]{0:T(256)S(1)}, f32[256]{0:T(256)}, u32[]{:S(2)}) copy-start(f32[256]{0:T(256)} %copy-done.86) | copy-start | bytes 3076
  228.8 13.3 %copy-start.61 = (f32[256,128]{1,0:T(8,128)}, f32[256,128]{1,0:T(8,128)S(1)}, u32[]{:S(2)}) copy-start(f32[256,128]{1,0:T(8,128)S(1)} %get-tuple-element.232) | copy-start | bytes 393220
  228.8 27.6 %copy-start.46 = (f32[256,128]{1,0:T(8,128)}, f32[256,128]{1,0:T(8,128)S(1)}, u32[]{:S(2)}) copy-start(f32[256,128]{1,0:T(8,128)S(1)} %get-tuple-element.233) | copy-start | bytes 393220
  229.6 12.5 %copy-start.25 = (f32[256,3072]{1,0:T(8,128)S(1)}, f32[256,3072]{1,0:T(8,128)}, u32[]{:S(2)}) copy-start(f32[256,3072]{1,0:T(8,128)} %copy-done.24) | copy-start | bytes 9437188
  229.7 13.9 %copy-start.57 = (bf16[1,256,2,128]{3,1,2,0:T(8,128)(2,1)}, bf16[1,256,2,128]{3,1,2,0:T(8,128)(2,1)S(1)}, u32[]{:S(2)}) copy-start(bf16[1,256,2,128]{3,1,2,0:T(8,128)(2,1)S(1)} %get-tuple-element.219) | copy-start | bytes 393220
  229.7 13.9 %copy-start.59 = (bf16[1,256,2,128]{3,1,2,0:T(8,128)(2,1)}, bf16[1,256,2,128]{3,1,2,0:T(8,128)(2,1)S(1)}, u32[]{:S(2)}) copy-start(bf16[1,256,2,128]{3,1,2,0:T(8,128)(2,1)S(1)} %get-tuple-element.220) | copy-start | bytes 393220
  230.6 40.8 %collective-permute-start.1 = (bf16[2,256,2,256]{3,1,2,0:T(8,128)(2,1)}, bf16[2,256,2,256]{3,1,2,0:T(8,128)(2,1)}, u32[]{:S(2)}, u32[]{:S(2)}) collective-permute-start(bf16[2,256,2,256]{3,1,2,0:T(8,128)(2,1)} %pad_maximum_fusion.9), channel_id=1, source_target_pairs={{0,1},{1,2},{2,3},{4,5},{5,6},{6,7},{8,9},{9,10},{10,11},{12,13},{... | collective-permute-start | bytes 1572872 | tf_op jit(solution)/shard_map/ppermute | solution.py:746
  235.4 36.0 %collective-permute-start = (bf16[2,256,2,256]{3,1,2,0:T(8,128)(2,1)}, bf16[2,256,2,256]{3,1,2,0:T(8,128)(2,1)}, u32[]{:S(2)}, u32[]{:S(2)}) collective-permute-start(bf16[2,256,2,256]{3,1,2,0:T(8,128)(2,1)} %pad_maximum_fusion.9), channel_id=1, source_target_pairs={{0,2},{1,3},{4,6},{5,7},{8,10},{9,11},{12,14},{13,15},{16,18},{17,... | collective-permute-start | bytes 1572872 | tf_op jit(solution)/shard_map/ppermute | solution.py:746
  248.3 8.1 copy-start.11
  257.8 6.5 copy-start.116
  261.8 11.7 %copy-start.48 = (bf16[256,8,128]{2,0,1:T(8,128)(2,1)}, bf16[256,8,128]{2,0,1:T(8,128)(2,1)S(1)}, u32[]{:S(2)}) copy-start(bf16[256,8,128]{2,0,1:T(8,128)(2,1)S(1)} %copy.318) | copy-start | bytes 1572868
  263.1 10.4 %copy-start.50 = (bf16[256,8,128]{2,0,1:T(8,128)(2,1)}, bf16[256,8,128]{2,0,1:T(8,128)(2,1)S(1)}, u32[]{:S(2)}) copy-start(bf16[256,8,128]{2,0,1:T(8,128)(2,1)S(1)} %copy.317) | copy-start | bytes 1572868
  271.3 15.0 %copy-start.109 = (f32[256]{0:T(256)}, f32[256]{0:T(256)S(1)}, u32[]{:S(2)}) copy-start(f32[256]{0:T(256)S(1)} %get-tuple-element.236) | copy-start | bytes 3076
  271.4 15.5 %copy-start.13 = (f32[256,2048]{1,0:T(8,128)}, f32[256,2048]{1,0:T(8,128)S(1)}, u32[]{:S(2)}) copy-start(f32[256,2048]{1,0:T(8,128)S(1)} %get-tuple-element.237) | copy-start | bytes 6291460
  280.1 6.2 copy-start.54
  280.1 6.8 copy-start.81
  280.1 6.8 copy-start.83
  280.1 6.8 copy-start.88
  343.7 30.4 %copy-start.5 = (bf16[4,256,2048]{2,1,0:T(8,128)(2,1)}, bf16[4,256,2048]{2,1,0:T(8,128)(2,1)S(1)}, u32[]{:S(2)}) copy-start(bf16[4,256,2048]{2,1,0:T(8,128)(2,1)S(1)} %get-tuple-element.34) | copy-start | bytes 12582916
  343.7 16.0 %copy-start.122 = (bf16[8,256,2048]{2,1,0:T(8,128)(2,1)S(1)}, bf16[8,256,2048]{2,1,0:T(8,128)(2,1)}, u32[]{:S(2)}) copy-start(bf16[8,256,2048]{2,1,0:T(8,128)(2,1)} %get-tuple-element.31) | copy-start | bytes 25165828
  343.7 16.0 %copy-start.123 = (bf16[4,8,64,1024]{3,2,1,0:T(8,128)(2,1)S(1)}, bf16[4,8,64,1024]{3,2,1,0:T(8,128)(2,1)}, u32[]{:S(2)}) copy-start(bf16[4,8,64,1024]{3,2,1,0:T(8,128)(2,1)} %get-tuple-element.33) | copy-start | bytes 12582916
  427.6 5.7 copy-start.15
  430.0 5.4 copy-start.67
  484.8 53.4 %slice-start = ((s8[8388608]{0:T(1024)(128)(4,1)}), s8[4194304]{0:T(1024)(128)(4,1)S(1)}, s32[]{:S(2)}) async-start(s8[8388608]{0:T(1024)(128)(4,1)} %bitcast.219), calls=%async_computation | async-start | bytes 8388608
  509.4 15.7 %copy-start.128 = (bf16[2048,1024]{1,0:T(8,128)(2,1)S(1)}, bf16[2048,1024]{1,0:T(8,128)(2,1)}, u32[]{:S(2)}) copy-start(bf16[2048,1024]{1,0:T(8,128)(2,1)} %get-tuple-element.181) | copy-start | bytes 12582916
  509.4 28.8 %slice-start.1 = ((s8[8388608]{0:T(1024)(128)(4,1)}), s8[4194304]{0:T(1024)(128)(4,1)S(1)}, s32[]{:S(2)}) async-start(s8[8388608]{0:T(1024)(128)(4,1)} %bitcast.219), calls=%async_computation.1 | async-start | bytes 8388608
  509.4 39.6 %slice-start.4 = ((s8[8388608]{0:T(1024)(128)(4,1)}), s8[4194304]{0:T(1024)(128)(4,1)S(1)}, s32[]{:S(2)}) async-start(s8[8388608]{0:T(1024)(128)(4,1)} %bitcast.331), calls=%async_computation.4 | async-start | bytes 8388608
  525.1 13.1 %copy-start.125 = (bf16[2048,1024]{1,0:T(8,128)(2,1)S(1)}, bf16[2048,1024]{1,0:T(8,128)(2,1)}, u32[]{:S(2)}) copy-start(bf16[2048,1024]{1,0:T(8,128)(2,1)} %get-tuple-element.242) | copy-start | bytes 12582916
  525.1 23.9 %slice-start.5 = ((s8[8388608]{0:T(1024)(128)(4,1)}), s8[4194304]{0:T(1024)(128)(4,1)S(1)}, s32[]{:S(2)}) async-start(s8[8388608]{0:T(1024)(128)(4,1)} %bitcast.331), calls=%async_computation.5 | async-start | bytes 8388608
  538.2 10.8 %copy-start.126 = (bf16[2048,1024]{1,0:T(8,128)(2,1)S(1)}, bf16[2048,1024]{1,0:T(8,128)(2,1)}, u32[]{:S(2)}) copy-start(bf16[2048,1024]{1,0:T(8,128)(2,1)} %get-tuple-element.180) | copy-start | bytes 12582916
  549.0 10.8 %copy-start.124 = (bf16[4,8,64,1024]{3,2,1,0:T(8,128)(2,1)S(1)}, bf16[4,8,64,1024]{3,2,1,0:T(8,128)(2,1)}, u32[]{:S(2)}) copy-start(bf16[4,8,64,1024]{3,2,1,0:T(8,128)(2,1)} %get-tuple-element.33) | copy-start | bytes 12582916
  549.0 10.8 %copy-start.127 = (bf16[2048,1024]{1,0:T(8,128)(2,1)S(1)}, bf16[2048,1024]{1,0:T(8,128)(2,1)}, u32[]{:S(2)}) copy-start(bf16[2048,1024]{1,0:T(8,128)(2,1)} %get-tuple-element.180) | copy-start | bytes 12582916
  645.0 12.6 %slice-start.2 = ((s8[6291456]{0:T(1024)(128)(4,1)}), s8[2097152]{0:T(1024)(128)(4,1)S(1)}, s32[]{:S(2)}) async-start(s8[6291456]{0:T(1024)(128)(4,1)} %bitcast.228), calls=%async_computation.2 | async-start | bytes 4194304
  658.6 8.4 copy-start.36
  661.8 5.3 copy-start.38
  668.4 31.3 %collective-permute-start.3 = (bf16[2,256,2,256]{3,1,2,0:T(8,128)(2,1)}, bf16[2,256,2,256]{3,1,2,0:T(8,128)(2,1)}, u32[]{:S(2)}, u32[]{:S(2)}) collective-permute-start(bf16[2,256,2,256]{3,1,2,0:T(8,128)(2,1)} %get-tuple-element.206), channel_id=1, source_target_pairs={{2,0},{3,1},{6,4},{7,5},{10,8},{11,9},{14,12},{15,13},{18,16},{19,... | collective-permute-start | bytes 1572872 | tf_op jit(solution)/shard_map/ppermute | solution.py:746
  669.6 30.0 %collective-permute-start.2 = (bf16[2,256,2,256]{3,1,2,0:T(8,128)(2,1)}, bf16[2,256,2,256]{3,1,2,0:T(8,128)(2,1)}, u32[]{:S(2)}, u32[]{:S(2)}) collective-permute-start(bf16[2,256,2,256]{3,1,2,0:T(8,128)(2,1)} %get-tuple-element.205), channel_id=1, source_target_pairs={{1,0},{2,1},{3,2},{5,4},{6,5},{7,6},{9,8},{10,9},{11,10},{13,12},{... | collective-permute-start | bytes 1572872 | tf_op jit(solution)/shard_map/ppermute | solution.py:746
  686.0 69.1 %collective-permute-start.4 = (bf16[2,8,64,1024]{3,2,1,0:T(8,128)(2,1)}, bf16[2,8,64,1024]{3,2,1,0:T(8,128)(2,1)}, u32[]{:S(2)}, u32[]{:S(2)}) collective-permute-start(bf16[2,8,64,1024]{3,2,1,0:T(8,128)(2,1)} %pad_maximum_fusion.2), channel_id=1, source_target_pairs={{0,16},{16,0},{1,17},{17,1},{2,18},{18,2},{3,19},{19,3},{4,20},{20... | collective-permute-start | bytes 6291464 | tf_op jit(solution)/shard_map/ppermute | solution.py:739
  687.9 64.3 %collective-permute-start.5 = (bf16[256,2048]{1,0:T(8,128)(2,1)}, bf16[256,2048]{1,0:T(8,128)(2,1)}, u32[]{:S(2)}, u32[]{:S(2)}) collective-permute-start(bf16[256,2048]{1,0:T(8,128)(2,1)} %slice_bitcast_fusion), channel_id=1, source_target_pairs={{0,2},{2,0},{1,3},{3,1},{4,6},{6,4},{5,7},{7,5},{8,10},{10,8},{9,1... | collective-permute-start | bytes 3145736 | tf_op jit(solution)/shard_map/ppermute | solution.py:931
  692.4 7.3 copy-start.37
  692.4 7.3 copy-start.39
  737.4 17.7 %copy-start.44 = (bf16[2048,1024]{1,0:T(8,128)(2,1)S(1)}, bf16[2048,1024]{1,0:T(8,128)(2,1)}, u32[]{:S(2)}) copy-start(bf16[2048,1024]{1,0:T(8,128)(2,1)} %convolution_convert_fusion.5) | copy-start | bytes 12582916
  959.1 10.6 %copy-start.53 = (f32[64,8192]{1,0:T(8,128)S(1)}, f32[64,8192]{1,0:T(8,128)}, u32[]{:S(2)}) copy-start(f32[64,8192]{1,0:T(8,128)} %get-tuple-element.279) | copy-start | bytes 6291460
  (93 other events, 233.7 us)

commit v5 on v4

--- a/solution.py
+++ b/solution.py
@@ -42,15 +42,119 @@
     half = HEAD_SIZE // 2
     rate = ROPE_BASE ** (-jnp.arange(half, dtype=F32) * 2.0 / HEAD_SIZE)
     angle = positions.astype(F32)[:, None] * rate[None, :]
-    return jnp.cos(angle)[:, None, :], jnp.sin(angle)[:, None, :]
-
-
-def rotate(value, cosine, sine):
-    half = value.shape[-1] // 2
-    first, second = value[..., :half], value[..., half:]
-    return jnp.concatenate(
-        [first * cosine - second * sine, second * cosine + first * sine], axis=-1
-    )
+    return jnp.cos(angle), jnp.sin(angle)
+
+
+def head_columns(head):
+    return pl.ds(head * HEAD_SIZE, HEAD_SIZE)
+
+
+def heads_kernel(raw_ref, cos_ref, sin_ref, gain_ref, query_ref, pair_ref):
+    half = HEAD_SIZE // 2
+    cosine, sine = cos_ref[...], sin_ref[...]
+    for head in range(QUERY_HEADS + 2 * KEY_VALUE_HEADS):
+        value = raw_ref[:, head_columns(head)]
+        value = value * inverse_rms(value)
+        slot, kind = head - QUERY_HEADS, (head - QUERY_HEADS) // KEY_VALUE_HEADS
+        if kind == 1:
+            pair_ref[1, :, head_columns(slot - KEY_VALUE_HEADS)] = value.astype(BF16)
+            continue
+        value = value * gain_ref[pl.ds(0 if slot < 0 else 1, 1), :]
+        first, second = value[:, :half], value[:, half:]
+        turned = jnp.concatenate(
+            [first * cosine - second * sine, second * cosine + first * sine], axis=1
+        ).astype(BF16)
+        if slot < 0:
+            query_ref[:, head_columns(head)] = turned
+        else:
+            pair_ref[0, :, head_columns(slot)] = turned
+
+
+def heads_back_kernel(
+    raw_ref, query_ref, pair_ref, cos_ref, sin_ref, gain_ref, out_ref, gain_grad_ref
+):
+    half = HEAD_SIZE // 2
+    cosine, sine = cos_ref[...], sin_ref[...]
+
+    @pl.when(pl.program_id(0) == 0)
+    def _():
+        gain_grad_ref[...] = jnp.zeros_like(gain_grad_ref)
+
+    for head in range(QUERY_HEADS + 2 * KEY_VALUE_HEADS):
+        value = raw_ref[:, head_columns(head)]
+        slot, kind = head - QUERY_HEADS, (head - QUERY_HEADS) // KEY_VALUE_HEADS
+        if slot < 0:
+            grad = query_ref[:, head_columns(head)]
+        else:
+            grad = pair_ref[kind, :, head_columns(slot - kind * KEY_VALUE_HEADS)]
+        gain = 1.0
+        if kind < 1:
+            row = pl.ds(0 if slot < 0 else 1, 1)
+            gain = gain_ref[row, :]
+            first, second = grad[:, :half], grad[:, half:]
+            grad = jnp.concatenate(
+                [first * cosine + second * sine, second * cosine - first * sine], axis=1
+            )
+        result, gain_part = rms_back(value, inverse_rms(value), gain, grad)
+        out_ref[:, head_columns(head)] = result.astype(BF16)
+        if kind < 1:
+            gain_grad_ref[row, :] += jnp.sum(gain_part, axis=0, keepdims=True)
+
+
+def strip_spec(rows, *shape):
+    front = len(shape) - 2
+    return pl.BlockSpec(
+        (*shape[:front], rows, shape[-1]), lambda i: (*(0,) * front, i, 0)
+    )
+
+
+def heads(raw, cosine, sine, gain):
+    rows, width = raw.shape
+    strip = min(64, rows)
+    query_width, pair_width = QUERY_HEADS * HEAD_SIZE, KEY_VALUE_HEADS * HEAD_SIZE
+    return pl.pallas_call(
+        heads_kernel,
+        out_shape=(
+            jax.ShapeDtypeStruct((rows, query_width), BF16),
+            jax.ShapeDtypeStruct((2, rows, pair_width), BF16),
+        ),
+        grid=(rows // strip,),
+        in_specs=[
+            strip_spec(strip, rows, width),
+            strip_spec(strip, *cosine.shape),
+            strip_spec(strip, *sine.shape),
+            pl.BlockSpec(gain.shape, lambda i: (0, 0)),
+        ],
+        out_specs=(
+            strip_spec(strip, rows, query_width),
+            strip_spec(strip, 2, rows, pair_width),
+        ),
+    )(raw, cosine, sine, gain)
+
+
+def heads_back(raw, query_grad, pair_grad, cosine, sine, gain):
+    rows, width = raw.shape
+    strip = min(64, rows)
+    return pl.pallas_call(
+        heads_back_kernel,
+        out_shape=(
+            jax.ShapeDtypeStruct((rows, width), BF16),
+            jax.ShapeDtypeStruct(gain.shape, F32),
+        ),
+        grid=(rows // strip,),
+        in_specs=[
+            strip_spec(strip, rows, width),
+            strip_spec(strip, *query_grad.shape),
+            strip_spec(strip, *pair_grad.shape),
+            strip_spec(strip, *cosine.shape),
+            strip_spec(strip, *sine.shape),
+            pl.BlockSpec(gain.shape, lambda i: (0, 0)),
+        ],
+        out_specs=(
+            strip_spec(strip, rows, width),
+            pl.BlockSpec(gain.shape, lambda i: (0, 0)),
+        ),
+    )(raw, query_grad, pair_grad, cosine, sine, gain)
 
 
 def gelu_tanh(value):
@@ -111,8 +215,8 @@
 
 
 def strips(ref):
-    if len(ref.shape) == 3:
-        return [ref.at[i] for i in range(ref.shape[0])]
+    if len(ref.shape) == 4:
+        return [ref.at[i, j] for i in range(ref.shape[0]) for j in range(ref.shape[1])]
     step = min(16, ref.shape[0])
     return [ref.at[pl.ds(i, step)] for i in range(0, ref.shape[0], step)]
 
@@ -348,8 +452,8 @@
     peers = []
     for i in range(1, 8):
         far, side = lax.rem(xc + i // 2, 4), lax.rem(l + i % 2, 2)
-        peers.append((far * 2 + side, {"xc": far, "l": side}))
-    return xc * 2 + l, peers
+        peers.append(((far, side), {"xc": far, "l": side}))
+    return (xc, l), peers
 
 
 def full_places():
@@ -394,7 +498,7 @@
 ):
     rank, peers = full_places()
     me, team = team_peers()
-    spot = copy_places()
+    y, h = lax.axis_index("y"), lax.axis_index("h")
 
     def at(plane, depth):
         return o_ref.at[rank(plane, depth)]
@@ -408,7 +512,7 @@
                 pieces.append(
                     pltpu.make_async_copy(
                         source.at[:, pl.ds(begin * width, width)],
-                        target.at[r, :, pl.ds(c * width, width)],
+                        target.at[r // 2, r % 2, :, pl.ds(c * width, width)],
                         split.at[len(pieces)],
                     )
                 )
@@ -416,8 +520,8 @@
         piece.start()
     keeps = [
         pltpu.make_async_copy(x_ref, at("O", "O"), local.at[0]),
-        pltpu.make_async_copy(gate_ref.at[me], gates_ref.at[spot["O"], me], local.at[1]),
-        pltpu.make_async_copy(up_ref.at[me], ups_ref.at[spot["O"], me], local.at[2]),
+        pltpu.make_async_copy(gate_ref.at[me], gates_ref.at[y, me[0], h, me[1]], local.at[1]),
+        pltpu.make_async_copy(up_ref.at[me], ups_ref.at[y, me[0], h, me[1]], local.at[2]),
     ]
     keeps[0].start()
     greet([peer for _, peer in team] + [peers["Y"], peers["H"]])
@@ -430,8 +534,8 @@
     keeps[1].start()
     keeps[2].start()
     for place, peer in team:
-        swaps.append(out.go(gate_ref.at[place], gates_ref.at[spot["O"], me], peer))
-        swaps.append(out.go(up_ref.at[place], ups_ref.at[spot["O"], me], peer))
+        swaps.append(out.go(gate_ref.at[place], gates_ref.at[y, me[0], h, me[1]], peer))
+        swaps.append(out.go(up_ref.at[place], ups_ref.at[y, me[0], h, me[1]], peer))
     direct, bent = {}, {}
 
     def begin(depth):
@@ -458,13 +562,13 @@
     flats, arrivals = {}, []
 
     def spread(name):
-        mine = blocks[name].at[spot["O"]]
+        mine = blocks[name].at[y, :, h]
         flats[name] = out.go(mine, mine, peers["H"])
         arrivals.append(out.go(mine, mine, peers["Y"]))
 
     def corner(name):
         flats[name].wait_recv()
-        piece = blocks[name].at[spot["H"]]
+        piece = blocks[name].at[y, :, 1 - h]
         arrivals.append(out.go(piece, piece, peers["Y"]))
 
     begin("O")
@@ -500,11 +604,13 @@
 
 def weights_in(columns, gate, up, down):
     rows, width = columns.shape
-    ranks, depth, part = 8, gate.shape[0], gate.shape[1] // 8
+    depth, part = gate.shape[0], gate.shape[1] // 8
     if not small_grid():
         full = lax.all_gather(columns, AXES, axis=0, tiled=False)
         gates, ups = (
-            lax.all_gather(lax.all_to_all(b, TEAM, 0, 0), COPIES, axis=0, tiled=False)
+            rows_in_order(
+                lax.all_gather(lax.all_to_all(b, TEAM, 0, 0), COPIES, axis=0, tiled=False)
+            )
             for b in (column_blocks(gate), column_blocks(up))
         )
         far = None
@@ -513,8 +619,8 @@
             weights_in_kernel,
             (
                 jax.ShapeDtypeStruct((32, rows, width), BF16),
-                jax.ShapeDtypeStruct((4, ranks, depth, part), BF16),
-                jax.ShapeDtypeStruct((4, ranks, depth, part), BF16),
+                jax.ShapeDtypeStruct((2, 4, 2, 2, depth, part), BF16),
+                jax.ShapeDtypeStruct((2, 4, 2, 2, depth, part), BF16),
                 jax.ShapeDtypeStruct(down.shape, BF16),
             ),
             14 + 3 + 28 + 7,
@@ -522,8 +628,8 @@
             [
                 pltpu.SemaphoreType.DMA((3,)),
                 pltpu.SemaphoreType.DMA((64,)),
-                pltpu.VMEM((ranks, depth, part), BF16),
-                pltpu.VMEM((ranks, depth, part), BF16),
+                pltpu.VMEM((4, 2, depth, part), BF16),
+                pltpu.VMEM((4, 2, depth, part), BF16),
             ],
             spaces=[pl.ANY] * 4,
             inputs=4,
@@ -544,7 +650,7 @@
     flat_far, flat_y = refs[n + 21], refs[n + 22 :]
     rank, peers = full_places()
     me, team = team_peers()
-    spot = copy_places()
+    y, h = lax.axis_index("y"), lax.axis_index("h")
     half = mine.shape[2] // 2
     top, low = pl.ds(0, half), pl.ds(half, half)
     loads, swaps, flights = {}, {}, {}
@@ -564,8 +670,8 @@
                 load(part.at[place], mine.at[t, k, :, pl.ds(begin, part.shape[2])])
                 for part, begin in zip(parts, edges)
             ]
-    own_loads = [load(near_ref, flat[0]), load(raw_ref.at[spot["O"]], flat[1])]
-    far_load = load(raw_ref.at[spot["H"]], flat_far)
+    own_loads = [load(near_ref, flat[0]), load(raw_ref.at[y, :, h], flat[1])]
+    far_load = load(raw_ref.at[y, :, 1 - h], flat_far)
     greet([peer for _, peer in team] + [peers["Y"], peers["H"]])
     out = Sender(send, recv)
 
@@ -611,7 +717,7 @@
 
     swap(0)
     h_side = [out.go(far_ref, flat_h[0], peers["H"])]
-    y_side = [out.go(raw_ref.at[spot["D"]], flat_y[0], peers["Y"])]
+    y_side = [out.go(raw_ref.at[1 - y, :, 1 - h], flat_y[0], peers["Y"])]
     swap(1)
     swap(2)
     swap(3)
@@ -626,7 +732,7 @@
     y_side[0].wait_recv()
     add_into(flat_far, flat_y[0])
     h_side.append(out.go(flat_far, flat_h[1], peers["H"]))
-    y_side.append(out.go(raw_ref.at[spot["Y"]], flat_y[1], peers["Y"]))
+    y_side.append(out.go(raw_ref.at[1 - y, :, h], flat_y[1], peers["Y"]))
     bend(0)
     for k in (0, 1, 2):
         join(2, k)
@@ -675,7 +781,7 @@
             for c in range(4):
                 begin = ((c // 2 * 4 + r // 2) * 2 + c % 2) * 2 + r % 2
                 target[:, pl.ds(begin * width, width)] = back_in[i][
-                    r, :, pl.ds(c * width, width)
+                    r // 2, r % 2, :, pl.ds(c * width, width)
                 ].astype(F32)
     out.finish()
 
@@ -687,7 +793,7 @@
     if not small_grid():
         block = jnp.concatenate(blocks, axis=2)
         total = lax.psum_scatter(block, AXES, scatter_dimension=0, tiled=False).astype(F32)
-        up = lax.psum_scatter(up, COPIES, scatter_dimension=0, tiled=False)
+        up = lax.psum_scatter(rows_by_copy(up), COPIES, scatter_dimension=0, tiled=False)
         gate, up = (
             from_column_blocks(lax.all_to_all(value, TEAM, 0, 0)).astype(F32)
             for value in (gate, up)
@@ -702,8 +808,8 @@
         partial(grads_out_kernel, tuple(edges)),
         (
             jax.ShapeDtypeStruct((rows, width), F32),
-            jax.ShapeDtypeStruct((flat[1], 8 * flat[2]), F32),
-            jax.ShapeDtypeStruct((flat[1], 8 * flat[2]), F32),
+            jax.ShapeDtypeStruct((flat[2], 8 * flat[3]), F32),
+            jax.ShapeDtypeStruct((flat[2], 8 * flat[3]), F32),
         ),
         16 * len(parts) + 24 + 3 + 4 + 14,
         4,
@@ -729,15 +835,19 @@
 
 def lane_sums(value):
     if not small_grid():
-        return lax.psum_scatter(value, COPIES, scatter_dimension=0, tiled=False)
-    spot = copy_places()
-
-    def piece(k):
-        return lax.dynamic_index_in_dim(value, spot[k], axis=0, keepdims=False)
-
-    sent = jnp.stack([piece("D"), piece("Y")])
+        return lax.psum_scatter(rows_by_copy(value), COPIES, scatter_dimension=0, tiled=False)
+    y, h = lax.axis_index("y"), lax.axis_index("h")
+
+    def piece(a, b):
+        plane = lax.dynamic_index_in_dim(value, a, axis=0, keepdims=False)
+        return lax.dynamic_index_in_dim(plane, b, axis=1, keepdims=False)
+
+    sent = jnp.stack([piece(1 - y, 1 - h), piece(1 - y, h)])
     arrived = lax.ppermute(sent, "y", [(0, 1), (1, 0)])
-    return [plus(piece(k), arrived[j]).astype(BF16) for j, k in enumerate("HO")]
+    return [
+        plus(piece(y, 1 - h), arrived[0]).astype(BF16),
+        plus(piece(y, h), arrived[1]).astype(BF16),
+    ]
 
 
 def shift(block, distance):
@@ -760,18 +870,16 @@
     return split.reshape(depth, 8 * width)
 
 
-def depth_order(value):
+def rows_in_order(value):
     ys, hs = lax.axis_size("y"), lax.axis_size("h")
-    rows, width = value.shape
-    split = value.reshape(rows, ys, 4, hs, width // (4 * ys * hs))
-    return split.transpose(0, 1, 3, 2, 4).reshape(rows, width)
-
-
-def from_depth_order(value):
-    ys, hs = lax.axis_size("y"), lax.axis_size("h")
-    rows, width = value.shape
-    split = value.reshape(rows, ys, hs, 4, width // (4 * ys * hs))
-    return split.transpose(0, 1, 3, 2, 4).reshape(rows, width)
+    split = value.reshape(ys, hs, 4, 2, *value.shape[2:])
+    return split.transpose(0, 2, 1, 3, 4, 5)
+
+
+def rows_by_copy(value):
+    ys, hs = value.shape[0], value.shape[2]
+    split = value.transpose(0, 2, 1, 3, 4, 5)
+    return split.reshape(ys * hs, 8, *value.shape[4:])
 
 
 def layer(*args):
@@ -846,20 +954,12 @@
     normed = hidden * hidden_inv * gains[0]
     normed_low = normed.astype(BF16)
     raw = dot(normed_low, first)
-    query_raw = raw[:, :head_width].reshape(rows, QUERY_HEADS, HEAD_SIZE)
-    key_raw = raw[:, head_width : head_width + kv_width].reshape(rows, KEY_VALUE_HEADS, HEAD_SIZE)
-    value_raw = raw[:, head_width + kv_width :].reshape(
-        rows, KEY_VALUE_HEADS, HEAD_SIZE
-    )
     left_low = dot(normed_low, left_all).astype(BF16)
-    query_inv = inverse_rms(query_raw)
-    key_inv = inverse_rms(key_raw)
-    value_inv = inverse_rms(value_raw)
-    query_low = rotate(query_raw * query_inv * head_gain[0], cosine, sine).astype(BF16)
-    key_low = rotate(key_raw * key_inv * head_gain[1], cosine, sine).astype(BF16)
-    value_low = (value_raw * value_inv).astype(BF16)
-    moving = jnp.stack([key_low, value_low])
-    window = jnp.concatenate([shift(moving, hop) for hop in range(hops, 0, -1)] + [moving], axis=1)
+    query_low, pair_low = heads(raw, cosine, sine, head_gain)
+    pairs = [pair_low]
+    for _ in range(hops):
+        pairs.insert(0, shift(pairs[0], 1))
+    window = jnp.concatenate(pairs, axis=1).reshape(2, -1, KEY_VALUE_HEADS, HEAD_SIZE)
     grouped = query_low.reshape(rows, KEY_VALUE_HEADS, groups, HEAD_SIZE)
     scores = jnp.einsum("qkgd,tkd->kgqt", grouped, window[0], preferred_element_type=F32)
     allowed = (
@@ -889,7 +989,7 @@
     merged_inv = inverse_rms(merged)
     expand_low = (merged * merged_inv * gains[3]).astype(BF16)
 
-    expand_all, down_rows = team_gather_with(depth_order(expand_low), down_weight, far_down)
+    expand_all, down_rows = team_gather_with(expand_low, down_weight, far_down)
     gate_raw = dot(expand_all, gate_cols)
     up_raw = dot(expand_all, up_cols)
     act_low = (gelu(gate_raw) * up_raw).astype(BF16)
@@ -923,17 +1023,16 @@
     part_up = dot(expand_all, grad_up_low, 0, 0).astype(BF16)
     down_blocks = part_down.reshape(-1, *down_weight.shape)
     part_gate, part_up = (
-        value.reshape(-1, 8, depth, value.shape[1]) for value in (part_gate, part_up)
+        value.reshape(lax.axis_size("y"), 4, -1, 2, depth, value.shape[1])
+        for value in (part_gate, part_up)
     )
     part_low, part_gate, part_up = lax.optimization_barrier((part_low, part_gate, part_up))
     if small_grid():
         part, down_sums = team_scatter(part_low, down_blocks)
-        grad_down = plus(down_sums[1], lax.ppermute(down_sums[0], "h", [(0, 1), (1, 0)]))
     else:
         part = team_scatter(part_low)
-        grad_down = lax.psum_scatter(down_blocks, COPIES, scatter_dimension=0).astype(F32)
+        down_sums = None
     sums_gate = lane_sums(part_gate)
-    part = from_depth_order(part)
     grad_merged, gain_three = rms_back(merged, merged_inv, gains[3], part)
     grad_sum = (grad_after + grad_merged) * HALF_ROOT
     grad_right, gain_two = rms_back(right_raw, right_inv, gains[2], grad_sum)
@@ -951,34 +1050,23 @@
     grad_scores = (probs * (grad_probs - inner)).astype(BF16)
     grad_query_rot = jnp.einsum(
         "kgqt,tkd->qkgd", grad_scores, window[0], preferred_element_type=F32
-    ).reshape(rows, QUERY_HEADS, HEAD_SIZE)
+    ).reshape(rows, head_width)
     grad_window = jnp.stack(
         [
             jnp.einsum("kgqt,qkgd->tkd", grad_scores, grouped, preferred_element_type=F32),
             jnp.einsum("kgqt,qkgd->tkd", probs_low, grad_mixed, preferred_element_type=F32),
         ]
-    )
-    carried = grad_window[:, hops * rows :]
+    ).reshape(2, -1, kv_width)
+    carried = grad_window[:, :rows]
     for hop in range(1, hops + 1):
-        begin = (hops - hop) * rows
-        carried = carried + shift(
-            grad_window[:, begin : begin + rows].astype(BF16), -hop
-        ).astype(F32)
-    grad_query, head_zero = rms_back(
-        query_raw, query_inv, head_gain[0], rotate(grad_query_rot, cosine, -sine)
-    )
-    grad_key, head_one = rms_back(
-        key_raw, key_inv, head_gain[1], rotate(carried[0], cosine, -sine)
-    )
-    grad_value, _ = rms_back(value_raw, value_inv, 1.0, carried[1])
-    grad_raw = jnp.concatenate(
-        [
-            grad_query.reshape(rows, head_width).astype(BF16),
-            grad_key.reshape(rows, kv_width).astype(BF16),
-            grad_value.reshape(rows, kv_width).astype(BF16),
-        ],
-        axis=1,
-    )
+        carried = shift(carried.astype(BF16), -1).astype(F32)
+        carried = carried + grad_window[:, hop * rows : (hop + 1) * rows]
+    if down_sums is None:
+        grad_down = lax.psum_scatter(down_blocks, COPIES, scatter_dimension=0).astype(F32)
+    else:
+        carried, leaving = lax.optimization_barrier((carried, down_sums[0]))
+        grad_down = plus(down_sums[1], lax.ppermute(leaving, "h", [(0, 1), (1, 0)]))
+    grad_raw, head_grads = heads_back(raw, grad_query_rot, carried, cosine, sine, head_gain)
     grad_normed = grad_sum + dot(grad_raw, first, 1, 1) + dot(grad_left_low, left_all, 1, 1)
     grad_input, gain_zero = rms_back(hidden, hidden_inv, gains[0], grad_normed)
     grad_hidden = grad_sum + grad_input
@@ -989,8 +1077,6 @@
             for g in (gain_zero, gain_one, gain_two, gain_three, gain_four, gain_five)
         ]
     )
-    head_grads = jnp.stack([jnp.sum(head_zero, axis=(0, 1)), jnp.sum(head_one, axis=(0, 1))])
-
     head_column = jnp.pad(
         head_grads.T.reshape(-1, head_part, 2), ((0, 0), (0, depth - head_part), (0, 0))
     ).reshape(-1, 2)

time: 981 us -> 934 us (0.952)
  local copies, waits for them, and re-layouts: 96.6 us -> 57.1 us
  other arithmetic: 54.3 us -> 30.2 us
  waiting for transfers between devices: 14.8 us -> 25.6 us
    ppermute x4, waiting for transfers between devices: 0.01 us -> 25.6 us  [shift(): return lax.ppermute(block, ('h', 'l'), route)]
    unnamed x297 -> x163, local copies, waits for them, and re-layouts: 42.2 us -> 17 us
    ppermute x1, waiting for transfers between devices: 14.8 us -> 0.01 us  [layer(): grad_down = plus(down_sums[1], lax.ppermute(leaving, 'h', [(0, 1), (1, 0)]))]
    pallas_call x1, Pallas kernels: 200 us -> 187 us  [grads_out(): remote_call(partial(grads_out_kernel, tuple(edges)), (jax.ShapeDtypeStruc...]
  transfers between devices with their start and end apart: 6 -> 6, of which waited for: 1 -> 4; matrix products, arithmetic and copies ran while one was open for 9% -> 7% of each run, Pallas kernels for 0% -> 21%
where the time goes in v5:
time: 934 us; the launch traced here: 927 us
  Pallas kernels  580 us (62%)
  matrix products  216 us (23%)
  local copies, waits for them, and re-layouts  57.1 us (6%)
  other arithmetic  30.2 us (3%)
  waiting for transfers between devices  25.6 us (3%)
  starting transfers between devices  15.5 us (2%)
    pallas_call x1, Pallas kernels, weights_in(): remote_call(weights_in_kernel, (jax.ShapeDtypeStruct((32, rows, width), B...  202 us
    dot_general x27, matrix products, dot(): lax.dot_general(left, right, (((left_dim,), (right_dim,)), ((), ())), pre...  192 us
    pallas_call x1, Pallas kernels, grads_out(): remote_call(partial(grads_out_kernel, tuple(edges)), (jax.ShapeDtypeStruc...  187 us
    pallas_call x1, Pallas kernels, team_gather_with(): remote_call(partial(team_gather_kernel, True), (jax.ShapeDtypeStruct((8,...  49.7 us
    pallas_call x1, Pallas kernels, team_scatter(): remote_call(partial(team_scatter_kernel, True), (total, jax.ShapeDtypeStr...  48.1 us
    pallas_call x1, Pallas kernels, team_scatter(): remote_call(partial(team_scatter_kernel, False), total, 10, 1, [pltpu.Sem...  43.8 us
    pallas_call x1, Pallas kernels, team_gather(): remote_call(partial(team_gather_kernel, False), jax.ShapeDtypeStruct((8,...  39.4 us
    ppermute x4, waiting for transfers between devices, shift(): return lax.ppermute(block, ('h', 'l'), route)  25.6 us
  transfers between devices with their start and end apart: 6, of which 4 were waited for; matrix products, arithmetic and copies ran while one was open for 7% of the time, Pallas kernels for 21%

profile of v5, /device:TPU:1, one launch (start us, length us, event | category | flops | bytes accessed | tf_op | source)
XLA Modules:
  0.0 927.1 jit_solution(12323935531076469123)
XLA Ops:
  5.3 202.2 %shard_map.280 = (bf16[32,64,5888]{2,1,0:T(8,128)(2,1)}, bf16[2,4,2,2,64,1024]{5,4,3,2,1,0:T(8,128)(2,1)}, bf16[2,4,2,2,64,1024]{5,4,3,2,1,0:T(8,128)(2,1)}, bf16[256,2048]{1,0:T(8,128)(2,1)}) custom-call(bf16[64,5888]{1,0:T(8,128)(2,1)} %pad.29.x_ref, bf16[64,8192]{1,0:T(8,128)(2,1)} %gate_in.1, bf16[64,8192]{1,0:T(8,128)(2,1)} %up_in.1, ...), custom_call_target="tpu_custom_call" | custom-call | tf_op jit(solution)/shard_map/pallas_call | solution.py:618
  213.2 9.8 %fusion.3.raw_ref = f32[256,3072]{1,0:T(8,128)} fusion(bf16[2048,5888]{1,0:T(8,128)(2,1)} %bitcast.191, bf16[256,2048]{1,0:T(8,128)(2,1)S(1)} %copy-done.5, f32[2048]{0:T(1024)S(1)} %bitcast.210, f32[256]{0:T(256)S(1)} %add_rsqrt_fusion.5), kind=kOutput, calls=%fused_computation.7 | convolution fusion | flops 3223322624 | bytes 16786432 | tf_op jit(solution)/shard_map/dot_general | solution.py:25
  223.0 4.3 shard_map.281
  227.3 4.8 collective-permute-start
  237.5 5.0 collective-permute-done
  242.5 4.3 collective-permute-start.1
  247.8 9.1 collective-permute-done.1
  259.3 2.9 squeeze.28
  262.2 3.0 copy.118
  265.3 2.9 squeeze.27
  268.2 6.3 fusion.107
  274.5 4.1 fusion.51
  278.6 6.2 multiply_reduce_fusion.14
  288.8 49.7 %shard_map.282 = (bf16[8,256,2048]{2,1,0:T(8,128)(2,1)}, bf16[4,256,2048]{2,1,0:T(8,128)(2,1)S(1)}) custom-call(bf16[256,2048]{1,0:T(8,128)(2,1)S(1)} %multiply_convert_fusion.6.refs_0_, bf16[256,2048]{1,0:T(8,128)(2,1)S(1)} %copy-done.1, bf16[256,2048]{1,0:T(8,128)(2,1)S(1)} %copy-done.2), custom_call_target="tpu_custom_call" | custom-call | tf_op jit(solution)/shard_map/pallas_call | solution.py:336
  338.5 15.0 %fusion.108 = f32[2048,1024]{1,0:T(8,128)} fusion(bf16[2048,2048]{1,0:T(8,128)(2,1)} %bitcast.242, bf16[2048,1024]{1,0:T(8,128)(2,1)} %bitcast.250), kind=kOutput, calls=%fused_computation.195 | convolution fusion | flops 8589934592 | bytes 20971520 | tf_op jit(solution)/shard_map/dot_general | solution.py:25
  353.5 14.1 %multiply_convert_fusion.1 = (bf16[2048,1024]{1,0:T(8,128)(2,1)}, f32[2048,1024]{1,0:T(8,128)}) fusion(f32[2048,1024]{1,0:T(8,128)} %fusion.108, bf16[2048,2048]{1,0:T(8,128)(2,1)S(1)} %bitcast.244, bf16[2048,1024]{1,0:T(8,128)(2,1)S(1)} %bitcast.248), kind=kOutput, calls=%fused_computation.18 | convolution fusion | flops 8610906112 | bytes 33554432 | tf_op jit(solution)/shard_map/dot_general | solution.py:25
  367.6 10.7 %convolution_convert_fusion.2 = bf16[2048,2048]{1,0:T(8,128)(2,1)S(1)} fusion(bf16[2048,1024]{1,0:T(8,128)(2,1)} %get-tuple-element.153, bf16[1024,2048]{1,0:T(8,128)(2,1)S(1)} %bitcast.166), kind=kOutput, calls=%fused_computation.21 | convolution fusion | flops 8594128896 | bytes 16777216 | tf_op jit(solution)/shard_map/dot_general | solution.py:25
  378.4 43.8 %shard_map.283 = f32[256,2048]{1,0:T(8,128)S(1)} custom-call(bf16[8,256,2048]{2,1,0:T(8,128)(2,1)S(1)} %bitcast.163), custom_call_target="tpu_custom_call" | custom-call | tf_op jit(solution)/shard_map/pallas_call | solution.py:428
  434.8 2.7 multiply_reduce_fusion.1
  439.3 39.4 %shard_map.284 = bf16[8,256,2048]{2,1,0:T(8,128)(2,1)S(1)} custom-call(bf16[256,2048]{1,0:T(8,128)(2,1)S(1)} %multiply_convert_fusion.4.refs_0_), custom_call_target="tpu_custom_call" | custom-call | tf_op jit(solution)/shard_map/pallas_call | solution.py:320
  478.7 10.6 %convolution_convert_fusion.3 = bf16[1024,2048]{1,0:T(8,128)(2,1)} fusion(bf16[2048,1024]{1,0:T(8,128)(2,1)S(1)} %copy-done.68, bf16[2048,2048]{1,0:T(8,128)(2,1)S(1)} %bitcast.164), kind=kOutput, calls=%fused_computation.34 | convolution fusion | flops 8592031744 | bytes 16777216 | tf_op jit(solution)/shard_map/dot_general | solution.py:25
  489.2 21.3 %multiply_convert_fusion = (bf16[2048,1024]{1,0:T(8,128)(2,1)}, bf16[2048,1024]{1,0:T(8,128)(2,1)}) fusion(f32[2048,1024]{1,0:T(8,128)} %fusion.108, f32[2048,1024]{1,0:T(8,128)} %get-tuple-element.154, bf16[2048,2048]{1,0:T(8,128)(2,1)} %bitcast.165, bf16[1024,2048]{1,0:T(8,128)(2,1)S(1)} %bitcast.167), kind=kOutput, calls=%fused_computation.17 | convolution fusion | flops 8638169088 | bytes 37748736 | tf_op jit(solution)/shard_map/dot_general | solution.py:25
  510.5 14.1 %convolution_convert_fusion.5 = bf16[2048,1024]{1,0:T(8,128)(2,1)} fusion(bf16[2048,2048]{1,0:T(8,128)(2,1)} %bitcast.243, bf16[2048,1024]{1,0:T(8,128)(2,1)} %get-tuple-element.118), kind=kOutput, calls=%fused_computation.36 | convolution fusion | flops 8592031744 | bytes 16777216 | tf_op jit(solution)/shard_map/dot_general | solution.py:25
  524.6 11.7 %fusion.109 = f32[2048,2048]{1,0:T(8,128)} fusion(bf16[2048,1024]{1,0:T(8,128)(2,1)S(1)} %copy-done.70, bf16[2048,1024]{1,0:T(8,128)(2,1)S(1)} %bitcast.251), kind=kOutput, calls=%fused_computation.196 | convolution fusion | flops 8589934592 | bytes 25165824 | tf_op jit(solution)/shard_map/dot_general | solution.py:25
  536.4 11.2 %convolution_convert_fusion.4 = bf16[2048,1024]{1,0:T(8,128)(2,1)} fusion(bf16[2048,2048]{1,0:T(8,128)(2,1)S(1)} %bitcast.247, bf16[2048,1024]{1,0:T(8,128)(2,1)S(1)} %copy-done.69), kind=kOutput, calls=%fused_computation.35 | convolution fusion | flops 8592031744 | bytes 16777216 | tf_op jit(solution)/shard_map/dot_general | solution.py:25
  547.5 14.0 %add_convert_fusion = bf16[2048,2048]{1,0:T(8,128)(2,1)} fusion(f32[2048,2048]{1,0:T(8,128)} %fusion.109, bf16[2048,1024]{1,0:T(8,128)(2,1)S(1)} %copy-done.69, bf16[2048,1024]{1,0:T(8,128)(2,1)S(1)} %bitcast.249), kind=kOutput, calls=%fused_computation.1 | convolution fusion | flops 8598323200 | bytes 33554432 | tf_op jit(solution)/shard_map/dot_general | solution.py:25
  561.6 48.1 %shard_map.285 = (f32[256,2048]{1,0:T(8,128)S(1)}, bf16[2,256,2048]{2,1,0:T(8,128)(2,1)S(1)}) custom-call(bf16[8,256,2048]{2,1,0:T(8,128)(2,1)} %bitcast.171, bf16[4,256,2048]{2,1,0:T(8,128)(2,1)} %bitcast.175), custom_call_target="tpu_custom_call" | custom-call | tf_op jit(solution)/shard_map/pallas_call | solution.py:438
  612.0 2.5 multiply_reduce_fusion.3
  617.5 6.7 fusion.32
  625.7 5.1 fusion.47
  630.8 3.9 fusion.17
  638.3 2.3 fusion.110
  642.4 3.0 copy.135
  647.4 3.1 copy.134
  655.2 5.6 convolution_convert_fusion.1
  660.7 5.5 collective-permute-done.2
  671.0 2.9 copy.133.query_ref
  674.9 6.0 collective-permute-done.3
  680.9 2.3 fusion.61.pair_ref
  683.3 5.2 shard_map.286
  689.3 2.4 collective-permute-start.5
  691.7 9.1 fusion.28
  700.8 3.2 fusion.41
  705.6 4.0 fusion.31
  711.7 6.8 convolution_convert_fusion
  718.5 3.8 fusion.44
  722.3 187.2 %shard_map.287 = (f32[64,5888]{1,0:T(8,128)}, f32[64,8192]{1,0:T(8,128)}, f32[64,8192]{1,0:T(8,128)}) custom-call(bf16[32,64,3072]{2,1,0:T(8,128)(2,1)} %bitcast.168, bf16[32,64,2048]{2,1,0:T(8,128)(2,1)} %bitcast.169, bf16[32,64,256]{2,1,0:T(8,128)(2,1)} %bitcast.183, bf16[32,64,256]{2,1,0:T(8,128)(2,1)} %bitcast.205, bf16[32,64,256]{2,1,0:T(8,128)(2,1)} %bitcast.184, ...), custom_call_target="tpu_custom_call" | custom-call | tf_op jit(solution)/shard_map/pallas_call | solution.py:807
  920.0 3.0 convert_add_fusion.1
  (239 shorter events, 79.3 us)
Async XLA Ops:
  5.3 204.5 %copy-start.5 = (bf16[256,2048]{1,0:T(8,128)(2,1)S(1)}, bf16[256,2048]{1,0:T(8,128)(2,1)}, u32[]{:S(2)}) copy-start(bf16[256,2048]{1,0:T(8,128)(2,1)} %param.17) | copy-start | bytes 3145732
  210.1 75.2 %copy-start.43 = (f32[256]{0:T(256)}, f32[256]{0:T(256)S(1)}, u32[]{:S(2)}) copy-start(f32[256]{0:T(256)S(1)} %add_rsqrt_fusion.5) | copy-start | bytes 3076
  211.9 73.4 %copy-start.34 = (f32[1,2048]{1,0:T(1,128)}, f32[1,2048]{1,0:T(1,128)S(1)}, u32[]{:S(2)}) copy-start(f32[1,2048]{1,0:T(1,128)S(1)} %get-tuple-element.142) | copy-start | bytes 24580
  211.9 75.2 %copy-start.39 = (f32[1,2048]{1,0:T(1,128)}, f32[1,2048]{1,0:T(1,128)S(1)}, u32[]{:S(2)}) copy-start(f32[1,2048]{1,0:T(1,128)S(1)} %get-tuple-element.139) | copy-start | bytes 24580
  227.3 7.1 copy-start.31
  227.3 15.2 %collective-permute-start = (bf16[2,256,512]{2,1,0:T(8,128)(2,1)}, bf16[2,256,512]{2,1,0:T(8,128)(2,1)}, u32[]{:S(2)}, u32[]{:S(2)}) collective-permute-start(bf16[2,256,512]{2,1,0:T(8,128)(2,1)} %get-tuple-element.36), channel_id=1, source_target_pairs={{0,1},{1,2},{2,3},{4,5},{5,6},{6,7},{8,9},{9,10},{10,11},{12,13},{... | collective-permute-start | bytes 1572872 | tf_op jit(solution)/shard_map/ppermute | solution.py:856
  233.7 3.8 copy-start.36
  235.7 22.3 %copy-start.33 = (bf16[2,256,512]{2,1,0:T(8,128)(2,1)S(1)}, bf16[2,256,512]{2,1,0:T(8,128)(2,1)}, u32[]{:S(2)}) copy-start(bf16[2,256,512]{2,1,0:T(8,128)(2,1)} %get-tuple-element.36) | copy-start | bytes 1572868
  237.4 9.4 %copy-start.53 = (f32[256]{0:T(256)}, f32[256]{0:T(256)S(1)}, u32[]{:S(2)}) copy-start(f32[256]{0:T(256)S(1)} %get-tuple-element.147) | copy-start | bytes 3076
  237.5 47.9 %copy-start.7 = (f32[256,2048]{1,0:T(8,128)}, f32[256,2048]{1,0:T(8,128)S(1)}, u32[]{:S(2)}) copy-start(f32[256,2048]{1,0:T(8,128)S(1)} %get-tuple-element.148) | copy-start | bytes 6291460
  237.5 47.9 %copy-start.49 = (f32[256]{0:T(256)}, f32[256]{0:T(256)S(1)}, u32[]{:S(2)}) copy-start(f32[256]{0:T(256)S(1)} %add_rsqrt_fusion.3) | copy-start | bytes 3076
  242.5 14.4 %collective-permute-start.1 = (bf16[2,256,512]{2,1,0:T(8,128)(2,1)}, bf16[2,256,512]{2,1,0:T(8,128)(2,1)S(1)}, u32[]{:S(2)}, u32[]{:S(2)}) collective-permute-start(bf16[2,256,512]{2,1,0:T(8,128)(2,1)} %collective-permute-done), channel_id=1, source_target_pairs={{0,1},{1,2},{2,3},{4,5},{5,6},{6,7},{8,9},{9,10},{10,11},{12,13},{... | collective-permute-start | bytes 1572872 | tf_op jit(solution)/shard_map/ppermute | solution.py:856
  274.5 4.1 copy-start.59
  278.6 6.2 copy-start.28
  286.5 52.0 %copy-start.57 = (f32[256]{0:T(256)}, f32[256]{0:T(256)S(1)}, u32[]{:S(2)}) copy-start(f32[256]{0:T(256)S(1)} %get-tuple-element.115) | copy-start | bytes 3076
  286.5 135.9 %copy-start.3 = (f32[256,2048]{1,0:T(8,128)}, f32[256,2048]{1,0:T(8,128)S(1)}, u32[]{:S(2)}) copy-start(f32[256,2048]{1,0:T(8,128)S(1)} %get-tuple-element.116) | copy-start | bytes 6291460
  287.1 51.4 %copy-start.47 = (f32[256]{0:T(256)}, f32[256]{0:T(256)S(1)}, u32[]{:S(2)}) copy-start(f32[256]{0:T(256)S(1)} %get-tuple-element.146) | copy-start | bytes 3076
  338.5 15.0 %copy-start.64 = (bf16[8,256,2048]{2,1,0:T(8,128)(2,1)S(1)}, bf16[8,256,2048]{2,1,0:T(8,128)(2,1)}, u32[]{:S(2)}) copy-start(bf16[8,256,2048]{2,1,0:T(8,128)(2,1)} %get-tuple-element.39) | copy-start | bytes 25165828
  338.5 15.0 %copy-start.65 = (bf16[2,4,2,2,64,1024]{5,4,3,2,1,0:T(8,128)(2,1)S(1)}, bf16[2,4,2,2,64,1024]{5,4,3,2,1,0:T(8,128)(2,1)}, u32[]{:S(2)}) copy-start(bf16[2,4,2,2,64,1024]{5,4,3,2,1,0:T(8,128)(2,1)} %get-tuple-element.41) | copy-start | bytes 12582916
  439.3 39.4 %copy-start.68 = (bf16[2048,1024]{1,0:T(8,128)(2,1)S(1)}, bf16[2048,1024]{1,0:T(8,128)(2,1)}, u32[]{:S(2)}) copy-start(bf16[2048,1024]{1,0:T(8,128)(2,1)} %get-tuple-element.153) | copy-start | bytes 12582916
  478.6 10.6 %copy-start = (bf16[8,256,2048]{2,1,0:T(8,128)(2,1)}, bf16[8,256,2048]{2,1,0:T(8,128)(2,1)S(1)}, u32[]{:S(2)}) copy-start(bf16[8,256,2048]{2,1,0:T(8,128)(2,1)S(1)} %shard_map.284) | copy-start | bytes 25165828
  510.5 14.1 %copy-start.67 = (bf16[2,4,2,2,64,1024]{5,4,3,2,1,0:T(8,128)(2,1)S(1)}, bf16[2,4,2,2,64,1024]{5,4,3,2,1,0:T(8,128)(2,1)}, u32[]{:S(2)}) copy-start(bf16[2,4,2,2,64,1024]{5,4,3,2,1,0:T(8,128)(2,1)} %get-tuple-element.40) | copy-start | bytes 12582916
  510.5 14.1 %copy-start.70 = (bf16[2048,1024]{1,0:T(8,128)(2,1)S(1)}, bf16[2048,1024]{1,0:T(8,128)(2,1)}, u32[]{:S(2)}) copy-start(bf16[2048,1024]{1,0:T(8,128)(2,1)} %get-tuple-element.118) | copy-start | bytes 12582916
  510.5 25.8 %slice-start.2 = ((s8[8388608]{0:T(1024)(128)(4,1)}), s8[4194304]{0:T(1024)(128)(4,1)S(1)}, s32[]{:S(2)}) async-start(s8[8388608]{0:T(1024)(128)(4,1)} %bitcast.245), calls=%async_computation.2 | async-start | bytes 8388608
  524.6 11.7 %slice-start.3 = ((s8[8388608]{0:T(1024)(128)(4,1)}), s8[4194304]{0:T(1024)(128)(4,1)S(1)}, s32[]{:S(2)}) async-start(s8[8388608]{0:T(1024)(128)(4,1)} %bitcast.245), calls=%async_computation.3 | async-start | bytes 8388608
  524.6 11.7 %copy-start.69 = (bf16[2048,1024]{1,0:T(8,128)(2,1)S(1)}, bf16[2048,1024]{1,0:T(8,128)(2,1)}, u32[]{:S(2)}) copy-start(bf16[2048,1024]{1,0:T(8,128)(2,1)} %get-tuple-element.117) | copy-start | bytes 12582916
  536.4 11.2 %copy-start.66 = (bf16[2,4,2,2,64,1024]{5,4,3,2,1,0:T(8,128)(2,1)S(1)}, bf16[2,4,2,2,64,1024]{5,4,3,2,1,0:T(8,128)(2,1)}, u32[]{:S(2)}) copy-start(bf16[2,4,2,2,64,1024]{5,4,3,2,1,0:T(8,128)(2,1)} %get-tuple-element.41) | copy-start | bytes 12582916
  561.6 48.1 %copy-start.4 = (f32[256,2048]{1,0:T(8,128)S(1)}, f32[256,2048]{1,0:T(8,128)}, u32[]{:S(2)}) copy-start(f32[256,2048]{1,0:T(8,128)} %copy-done.3) | copy-start | bytes 6291460
  561.6 48.1 %copy-start.40 = (f32[1,2048]{1,0:T(1,128)S(1)}, f32[1,2048]{1,0:T(1,128)}, u32[]{:S(2)}) copy-start(f32[1,2048]{1,0:T(1,128)} %copy-done.39) | copy-start | bytes 24580
  561.6 48.1 %copy-start.48 = (f32[256]{0:T(256)S(1)}, f32[256]{0:T(256)}, u32[]{:S(2)}) copy-start(f32[256]{0:T(256)} %copy-done.47) | copy-start | bytes 3076
  561.6 48.9 %copy-start.17 = (f32[256,2048]{1,0:T(8,128)S(1)}, f32[256,2048]{1,0:T(8,128)}, u32[]{:S(2)}) copy-start(f32[256,2048]{1,0:T(8,128)} %copy-done.16) | copy-start | bytes 6291460
  625.7 5.1 copy-start.32
  625.7 9.1 slice-start
  630.8 4.0 slice-start.1
  640.6 4.8 copy-start.6
  640.6 4.8 copy-start.35
  640.6 4.8 copy-start.44
  651.7 3.5 copy-start.24
  651.7 14.5 %collective-permute-start.2 = (bf16[2,256,512]{2,1,0:T(8,128)(2,1)S(1)}, bf16[2,256,512]{2,1,0:T(8,128)(2,1)S(1)}, u32[]{:S(2)}, u32[]{:S(2)}) collective-permute-start(bf16[2,256,512]{2,1,0:T(8,128)(2,1)S(1)} %fusion.60), channel_id=1, source_target_pairs={{1,0},{2,1},{3,2},{5,4},{6,5},{7,6},{9,8},{10,9},{11,10},{13,12},{... | collective-permute-start | bytes 1572872 | tf_op jit(solution)/shard_map/ppermute | solution.py:856
  655.1 11.1 %copy-start.9 = (f32[1,768,512]{2,1,0:T(8,128)S(1)}, f32[1,768,512]{2,1,0:T(8,128)}, u32[]{:S(2)}) copy-start(f32[1,768,512]{2,1,0:T(8,128)} %copy.135) | copy-start | bytes 4718596
  655.1 11.0 %copy-start.11 = (f32[1,768,512]{2,1,0:T(8,128)S(1)}, f32[1,768,512]{2,1,0:T(8,128)}, u32[]{:S(2)}) copy-start(f32[1,768,512]{2,1,0:T(8,128)} %copy.134) | copy-start | bytes 4718596
  667.2 13.8 %collective-permute-start.3 = (bf16[2,256,512]{2,1,0:T(8,128)(2,1)}, bf16[2,256,512]{2,1,0:T(8,128)(2,1)}, u32[]{:S(2)}, u32[]{:S(2)}) collective-permute-start(bf16[2,256,512]{2,1,0:T(8,128)(2,1)} %fusion.58), channel_id=1, source_target_pairs={{1,0},{2,1},{3,2},{5,4},{6,5},{7,6},{9,8},{10,9},{11,10},{13,12},{... | collective-permute-start | bytes 1572872 | tf_op jit(solution)/shard_map/ppermute | solution.py:856
  670.0 48.5 %collective-permute-start.4 = (bf16[2,4,2,64,1024]{4,3,2,1,0:T(8,128)(2,1)}, bf16[2,4,2,64,1024]{4,3,2,1,0:T(8,128)(2,1)}, u32[]{:S(2)}, u32[]{:S(2)}) collective-permute-start(bf16[2,4,2,64,1024]{4,3,2,1,0:T(8,128)(2,1)} %pad_maximum_fusion), channel_id=1, source_target_pairs={{0,16},{16,0},{1,17},{17,1},{2,18},{18,2},{3,19},{19,3},{4,20},{20... | collective-permute-start | bytes 6291464 | tf_op jit(solution)/shard_map/ppermute | solution.py:846
  673.9 7.0 copy-start.10
  689.3 230.7 %collective-permute-start.5 = (bf16[256,2048]{1,0:T(8,128)(2,1)}, bf16[256,2048]{1,0:T(8,128)(2,1)}, u32[]{:S(2)}, u32[]{:S(2)}) collective-permute-start(bf16[256,2048]{1,0:T(8,128)(2,1)} %slice_bitcast_fusion.2), channel_id=1, source_target_pairs={{0,2},{2,0},{1,3},{3,1},{4,6},{6,4},{5,7},{7,5},{8,10},{10,8},{9,1... | collective-permute-start | bytes 3145736 | tf_op jit(solution)/shard_map/ppermute | solution.py:1068
  705.5 4.1 copy-start.13
  705.6 4.1 copy-start.20
  711.7 6.8 copy-start.21
  (33 other events, 64.9 us)

commit v6 on v5

--- a/solution.py
+++ b/solution.py
@@ -1026,7 +1026,7 @@
         value.reshape(lax.axis_size("y"), 4, -1, 2, depth, value.shape[1])
         for value in (part_gate, part_up)
     )
-    part_low, part_gate, part_up = lax.optimization_barrier((part_low, part_gate, part_up))
+    part_low, part_gate = lax.optimization_barrier((part_low, part_gate))
     if small_grid():
         part, down_sums = team_scatter(part_low, down_blocks)
     else:

time: 934 us -> 934 us (level)
  no operation moved by 1% of the time
where the time goes in v6:
time: 934 us; the launch traced here: 927 us
  Pallas kernels  580 us (62%)
  matrix products  216 us (23%)
  local copies, waits for them, and re-layouts  57.1 us (6%)
  other arithmetic  30.2 us (3%)
  waiting for transfers between devices  25.6 us (3%)
  starting transfers between devices  15.5 us (2%)
    pallas_call x1, Pallas kernels, weights_in(): remote_call(weights_in_kernel, (jax.ShapeDtypeStruct((32, rows, width), B...  202 us
    dot_general x27, matrix products, dot(): lax.dot_general(left, right, (((left_dim,), (right_dim,)), ((), ())), pre...  192 us
    pallas_call x1, Pallas kernels, grads_out(): remote_call(partial(grads_out_kernel, tuple(edges)), (jax.ShapeDtypeStruc...  187 us
    pallas_call x1, Pallas kernels, team_gather_with(): remote_call(partial(team_gather_kernel, True), (jax.ShapeDtypeStruct((8,...  49.7 us
    pallas_call x1, Pallas kernels, team_scatter(): remote_call(partial(team_scatter_kernel, True), (total, jax.ShapeDtypeStr...  48.1 us
    pallas_call x1, Pallas kernels, team_scatter(): remote_call(partial(team_scatter_kernel, False), total, 10, 1, [pltpu.Sem...  43.8 us
    pallas_call x1, Pallas kernels, team_gather(): remote_call(partial(team_gather_kernel, False), jax.ShapeDtypeStruct((8,...  39.4 us
    ppermute x4, waiting for transfers between devices, shift(): return lax.ppermute(block, ('h', 'l'), route)  25.6 us
  transfers between devices with their start and end apart: 6, of which 4 were waited for; matrix products, arithmetic and copies ran while one was open for 7% of the time, Pallas kernels for 21%

profile of v6, /device:TPU:1, one launch (start us, length us, event | category | flops | bytes accessed | tf_op | source)
XLA Modules:
  0.0 927.1 jit_solution(12323935531076469123)
XLA Ops:
  5.3 202.2 %shard_map.280 = (bf16[32,64,5888]{2,1,0:T(8,128)(2,1)}, bf16[2,4,2,2,64,1024]{5,4,3,2,1,0:T(8,128)(2,1)}, bf16[2,4,2,2,64,1024]{5,4,3,2,1,0:T(8,128)(2,1)}, bf16[256,2048]{1,0:T(8,128)(2,1)}) custom-call(bf16[64,5888]{1,0:T(8,128)(2,1)} %pad.29.x_ref, bf16[64,8192]{1,0:T(8,128)(2,1)} %gate_in.1, bf16[64,8192]{1,0:T(8,128)(2,1)} %up_in.1, ...), custom_call_target="tpu_custom_call" | custom-call | tf_op jit(solution)/shard_map/pallas_call | solution.py:618
  213.2 9.8 %fusion.3.raw_ref = f32[256,3072]{1,0:T(8,128)} fusion(bf16[2048,5888]{1,0:T(8,128)(2,1)} %bitcast.191, bf16[256,2048]{1,0:T(8,128)(2,1)S(1)} %copy-done.5, f32[2048]{0:T(1024)S(1)} %bitcast.210, f32[256]{0:T(256)S(1)} %add_rsqrt_fusion.5), kind=kOutput, calls=%fused_computation.7 | convolution fusion | flops 3223322624 | bytes 16786432 | tf_op jit(solution)/shard_map/dot_general | solution.py:25
  223.0 4.3 shard_map.281
  227.3 4.8 collective-permute-start
  237.5 5.0 collective-permute-done
  242.5 4.3 collective-permute-start.1
  247.8 9.1 collective-permute-done.1
  259.3 2.9 squeeze.28
  262.2 3.0 copy.118
  265.3 2.9 squeeze.27
  268.2 6.3 fusion.107
  274.5 4.1 fusion.51
  278.6 6.2 multiply_reduce_fusion.14
  288.8 49.7 %shard_map.282 = (bf16[8,256,2048]{2,1,0:T(8,128)(2,1)}, bf16[4,256,2048]{2,1,0:T(8,128)(2,1)S(1)}) custom-call(bf16[256,2048]{1,0:T(8,128)(2,1)S(1)} %multiply_convert_fusion.6.refs_0_, bf16[256,2048]{1,0:T(8,128)(2,1)S(1)} %copy-done.1, bf16[256,2048]{1,0:T(8,128)(2,1)S(1)} %copy-done.2), custom_call_target="tpu_custom_call" | custom-call | tf_op jit(solution)/shard_map/pallas_call | solution.py:336
  338.5 15.0 %fusion.108 = f32[2048,1024]{1,0:T(8,128)} fusion(bf16[2048,2048]{1,0:T(8,128)(2,1)} %bitcast.242, bf16[2048,1024]{1,0:T(8,128)(2,1)} %bitcast.250), kind=kOutput, calls=%fused_computation.195 | convolution fusion | flops 8589934592 | bytes 20971520 | tf_op jit(solution)/shard_map/dot_general | solution.py:25
  353.5 14.1 %multiply_convert_fusion.1 = (bf16[2048,1024]{1,0:T(8,128)(2,1)}, f32[2048,1024]{1,0:T(8,128)}) fusion(f32[2048,1024]{1,0:T(8,128)} %fusion.108, bf16[2048,2048]{1,0:T(8,128)(2,1)S(1)} %bitcast.244, bf16[2048,1024]{1,0:T(8,128)(2,1)S(1)} %bitcast.248), kind=kOutput, calls=%fused_computation.18 | convolution fusion | flops 8610906112 | bytes 33554432 | tf_op jit(solution)/shard_map/dot_general | solution.py:25
  367.6 10.7 %convolution_convert_fusion.2 = bf16[2048,2048]{1,0:T(8,128)(2,1)S(1)} fusion(bf16[2048,1024]{1,0:T(8,128)(2,1)} %get-tuple-element.151, bf16[1024,2048]{1,0:T(8,128)(2,1)S(1)} %bitcast.166), kind=kOutput, calls=%fused_computation.21 | convolution fusion | flops 8594128896 | bytes 16777216 | tf_op jit(solution)/shard_map/dot_general | solution.py:25
  378.4 43.8 %shard_map.283 = f32[256,2048]{1,0:T(8,128)S(1)} custom-call(bf16[8,256,2048]{2,1,0:T(8,128)(2,1)S(1)} %bitcast.163), custom_call_target="tpu_custom_call" | custom-call | tf_op jit(solution)/shard_map/pallas_call | solution.py:428
  434.8 2.7 multiply_reduce_fusion.1
  439.3 39.4 %shard_map.284 = bf16[8,256,2048]{2,1,0:T(8,128)(2,1)S(1)} custom-call(bf16[256,2048]{1,0:T(8,128)(2,1)S(1)} %multiply_convert_fusion.4.refs_0_), custom_call_target="tpu_custom_call" | custom-call | tf_op jit(solution)/shard_map/pallas_call | solution.py:320
  478.7 10.6 %convolution_convert_fusion.3 = bf16[1024,2048]{1,0:T(8,128)(2,1)} fusion(bf16[2048,1024]{1,0:T(8,128)(2,1)S(1)} %copy-done.68, bf16[2048,2048]{1,0:T(8,128)(2,1)S(1)} %bitcast.164), kind=kOutput, calls=%fused_computation.34 | convolution fusion | flops 8592031744 | bytes 16777216 | tf_op jit(solution)/shard_map/dot_general | solution.py:25
  489.2 21.3 %multiply_convert_fusion = (bf16[2048,1024]{1,0:T(8,128)(2,1)}, bf16[2048,1024]{1,0:T(8,128)(2,1)}) fusion(f32[2048,1024]{1,0:T(8,128)} %fusion.108, f32[2048,1024]{1,0:T(8,128)} %get-tuple-element.152, bf16[2048,2048]{1,0:T(8,128)(2,1)} %bitcast.165, bf16[1024,2048]{1,0:T(8,128)(2,1)S(1)} %bitcast.167), kind=kOutput, calls=%fused_computation.17 | convolution fusion | flops 8638169088 | bytes 37748736 | tf_op jit(solution)/shard_map/dot_general | solution.py:25
  510.5 14.1 %convolution_convert_fusion.5 = bf16[2048,1024]{1,0:T(8,128)(2,1)} fusion(bf16[2048,2048]{1,0:T(8,128)(2,1)} %bitcast.243, bf16[2048,1024]{1,0:T(8,128)(2,1)} %get-tuple-element.116), kind=kOutput, calls=%fused_computation.36 | convolution fusion | flops 8592031744 | bytes 16777216 | tf_op jit(solution)/shard_map/dot_general | solution.py:25
  524.6 11.7 %fusion.109 = f32[2048,2048]{1,0:T(8,128)} fusion(bf16[2048,1024]{1,0:T(8,128)(2,1)S(1)} %copy-done.70, bf16[2048,1024]{1,0:T(8,128)(2,1)S(1)} %bitcast.251), kind=kOutput, calls=%fused_computation.196 | convolution fusion | flops 8589934592 | bytes 25165824 | tf_op jit(solution)/shard_map/dot_general | solution.py:25
  536.4 11.2 %convolution_convert_fusion.4 = bf16[2048,1024]{1,0:T(8,128)(2,1)} fusion(bf16[2048,2048]{1,0:T(8,128)(2,1)S(1)} %bitcast.247, bf16[2048,1024]{1,0:T(8,128)(2,1)S(1)} %copy-done.69), kind=kOutput, calls=%fused_computation.35 | convolution fusion | flops 8592031744 | bytes 16777216 | tf_op jit(solution)/shard_map/dot_general | solution.py:25
  547.5 14.0 %add_convert_fusion = bf16[2048,2048]{1,0:T(8,128)(2,1)} fusion(f32[2048,2048]{1,0:T(8,128)} %fusion.109, bf16[2048,1024]{1,0:T(8,128)(2,1)S(1)} %copy-done.69, bf16[2048,1024]{1,0:T(8,128)(2,1)S(1)} %bitcast.249), kind=kOutput, calls=%fused_computation.1 | convolution fusion | flops 8598323200 | bytes 33554432 | tf_op jit(solution)/shard_map/dot_general | solution.py:25
  561.6 48.1 %shard_map.285 = (f32[256,2048]{1,0:T(8,128)S(1)}, bf16[2,256,2048]{2,1,0:T(8,128)(2,1)S(1)}) custom-call(bf16[8,256,2048]{2,1,0:T(8,128)(2,1)} %bitcast.171, bf16[4,256,2048]{2,1,0:T(8,128)(2,1)} %bitcast.175), custom_call_target="tpu_custom_call" | custom-call | tf_op jit(solution)/shard_map/pallas_call | solution.py:438
  612.0 2.5 multiply_reduce_fusion.3
  617.5 6.7 fusion.32
  625.7 5.1 fusion.47
  630.8 3.9 fusion.17
  638.3 2.3 fusion.110
  642.4 3.0 copy.135
  647.4 3.1 copy.134
  655.2 5.6 convolution_convert_fusion.1
  660.7 5.5 collective-permute-done.2
  671.0 2.9 copy.133.query_ref
  674.9 6.0 collective-permute-done.3
  680.9 2.3 fusion.61.pair_ref
  683.3 5.2 shard_map.286
  689.3 2.4 collective-permute-start.5
  691.7 9.1 fusion.28
  700.8 3.2 fusion.41
  705.6 4.0 fusion.31
  711.7 6.8 convolution_convert_fusion
  718.5 3.8 fusion.44
  722.3 187.2 %shard_map.287 = (f32[64,5888]{1,0:T(8,128)}, f32[64,8192]{1,0:T(8,128)}, f32[64,8192]{1,0:T(8,128)}) custom-call(bf16[32,64,3072]{2,1,0:T(8,128)(2,1)} %bitcast.168, bf16[32,64,2048]{2,1,0:T(8,128)(2,1)} %bitcast.169, bf16[32,64,256]{2,1,0:T(8,128)(2,1)} %bitcast.183, bf16[32,64,256]{2,1,0:T(8,128)(2,1)} %bitcast.205, bf16[32,64,256]{2,1,0:T(8,128)(2,1)} %bitcast.184, ...), custom_call_target="tpu_custom_call" | custom-call | tf_op jit(solution)/shard_map/pallas_call | solution.py:807
  920.0 3.0 convert_add_fusion.1
  (239 shorter events, 79.3 us)
Async XLA Ops:
  5.3 204.5 %copy-start.5 = (bf16[256,2048]{1,0:T(8,128)(2,1)S(1)}, bf16[256,2048]{1,0:T(8,128)(2,1)}, u32[]{:S(2)}) copy-start(bf16[256,2048]{1,0:T(8,128)(2,1)} %param.17) | copy-start | bytes 3145732
  210.1 75.2 %copy-start.43 = (f32[256]{0:T(256)}, f32[256]{0:T(256)S(1)}, u32[]{:S(2)}) copy-start(f32[256]{0:T(256)S(1)} %add_rsqrt_fusion.5) | copy-start | bytes 3076
  211.9 73.4 %copy-start.34 = (f32[1,2048]{1,0:T(1,128)}, f32[1,2048]{1,0:T(1,128)S(1)}, u32[]{:S(2)}) copy-start(f32[1,2048]{1,0:T(1,128)S(1)} %get-tuple-element.140) | copy-start | bytes 24580
  211.9 75.2 %copy-start.39 = (f32[1,2048]{1,0:T(1,128)}, f32[1,2048]{1,0:T(1,128)S(1)}, u32[]{:S(2)}) copy-start(f32[1,2048]{1,0:T(1,128)S(1)} %get-tuple-element.137) | copy-start | bytes 24580
  227.3 7.1 copy-start.31
  227.3 15.2 %collective-permute-start = (bf16[2,256,512]{2,1,0:T(8,128)(2,1)}, bf16[2,256,512]{2,1,0:T(8,128)(2,1)}, u32[]{:S(2)}, u32[]{:S(2)}) collective-permute-start(bf16[2,256,512]{2,1,0:T(8,128)(2,1)} %get-tuple-element.35), channel_id=1, source_target_pairs={{0,1},{1,2},{2,3},{4,5},{5,6},{6,7},{8,9},{9,10},{10,11},{12,13},{... | collective-permute-start | bytes 1572872 | tf_op jit(solution)/shard_map/ppermute | solution.py:856
  233.7 3.8 copy-start.36
  235.7 22.3 %copy-start.33 = (bf16[2,256,512]{2,1,0:T(8,128)(2,1)S(1)}, bf16[2,256,512]{2,1,0:T(8,128)(2,1)}, u32[]{:S(2)}) copy-start(bf16[2,256,512]{2,1,0:T(8,128)(2,1)} %get-tuple-element.35) | copy-start | bytes 1572868
  237.4 9.4 %copy-start.53 = (f32[256]{0:T(256)}, f32[256]{0:T(256)S(1)}, u32[]{:S(2)}) copy-start(f32[256]{0:T(256)S(1)} %get-tuple-element.145) | copy-start | bytes 3076
  237.5 47.9 %copy-start.7 = (f32[256,2048]{1,0:T(8,128)}, f32[256,2048]{1,0:T(8,128)S(1)}, u32[]{:S(2)}) copy-start(f32[256,2048]{1,0:T(8,128)S(1)} %get-tuple-element.146) | copy-start | bytes 6291460
  237.5 47.9 %copy-start.49 = (f32[256]{0:T(256)}, f32[256]{0:T(256)S(1)}, u32[]{:S(2)}) copy-start(f32[256]{0:T(256)S(1)} %add_rsqrt_fusion.3) | copy-start | bytes 3076
  242.5 14.4 %collective-permute-start.1 = (bf16[2,256,512]{2,1,0:T(8,128)(2,1)}, bf16[2,256,512]{2,1,0:T(8,128)(2,1)S(1)}, u32[]{:S(2)}, u32[]{:S(2)}) collective-permute-start(bf16[2,256,512]{2,1,0:T(8,128)(2,1)} %collective-permute-done), channel_id=1, source_target_pairs={{0,1},{1,2},{2,3},{4,5},{5,6},{6,7},{8,9},{9,10},{10,11},{12,13},{... | collective-permute-start | bytes 1572872 | tf_op jit(solution)/shard_map/ppermute | solution.py:856
  274.5 4.1 copy-start.59
  278.6 6.2 copy-start.28
  286.5 52.0 %copy-start.57 = (f32[256]{0:T(256)}, f32[256]{0:T(256)S(1)}, u32[]{:S(2)}) copy-start(f32[256]{0:T(256)S(1)} %get-tuple-element.113) | copy-start | bytes 3076
  286.5 135.9 %copy-start.3 = (f32[256,2048]{1,0:T(8,128)}, f32[256,2048]{1,0:T(8,128)S(1)}, u32[]{:S(2)}) copy-start(f32[256,2048]{1,0:T(8,128)S(1)} %get-tuple-element.114) | copy-start | bytes 6291460
  287.1 51.4 %copy-start.47 = (f32[256]{0:T(256)}, f32[256]{0:T(256)S(1)}, u32[]{:S(2)}) copy-start(f32[256]{0:T(256)S(1)} %get-tuple-element.144) | copy-start | bytes 3076
  338.5 15.0 %copy-start.64 = (bf16[8,256,2048]{2,1,0:T(8,128)(2,1)S(1)}, bf16[8,256,2048]{2,1,0:T(8,128)(2,1)}, u32[]{:S(2)}) copy-start(bf16[8,256,2048]{2,1,0:T(8,128)(2,1)} %get-tuple-element.38) | copy-start | bytes 25165828
  338.5 15.0 %copy-start.65 = (bf16[2,4,2,2,64,1024]{5,4,3,2,1,0:T(8,128)(2,1)S(1)}, bf16[2,4,2,2,64,1024]{5,4,3,2,1,0:T(8,128)(2,1)}, u32[]{:S(2)}) copy-start(bf16[2,4,2,2,64,1024]{5,4,3,2,1,0:T(8,128)(2,1)} %get-tuple-element.40) | copy-start | bytes 12582916
  439.3 39.4 %copy-start.68 = (bf16[2048,1024]{1,0:T(8,128)(2,1)S(1)}, bf16[2048,1024]{1,0:T(8,128)(2,1)}, u32[]{:S(2)}) copy-start(bf16[2048,1024]{1,0:T(8,128)(2,1)} %get-tuple-element.151) | copy-start | bytes 12582916
  478.6 10.6 %copy-start = (bf16[8,256,2048]{2,1,0:T(8,128)(2,1)}, bf16[8,256,2048]{2,1,0:T(8,128)(2,1)S(1)}, u32[]{:S(2)}) copy-start(bf16[8,256,2048]{2,1,0:T(8,128)(2,1)S(1)} %shard_map.284) | copy-start | bytes 25165828
  510.5 14.1 %copy-start.67 = (bf16[2,4,2,2,64,1024]{5,4,3,2,1,0:T(8,128)(2,1)S(1)}, bf16[2,4,2,2,64,1024]{5,4,3,2,1,0:T(8,128)(2,1)}, u32[]{:S(2)}) copy-start(bf16[2,4,2,2,64,1024]{5,4,3,2,1,0:T(8,128)(2,1)} %get-tuple-element.39) | copy-start | bytes 12582916
  510.5 14.1 %copy-start.70 = (bf16[2048,1024]{1,0:T(8,128)(2,1)S(1)}, bf16[2048,1024]{1,0:T(8,128)(2,1)}, u32[]{:S(2)}) copy-start(bf16[2048,1024]{1,0:T(8,128)(2,1)} %get-tuple-element.116) | copy-start | bytes 12582916
  510.5 25.8 %slice-start.2 = ((s8[8388608]{0:T(1024)(128)(4,1)}), s8[4194304]{0:T(1024)(128)(4,1)S(1)}, s32[]{:S(2)}) async-start(s8[8388608]{0:T(1024)(128)(4,1)} %bitcast.245), calls=%async_computation.2 | async-start | bytes 8388608
  524.6 11.7 %slice-start.3 = ((s8[8388608]{0:T(1024)(128)(4,1)}), s8[4194304]{0:T(1024)(128)(4,1)S(1)}, s32[]{:S(2)}) async-start(s8[8388608]{0:T(1024)(128)(4,1)} %bitcast.245), calls=%async_computation.3 | async-start | bytes 8388608
  524.6 11.7 %copy-start.69 = (bf16[2048,1024]{1,0:T(8,128)(2,1)S(1)}, bf16[2048,1024]{1,0:T(8,128)(2,1)}, u32[]{:S(2)}) copy-start(bf16[2048,1024]{1,0:T(8,128)(2,1)} %get-tuple-element.115) | copy-start | bytes 12582916
  536.4 11.2 %copy-start.66 = (bf16[2,4,2,2,64,1024]{5,4,3,2,1,0:T(8,128)(2,1)S(1)}, bf16[2,4,2,2,64,1024]{5,4,3,2,1,0:T(8,128)(2,1)}, u32[]{:S(2)}) copy-start(bf16[2,4,2,2,64,1024]{5,4,3,2,1,0:T(8,128)(2,1)} %get-tuple-element.40) | copy-start | bytes 12582916
  561.6 48.1 %copy-start.4 = (f32[256,2048]{1,0:T(8,128)S(1)}, f32[256,2048]{1,0:T(8,128)}, u32[]{:S(2)}) copy-start(f32[256,2048]{1,0:T(8,128)} %copy-done.3) | copy-start | bytes 6291460
  561.6 48.1 %copy-start.40 = (f32[1,2048]{1,0:T(1,128)S(1)}, f32[1,2048]{1,0:T(1,128)}, u32[]{:S(2)}) copy-start(f32[1,2048]{1,0:T(1,128)} %copy-done.39) | copy-start | bytes 24580
  561.6 48.1 %copy-start.48 = (f32[256]{0:T(256)S(1)}, f32[256]{0:T(256)}, u32[]{:S(2)}) copy-start(f32[256]{0:T(256)} %copy-done.47) | copy-start | bytes 3076
  561.6 48.9 %copy-start.17 = (f32[256,2048]{1,0:T(8,128)S(1)}, f32[256,2048]{1,0:T(8,128)}, u32[]{:S(2)}) copy-start(f32[256,2048]{1,0:T(8,128)} %copy-done.16) | copy-start | bytes 6291460
  625.7 5.1 copy-start.32
  625.7 9.1 slice-start
  630.8 4.0 slice-start.1
  640.6 4.8 copy-start.6
  640.6 4.8 copy-start.35
  640.6 4.8 copy-start.44
  651.7 3.5 copy-start.24
  651.7 14.5 %collective-permute-start.2 = (bf16[2,256,512]{2,1,0:T(8,128)(2,1)S(1)}, bf16[2,256,512]{2,1,0:T(8,128)(2,1)S(1)}, u32[]{:S(2)}, u32[]{:S(2)}) collective-permute-start(bf16[2,256,512]{2,1,0:T(8,128)(2,1)S(1)} %fusion.60), channel_id=1, source_target_pairs={{1,0},{2,1},{3,2},{5,4},{6,5},{7,6},{9,8},{10,9},{11,10},{13,12},{... | collective-permute-start | bytes 1572872 | tf_op jit(solution)/shard_map/ppermute | solution.py:856
  655.1 11.1 %copy-start.9 = (f32[1,768,512]{2,1,0:T(8,128)S(1)}, f32[1,768,512]{2,1,0:T(8,128)}, u32[]{:S(2)}) copy-start(f32[1,768,512]{2,1,0:T(8,128)} %copy.135) | copy-start | bytes 4718596
  655.1 11.0 %copy-start.11 = (f32[1,768,512]{2,1,0:T(8,128)S(1)}, f32[1,768,512]{2,1,0:T(8,128)}, u32[]{:S(2)}) copy-start(f32[1,768,512]{2,1,0:T(8,128)} %copy.134) | copy-start | bytes 4718596
  667.2 13.8 %collective-permute-start.3 = (bf16[2,256,512]{2,1,0:T(8,128)(2,1)}, bf16[2,256,512]{2,1,0:T(8,128)(2,1)}, u32[]{:S(2)}, u32[]{:S(2)}) collective-permute-start(bf16[2,256,512]{2,1,0:T(8,128)(2,1)} %fusion.58), channel_id=1, source_target_pairs={{1,0},{2,1},{3,2},{5,4},{6,5},{7,6},{9,8},{10,9},{11,10},{13,12},{... | collective-permute-start | bytes 1572872 | tf_op jit(solution)/shard_map/ppermute | solution.py:856
  670.0 48.5 %collective-permute-start.4 = (bf16[2,4,2,64,1024]{4,3,2,1,0:T(8,128)(2,1)}, bf16[2,4,2,64,1024]{4,3,2,1,0:T(8,128)(2,1)}, u32[]{:S(2)}, u32[]{:S(2)}) collective-permute-start(bf16[2,4,2,64,1024]{4,3,2,1,0:T(8,128)(2,1)} %pad_maximum_fusion), channel_id=1, source_target_pairs={{0,16},{16,0},{1,17},{17,1},{2,18},{18,2},{3,19},{19,3},{4,20},{20... | collective-permute-start | bytes 6291464 | tf_op jit(solution)/shard_map/ppermute | solution.py:846
  673.9 7.0 copy-start.10
  689.3 230.7 %collective-permute-start.5 = (bf16[256,2048]{1,0:T(8,128)(2,1)}, bf16[256,2048]{1,0:T(8,128)(2,1)}, u32[]{:S(2)}, u32[]{:S(2)}) collective-permute-start(bf16[256,2048]{1,0:T(8,128)(2,1)} %slice_bitcast_fusion.2), channel_id=1, source_target_pairs={{0,2},{2,0},{1,3},{3,1},{4,6},{6,4},{5,7},{7,5},{8,10},{10,8},{9,1... | collective-permute-start | bytes 3145736 | tf_op jit(solution)/shard_map/ppermute | solution.py:1068
  705.5 4.1 copy-start.13
  705.6 4.1 copy-start.20
  711.7 6.8 copy-start.21
  (33 other events, 64.9 us)
